TPU v7x, 256 devices: a whole 4x4x8 slice. The times are simulated.
256 devices in a mesh: dp: 8 (over x, y_lo), seq: 32 (over z, y_hi, core).
Axes of the slice: x: 4, y: 4 (y_hi: 2, y_lo: 2; y = y_hi * 2 + y_lo), z: 8, core: 2. Of those that a mesh axis runs over, the one named last changes fastest.
Arguments:
- x_fwd: bfloat16 [131072, 1024], P(('dp', 'seq')), parts along dimension 0, may hold values from -6 to 6
- x_rev: bfloat16 [131072, 1024], P(('dp', 'seq')), parts along dimension 0, may hold values from -6 to 6
- gain: bfloat16 [1024], replicated, may hold values from 0.099609375 to 1.8984375
- w_qkv: bfloat16 [1024, 3072], replicated
Outputs:
- y_fwd: bfloat16 [131072, 1024], P(('dp', 'seq')), parts along dimension 0
- y_rev: bfloat16 [131072, 1024], P(('dp', 'seq')), parts along dimension 0
There are 8 independent parts, one for each index of `dp`. A program takes and returns all parts, laid end to end along the dimension named above; an argument that names none is the same for every part. Nothing has to cross between parts.
All inputs are finite; a program needn't handle non-finite values.
Results may differ from a plain program's by a relative error of at most 0.012.
Values may be sent and summed in bfloat16 or wider, within the bound.
No kernel may reach another device: no remote copies, remote signals or barrier semaphores. Data moves between devices by JAX's collectives and lax.ppermute only.
A program may use at most 128 MiB of HBM per device.

v0:
```python
import functools

import jax
import jax.numpy as jnp
from jax import lax
from jax.experimental import pallas as pl
from jax.experimental.pallas import tpu as pltpu
from jax.sharding import PartitionSpec as P

HEADS = 16
WINDOW = 512
LOG2E = 1.4426950408889634
NEG = -1e30
SMALL = pl.CostEstimate(flops=1, bytes_accessed=1, transcendentals=0)
VMEM_LIMIT = 64 * 1024 * 1024 - 256 * 1024
A_CHUNKS = (4, 4)
CHUNKS = (2, 2, 2, 2)
EIGHTHS = ()


def after(x, *others):
    return lax.optimization_barrier((x, *others))[0]


def exchange_matrix(n):
    r = lax.broadcasted_iota(jnp.int32, (n, n), 0)
    c = lax.broadcasted_iota(jnp.int32, (n, n), 1)
    return (r + c == n - 1).astype(jnp.bfloat16)


def rows_reversed(x, out_ref):
    half = x.shape[0] // 2
    ex = exchange_matrix(half)
    out_ref[:half] = jnp.dot(ex, x[half:], preferred_element_type=jnp.float32).astype(out_ref.dtype)
    out_ref[half:] = jnp.dot(ex, x[:half], preferred_element_type=jnp.float32).astype(out_ref.dtype)


def columns_reversed(x, out_ref):
    width = x.shape[1]
    size = min(256, width)
    ex = exchange_matrix(size)
    for n in range(width // size):
        t = jnp.dot(x[:, n * size : (n + 1) * size], ex, preferred_element_type=jnp.float32)
        out_ref[:, width - (n + 1) * size : width - n * size] = t.astype(out_ref.dtype)


def project_kernel(scale, mirrored, with_q, n, *refs):
    x_refs = refs[:n]
    gain_ref, w_ref = refs[n : n + 2]
    refs = refs[n + 2 :]
    if with_q:
        q_ref, kv_ref, hn_ref, turned_ref = refs
    else:
        kv_ref, hn_ref, turned_ref = refs
    j = pl.program_id(0)
    rows = x_refs[0].shape[0]

    @pl.when(j == 0)
    def _():
        for m in range(n):
            xf = x_refs[m][...].astype(jnp.float32)
            meansq = jnp.mean(xf * xf, axis=-1, keepdims=True)
            hn = xf * lax.rsqrt(meansq + 1e-6) * gain_ref[...].astype(jnp.float32)
            hn_ref[m * rows : (m + 1) * rows] = hn.astype(jnp.bfloat16)

    def product(h):
        return jnp.dot(h, w_ref[...], preferred_element_type=jnp.float32)

    first = 1 if with_q else 0
    if with_q:

        @pl.when(j == 0)
        def _():
            if mirrored:
                rows_reversed(hn_ref[:rows], turned_ref)
                q_ref[...] = (product(turned_ref[...]) * scale).astype(jnp.bfloat16)
            else:
                q_ref[...] = (product(hn_ref[:rows]) * scale).astype(jnp.bfloat16)

    @pl.when(j == first)
    def _():
        kv_ref[...] = product(hn_ref[...]).astype(jnp.bfloat16)

    @pl.when(j == first + 1)
    def _():
        v = product(hn_ref[...]).astype(jnp.bfloat16)
        if mirrored:
            columns_reversed(v, kv_ref)
        else:
            kv_ref[...] = v


def project(xs, gain, w, scale, mirrored, with_q):
    rows, width = xs[0].shape
    n = len(xs)
    first = 1 if with_q else 0
    kv = jax.ShapeDtypeStruct((n * rows, 2 * width), jnp.bfloat16)
    kv_spec = pl.BlockSpec((n * rows, width), lambda j: (0, jnp.maximum(j - first, 0)))
    q = jax.ShapeDtypeStruct((rows, width), jnp.bfloat16)
    q_spec = pl.BlockSpec((rows, width), lambda j: (0, 0))
    return pl.pallas_call(
        functools.partial(project_kernel, scale, mirrored, with_q, n),
        out_shape=(q, kv) if with_q else kv,
        grid=(2 + first,),
        in_specs=[pl.BlockSpec((rows, width), lambda j: (0, 0))] * n
        + [
            pl.BlockSpec((1, width), lambda j: (0, 0)),
            pl.BlockSpec((width, width), lambda j: (0, j + 1 - first)),
        ],
        out_specs=(q_spec, kv_spec) if with_q else kv_spec,
        scratch_shapes=[
            pltpu.VMEM((n * rows, width), jnp.bfloat16),
            pltpu.VMEM((rows, width), jnp.bfloat16),
        ],
        compiler_params=pltpu.CompilerParams(vmem_limit_bytes=VMEM_LIMIT),
        cost_estimate=SMALL,
        name="project",
    )(*xs, gain, w)


def attention_kernel(tile, mirrored, nears, flags_ref, q_ref, ko_ref, ks_ref, kr_ref, vo_ref, vs_ref, vr_ref, *refs):
    near_refs = refs[:nears]
    out_ref, kbuf, vbuf = refs[nears:]
    rows, width = q_ref.shape
    head = width // 2
    sibling_left = flags_ref[0] > 0
    has_remote = flags_ref[1] > 0
    at_s = pl.multiple_of(jnp.where(sibling_left, 0, 2 * rows), rows)
    at_r = pl.multiple_of(jnp.where(sibling_left, 2 * rows, 0), rows)
    ones = jnp.ones((rows, width), jnp.bfloat16)
    none = jnp.zeros((rows, width), jnp.bfloat16)
    kbuf[rows : 2 * rows] = ko_ref[...]
    vbuf[rows : 2 * rows, :width] = vo_ref[...]
    vbuf[rows : 2 * rows, width:] = ones
    kbuf[pl.ds(at_s, rows)] = ks_ref[...]
    vbuf[pl.ds(at_s, rows), :width] = vs_ref[...]
    vbuf[pl.ds(at_s, rows), width:] = ones
    kbuf[pl.ds(at_r, rows)] = jnp.where(has_remote, kr_ref[...], ko_ref[...])
    vbuf[pl.ds(at_r, rows), :width] = jnp.where(has_remote, vr_ref[...], none)
    vbuf[pl.ds(at_r, rows), width:] = jnp.where(has_remote, ones, none)

    span = tile + 2 * WINDOW
    r = lax.broadcasted_iota(jnp.int32, (tile, tile), 0)
    c = lax.broadcasted_iota(jnp.int32, (tile, tile), 1)
    if mirrored:
        r = tile - 1 - r
    low = c >= r
    high = c <= r
    lane = lax.broadcasted_iota(jnp.int32, (tile, width), 1)
    tiles = rows // tile
    for t in range(tiles):
        here = slice(t * tile, (t + 1) * tile)
        q = q_ref[here, :]
        first = (tiles - 1 - t if mirrored else t) * tile
        keys = kbuf[first : first + span, :]
        values = vbuf[first : first + span, :]
        outs = []
        for h in range(2):
            mine = (lane < head) if h == 0 else (lane >= head)
            qh = jnp.where(mine, q, jnp.zeros_like(q))
            s = lax.dot_general(
                qh, keys, (((1,), (1,)), ((), ())), preferred_element_type=jnp.float32
            )
            s_low = jnp.where(low, s[:, :tile], NEG)
            s_mid = s[:, tile : 2 * WINDOW]
            s_high = jnp.where(high, s[:, 2 * WINDOW :], NEG)
            s = jnp.concatenate([s_low, s_mid, s_high], axis=1)
            top = jnp.max(s, axis=-1, keepdims=True)
            p = jnp.exp2(s - top).astype(jnp.bfloat16)
            o = jnp.dot(p, values, preferred_element_type=jnp.float32)
            outs.append(o[:, :width] / o[:, width:])
        if mirrored:
            outs = outs[::-1]
        a = jnp.where(lane < head, outs[0], outs[1]).astype(jnp.bfloat16)
        if nears:
            near = near_refs[0][here, :]
            if nears == 2:
                near = jnp.where(flags_ref[2] > 0, near, near_refs[1][here, :])
            a = (near.astype(jnp.float32) + a.astype(jnp.float32)).astype(jnp.bfloat16)
        out_ref[here, :] = a


def attention(q, chip, remote, flags, first, count, near=(), near_first=0):
    rows, width = q.shape
    pw = 2 * (width // HEADS)
    n = width // pw
    f = first
    mirrored = len(near) > 0

    def keys(row):
        return pl.BlockSpec((rows, pw), lambda g: (row, n - 1 - f - g if mirrored else f + g))

    def values(row):
        return pl.BlockSpec((rows, pw), lambda g: (row, n + f + g))

    near_spec = pl.BlockSpec((rows, pw), lambda g: (0, near_first + g))
    out_spec = pl.BlockSpec((rows, pw), lambda g: (0, g))
    return pl.pallas_call(
        functools.partial(attention_kernel, min(256, rows), mirrored, len(near)),
        out_shape=jax.ShapeDtypeStruct((rows, count * pw), jnp.bfloat16),
        grid=(count,),
        in_specs=[pl.BlockSpec(memory_space=pltpu.SMEM)]
        + [keys(0), keys(0), keys(1), keys(0), values(0), values(1), values(0)]
        + [near_spec] * len(near),
        out_specs=out_spec,
        scratch_shapes=[
            pltpu.VMEM((rows + 2 * WINDOW, pw), jnp.bfloat16),
            pltpu.VMEM((rows + 2 * WINDOW, 2 * pw), jnp.bfloat16),
        ],
        compiler_params=pltpu.CompilerParams(vmem_limit_bytes=VMEM_LIMIT),
        cost_estimate=SMALL,
        name="attention_mirrored" if mirrored else "attention",
    )(flags, q, chip, chip, remote, chip, chip, remote, *near)


def finish_kernel(flags_ref, mine_ref, moved_ref, *refs):
    fwd_ref, rev_ref = refs[-2:]
    fetched = flags_ref[2] > 0
    mine, moved = mine_ref[...], moved_ref[...]
    fwd_ref[...] = jnp.where(fetched, mine, moved)
    t = jnp.where(fetched, moved, mine)
    t = jnp.dot(t, exchange_matrix(t.shape[1]), preferred_element_type=jnp.float32)
    rows_reversed(t.astype(jnp.bfloat16), rev_ref)


def finish(flags, mine, moved, first, width, held):
    rows, piece = mine.shape
    pw = 2 * (width // HEADS)
    n = width // pw
    f = first
    out = jax.ShapeDtypeStruct((rows, width), jnp.bfloat16)
    block = pl.BlockSpec((rows, pw), lambda g: (0, g))
    return pl.pallas_call(
        finish_kernel,
        out_shape=(out, out),
        grid=(piece // pw,),
        in_specs=[pl.BlockSpec(memory_space=pltpu.SMEM), block, block]
        + [pl.BlockSpec(memory_space=pl.ANY)] * len(held),
        out_specs=(
            pl.BlockSpec((rows, pw), lambda g: (0, f + g)),
            pl.BlockSpec((rows, pw), lambda g: (0, n - 1 - f - g)),
        ),
        input_output_aliases={3: 0, 4: 1} if held else {},
        compiler_params=pltpu.CompilerParams(vmem_limit_bytes=VMEM_LIMIT),
        cost_estimate=SMALL,
        name="finish",
    )(flags, mine, moved, *held)


def routes(count):
    fetch = [i * 8 // count in EIGHTHS for i in range(count)]
    place = [count - 1 - i if fetch[i] else i for i in range(count)]
    pairs, home, has = [], [True] * count, [False] * count
    for i in range(count):
        wanted = 2 * place[i] - place[i ^ 1]
        if 0 <= wanted < count:
            has[i] = True
            beside = i - 1 if i % 2 == 0 else i + 1
            if fetch[i] and 0 <= beside < count and fetch[beside]:
                source, home[beside] = beside, False
            else:
                source = wanted
            pairs.append((source, i))
    assert len({s for s, _ in pairs}) == len(pairs)
    for s, i in pairs:
        wanted = 2 * place[i] - place[i ^ 1]
        assert (s if home[s] else place[s]) == wanted
    return fetch, place, pairs, home, has


def per_device(x_fwd, x_rev, gain, w_qkv):
    count = lax.axis_size("seq")
    index = lax.axis_index("seq")
    rows, width = x_fwd.shape
    scale = (width // HEADS) ** (-0.5) * LOG2E
    gain = gain.reshape(1, width)
    fetch, place, s_pairs, home, s_has = routes(count)
    sibling = [(i, i ^ 1) for i in range(count)]
    beside = [(i, i - 1 if i % 2 == 0 else i + 1) for i in range(1, count - 1)]
    mirror = [(i, count - 1 - i) for i in range(count)]

    def pick(values):
        return jnp.asarray(values, jnp.int32)[index]

    def send(x, pairs):
        return lax.ppermute(x, "seq", pairs)

    f_flags = jnp.stack([index % 2, (index > 0) & (index < count - 1), index]).astype(jnp.int32)
    s_flags = jnp.stack([pick([place[i ^ 1] < place[i] for i in range(count)]), pick(s_has), pick(fetch)])

    f_x = send(x_fwd, beside)
    f_y = send(x_fwd, sibling)
    own = x_rev
    payload = x_rev
    if any(fetch):
        swapped = send(x_rev, [m for m in mirror if fetch[m[0]]])
        own = jnp.where(pick(fetch) > 0, swapped, x_rev)
        payload = jnp.where(pick(home) > 0, x_rev, swapped)
    f_q, f_chip = project([x_fwd, f_y], gain, w_qkv, scale, False, True)

    payload = after(payload, f_x, f_q)
    s_x = send(payload, s_pairs)
    s_y = send(after(own, payload), sibling)
    f_rem = project([after(f_x, payload)], gain, w_qkv, scale, False, False)

    a_firsts = [sum(A_CHUNKS[:k]) for k in range(len(A_CHUNKS))]
    firsts = [sum(CHUNKS[:k]) for k in range(len(CHUNKS))]
    a_f, a_moved = [], []
    for k in range(len(A_CHUNKS)):
        if k == 1:
            s_q, s_chip = project([own, after(s_y, a_f[0])], gain, w_qkv, scale, True, True)
            f_flags = after(f_flags, s_chip)
        a = attention(f_q, f_chip, f_rem, f_flags, a_firsts[k], A_CHUNKS[k])
        f_flags = after(f_flags, a)
        a_f.append(a)
        if not all(fetch):
            a_moved.append(send(a, [m for m in mirror if not fetch[m[0]]]))
    s_rem = project([after(s_x, a_f[-1])], gain, w_qkv, scale, True, False)

    mine, moved = [], []
    for k in range(len(CHUNKS)):
        at = max(m for m in range(len(A_CHUNKS)) if a_firsts[m] <= firsts[k])
        near = [a_f[at]] if any(fetch) else []
        near += [a_moved[at]] if not all(fetch) else []
        if k >= 2:
            moved[k - 2], s_flags = lax.optimization_barrier((moved[k - 2], s_flags))
        y = attention(s_q, s_chip, s_rem, s_flags, firsts[k], CHUNKS[k], near, firsts[k] - a_firsts[at])
        s_flags = after(s_flags, y)
        mine.append(y)
        moved.append(send(y, mirror))
    held = ()
    for k in range(len(CHUNKS)):
        held = finish(s_flags, mine[k], moved[k], firsts[k], width, held)
    return held


def solution(mesh):
    in_specs = (P(("dp", "seq"), None), P(("dp", "seq"), None), P(), P())
    out_specs = (P(("dp", "seq"), None), P(("dp", "seq"), None))
    return jax.shard_map(
        per_device, mesh=mesh, in_specs=in_specs, out_specs=out_specs, check_vma=False
    )
```

profile of v0, /device:TPU:25, one launch (start us, length us, event | category | flops | bytes accessed | tf_op | source)
XLA Modules:
  0.0 160.9 jit_solution(7242339943031783396)
XLA Ops:
  1.4 4.1 %collective-permute-start = (bf16[512,1024]{1,0:T(8,128)(2,1)}, bf16[512,1024]{1,0:T(8,128)(2,1)}, u32[]{:S(2)}, u32[]{:S(2)}) collective-permute-start(bf16[512,1024]{1,0:T(8,128)(2,1)} %refs_0_.2), channel_id=1, source_target_pairs={{1,2},{2,1},{3,4},{4,3},{5,6},{6,5},{7,8},{8,7},{9,10},{10,9},{11,... | collective-permute-start | bytes 3145736 | tf_op jit(solution)/shard_map/ppermute | solution.py:286
  5.5 1.3 reshape.7.refs_2_.refs_1_
  6.8 10.4 %project.4 = (bf16[512,1024]{1,0:T(8,128)(2,1)}, bf16[1024,2048]{1,0:T(8,128)(2,1)}) custom-call(bf16[512,1024]{1,0:T(8,128)(2,1)} %refs_0_.2, bf16[512,1024]{1,0:T(8,128)(2,1)} %collective-permute-done.1.refs_1_, bf16[1,1024]{1,0:T(2,128)(2,1)} %reshape.7.refs_2_.refs_1_, bf16[1024,3072]{1,0:T(8,128)(2,1)} %refs_2_.3), custom_call_target="tpu_custom_call" | custom-call | flops 1 | bytes 1 | tf_op jit(solution)/shard_map/project/pallas_call | solution.py:101
  17.2 3.1 %collective-permute-done.refs_0_ = bf16[512,1024]{1,0:T(8,128)(2,1)} collective-permute-done((bf16[512,1024]{1,0:T(8,128)(2,1)}, bf16[512,1024]{1,0:T(8,128)(2,1)}, u32[]{:S(2)}, u32[]{:S(2)}) %collective-permute-start) | collective-permute-done | bytes 1048608 | tf_op jit(solution)/shard_map/ppermute | solution.py:286
  20.3 10.3 %collective-permute-start.2 = (bf16[512,1024]{1,0:T(8,128)(2,1)}, bf16[512,1024]{1,0:T(8,128)(2,1)}, u32[]{:S(2)}, u32[]{:S(2)}) collective-permute-start(bf16[512,1024]{1,0:T(8,128)(2,1)} %refs_0_.3), channel_id=1, source_target_pairs={{0,1},{1,0},{2,3},{3,2},{4,5},{5,4},{6,7},{7,6},{8,9},{9,8},{10,11... | collective-permute-start | bytes 3145736 | tf_op jit(solution)/shard_map/ppermute | solution.py:286
  30.6 4.6 %collective-permute-start.3 = (bf16[512,1024]{1,0:T(8,128)(2,1)}, bf16[512,1024]{1,0:T(8,128)(2,1)}, u32[]{:S(2)}, u32[]{:S(2)}) collective-permute-start(bf16[512,1024]{1,0:T(8,128)(2,1)} %refs_0_.3), channel_id=1, source_target_pairs={{2,1},{1,2},{4,3},{3,4},{6,5},{5,6},{8,7},{7,8},{10,9},{9,10},{12,... | collective-permute-start | bytes 3145736 | tf_op jit(solution)/shard_map/ppermute | solution.py:286
  35.9 5.6 %project.5.kr_ref.vr_ref = bf16[512,2048]{1,0:T(8,128)(2,1)} custom-call(bf16[512,1024]{1,0:T(8,128)(2,1)} %collective-permute-done.refs_0_, bf16[1,1024]{1,0:T(2,128)(2,1)} %reshape.7.refs_2_.refs_1_, bf16[1024,3072]{1,0:T(8,128)(2,1)} %refs_2_.3), custom_call_target="tpu_custom_call" | custom-call | flops 1 | bytes 1 | tf_op jit(solution)/shard_map/project/pallas_call | solution.py:101
  41.5 10.7 %attention.2 = bf16[512,512]{1,0:T(8,128)(2,1)} custom-call(s32[3]{0:T(128)} %pad_add_fusion.1.flags_ref, bf16[512,1024]{1,0:T(8,128)(2,1)} %get-tuple-element.27.q_ref, bf16[1024,2048]{1,0:T(8,128)(2,1)} %get-tuple-element.30.ko_ref.ks_ref.vo_ref.vs_ref, bf16[1024,2048]{1,0:T(8,128)(2,1)} %get-tuple-element.30.ko_ref.ks_ref.vo_ref.vs_ref, ...), custom_call_target="tpu_custom_call" | custom-call | flops 1 | bytes 1 | tf_op jit(solution)/shard_map/attention/pallas_call | solution.py:198
  52.2 6.3 %collective-permute-start.4 = (bf16[512,512]{1,0:T(8,128)(2,1)}, bf16[512,512]{1,0:T(8,128)(2,1)}, u32[]{:S(2)}, u32[]{:S(2)}) collective-permute-start(bf16[512,512]{1,0:T(8,128)(2,1)} %attention.2), channel_id=1, source_target_pairs={{0,31},{1,30},{2,29},{3,28},{4,27},{5,26},{6,25},{7,24},{8,23},{9,... | collective-permute-start | bytes 1572872 | tf_op jit(solution)/shard_map/ppermute | solution.py:286
  58.5 11.2 %project.6 = (bf16[512,1024]{1,0:T(8,128)(2,1)}, bf16[1024,2048]{1,0:T(8,128)(2,1)}) custom-call(bf16[512,1024]{1,0:T(8,128)(2,1)} %refs_0_.3, bf16[512,1024]{1,0:T(8,128)(2,1)} %collective-permute-done.2.refs_1_, bf16[1,1024]{1,0:T(2,128)(2,1)} %reshape.7.refs_2_.refs_1_, bf16[1024,3072]{1,0:T(8,128)(2,1)} %refs_2_.3), custom_call_target="tpu_custom_call" | custom-call | flops 1 | bytes 1 | tf_op jit(solution)/shard_map/project/pallas_call | solution.py:101
  69.8 10.7 %attention.3 = bf16[512,512]{1,0:T(8,128)(2,1)} custom-call(s32[3]{0:T(128)} %pad_add_fusion.1.flags_ref, bf16[512,1024]{1,0:T(8,128)(2,1)} %get-tuple-element.27.q_ref, bf16[1024,2048]{1,0:T(8,128)(2,1)} %get-tuple-element.30.ko_ref.ks_ref.vo_ref.vs_ref, bf16[1024,2048]{1,0:T(8,128)(2,1)} %get-tuple-element.30.ko_ref.ks_ref.vo_ref.vs_ref, ...), custom_call_target="tpu_custom_call" | custom-call | flops 1 | bytes 1 | tf_op jit(solution)/shard_map/attention/pallas_call | solution.py:198
  81.8 1.9 %pad_add_fusion.flags_ref = s32[3]{0:T(128)} fusion(s32[1]{0:T(128)} %constant.31, s32[1]{0:T(128)} %dynamic_slice.10, s32[1]{0:T(128)} %dynamic_slice.9), kind=kLoop, calls=%fused_computation | loop fusion | flops 6 | bytes 24 | tf_op jit(solution)/shard_map/stack | solution.py:289
  83.7 5.9 %project.7.kr_ref.vr_ref = bf16[512,2048]{1,0:T(8,128)(2,1)} custom-call(bf16[512,1024]{1,0:T(8,128)(2,1)} %collective-permute-done.3.refs_0_, bf16[1,1024]{1,0:T(2,128)(2,1)} %reshape.7.refs_2_.refs_1_, bf16[1024,3072]{1,0:T(8,128)(2,1)} %refs_2_.3), custom_call_target="tpu_custom_call" | custom-call | flops 1 | bytes 1 | tf_op jit(solution)/shard_map/project/pallas_call | solution.py:101
  89.6 6.4 %attention_mirrored.4.mine_ref = bf16[512,256]{1,0:T(8,128)(2,1)} custom-call(s32[3]{0:T(128)} %pad_add_fusion.flags_ref, bf16[512,1024]{1,0:T(8,128)(2,1)} %get-tuple-element.33.q_ref, bf16[1024,2048]{1,0:T(8,128)(2,1)} %get-tuple-element.34.ko_ref.ks_ref.vo_ref.vs_ref, bf16[1024,2048]{1,0:T(8,128)(2,1)} %get-tuple-element.34.ko_ref.ks_ref.vo_ref.vs_ref, ...), custom_call_target="tpu_custom_call" | custom-call | flops 1 | bytes 1 | tf_op jit(solution)/shard_map/attention_mirrored/pallas_call | solution.py:198
  96.0 5.3 %collective-permute-start.6 = (bf16[512,256]{1,0:T(8,128)(2,1)}, bf16[512,256]{1,0:T(8,128)(2,1)}, u32[]{:S(2)}, u32[]{:S(2)}) collective-permute-start(bf16[512,256]{1,0:T(8,128)(2,1)} %attention_mirrored.4.mine_ref), channel_id=1, source_target_pairs={{0,31},{1,30},{2,29},{3,28},{4,27},{5,26},{6,25},{7,24},{8,23},{9,... | collective-permute-start | bytes 786440 | tf_op jit(solution)/shard_map/ppermute | solution.py:286
  101.4 6.4 %attention_mirrored.5.mine_ref = bf16[512,256]{1,0:T(8,128)(2,1)} custom-call(s32[3]{0:T(128)} %pad_add_fusion.flags_ref, bf16[512,1024]{1,0:T(8,128)(2,1)} %get-tuple-element.33.q_ref, bf16[1024,2048]{1,0:T(8,128)(2,1)} %get-tuple-element.34.ko_ref.ks_ref.vo_ref.vs_ref, bf16[1024,2048]{1,0:T(8,128)(2,1)} %get-tuple-element.34.ko_ref.ks_ref.vo_ref.vs_ref, ...), custom_call_target="tpu_custom_call" | custom-call | flops 1 | bytes 1 | tf_op jit(solution)/shard_map/attention_mirrored/pallas_call | solution.py:198
  107.8 24.9 %collective-permute-done.6.moved_ref = bf16[512,256]{1,0:T(8,128)(2,1)} collective-permute-done((bf16[512,256]{1,0:T(8,128)(2,1)}, bf16[512,256]{1,0:T(8,128)(2,1)}, u32[]{:S(2)}, u32[]{:S(2)}) %collective-permute-start.6) | collective-permute-done | bytes 262176 | tf_op jit(solution)/shard_map/ppermute | solution.py:286
  132.7 6.4 %attention_mirrored.6.mine_ref = bf16[512,256]{1,0:T(8,128)(2,1)} custom-call(s32[3]{0:T(128)} %pad_add_fusion.flags_ref, bf16[512,1024]{1,0:T(8,128)(2,1)} %get-tuple-element.33.q_ref, bf16[1024,2048]{1,0:T(8,128)(2,1)} %get-tuple-element.34.ko_ref.ks_ref.vo_ref.vs_ref, bf16[1024,2048]{1,0:T(8,128)(2,1)} %get-tuple-element.34.ko_ref.ks_ref.vo_ref.vs_ref, ...), custom_call_target="tpu_custom_call" | custom-call | flops 1 | bytes 1 | tf_op jit(solution)/shard_map/attention_mirrored/pallas_call | solution.py:198
  139.2 6.5 %attention_mirrored.7.mine_ref = bf16[512,256]{1,0:T(8,128)(2,1)} custom-call(s32[3]{0:T(128)} %pad_add_fusion.flags_ref, bf16[512,1024]{1,0:T(8,128)(2,1)} %get-tuple-element.33.q_ref, bf16[1024,2048]{1,0:T(8,128)(2,1)} %get-tuple-element.34.ko_ref.ks_ref.vo_ref.vs_ref, bf16[1024,2048]{1,0:T(8,128)(2,1)} %get-tuple-element.34.ko_ref.ks_ref.vo_ref.vs_ref, ...), custom_call_target="tpu_custom_call" | custom-call | flops 1 | bytes 1 | tf_op jit(solution)/shard_map/attention_mirrored/pallas_call | solution.py:198
  145.6 5.3 %collective-permute-start.8 = (bf16[512,256]{1,0:T(8,128)(2,1)}, bf16[512,256]{1,0:T(8,128)(2,1)}, u32[]{:S(2)}, u32[]{:S(2)}) collective-permute-start(bf16[512,256]{1,0:T(8,128)(2,1)} %attention_mirrored.7.mine_ref), channel_id=1, source_target_pairs={{0,31},{1,30},{2,29},{3,28},{4,27},{5,26},{6,25},{7,24},{8,23},{9,... | collective-permute-start | bytes 786440 | tf_op jit(solution)/shard_map/ppermute | solution.py:286
  151.0 2.5 %finish.4 = (bf16[512,1024]{1,0:T(8,128)(2,1)}, bf16[512,1024]{1,0:T(8,128)(2,1)}) custom-call(s32[3]{0:T(128)} %pad_add_fusion.flags_ref, bf16[512,256]{1,0:T(8,128)(2,1)} %attention_mirrored.4.mine_ref, bf16[512,256]{1,0:T(8,128)(2,1)} %collective-permute-done.6.moved_ref), custom_call_target="tpu_custom_call" | custom-call | flops 1 | bytes 1 | tf_op jit(solution)/shard_map/finish/pallas_call | solution.py:233
  153.4 2.5 %finish.5 = (bf16[512,1024]{1,0:T(8,128)(2,1)}, bf16[512,1024]{1,0:T(8,128)(2,1)}) custom-call(s32[3]{0:T(128)} %pad_add_fusion.flags_ref, bf16[512,256]{1,0:T(8,128)(2,1)} %attention_mirrored.5.mine_ref, bf16[512,256]{1,0:T(8,128)(2,1)} %collective-permute-done.5.moved_ref, ...), custom_call_target="tpu_custom_call", output_to_operand_aliasing={{0}: (3, {}), {1}: (4, {})} | custom-call | flops 1 | bytes 1 | tf_op jit(solution)/shard_map/finish/pallas_call | solution.py:233
  155.9 2.5 %finish.6 = (bf16[512,1024]{1,0:T(8,128)(2,1)}, bf16[512,1024]{1,0:T(8,128)(2,1)}) custom-call(s32[3]{0:T(128)} %pad_add_fusion.flags_ref, bf16[512,256]{1,0:T(8,128)(2,1)} %attention_mirrored.6.mine_ref, bf16[512,256]{1,0:T(8,128)(2,1)} %collective-permute-done.9.moved_ref, ...), custom_call_target="tpu_custom_call", output_to_operand_aliasing={{0}: (3, {}), {1}: (4, {})} | custom-call | flops 1 | bytes 1 | tf_op jit(solution)/shard_map/finish/pallas_call | solution.py:233
  158.4 2.5 %finish.7 = (bf16[512,1024]{1,0:T(8,128)(2,1)}, bf16[512,1024]{1,0:T(8,128)(2,1)}) custom-call(s32[3]{0:T(128)} %pad_add_fusion.flags_ref, bf16[512,256]{1,0:T(8,128)(2,1)} %attention_mirrored.7.mine_ref, bf16[512,256]{1,0:T(8,128)(2,1)} %collective-permute-done.8.moved_ref, ...), custom_call_target="tpu_custom_call", output_to_operand_aliasing={{0}: (3, {}), {1}: (4, {})} | custom-call | flops 1 | bytes 1 | tf_op jit(solution)/shard_map/finish/pallas_call | solution.py:233
  (19 shorter events, 2.8 us)
Async XLA Ops:
  0.6 6.2 %collective-permute-start.1 = (bf16[512,1024]{1,0:T(8,128)(2,1)}, bf16[512,1024]{1,0:T(8,128)(2,1)}, u32[]{:S(2)}, u32[]{:S(2)}) collective-permute-start(bf16[512,1024]{1,0:T(8,128)(2,1)} %refs_0_.2), channel_id=1, source_target_pairs={{0,1},{1,0},{2,3},{3,2},{4,5},{5,4},{6,7},{7,6},{8,9},{9,8},{10,11... | collective-permute-start | bytes 3145736 | tf_op jit(solution)/shard_map/ppermute | solution.py:286
  1.4 18.9 %collective-permute-start = (bf16[512,1024]{1,0:T(8,128)(2,1)}, bf16[512,1024]{1,0:T(8,128)(2,1)}, u32[]{:S(2)}, u32[]{:S(2)}) collective-permute-start(bf16[512,1024]{1,0:T(8,128)(2,1)} %refs_0_.2), channel_id=1, source_target_pairs={{1,2},{2,1},{3,4},{4,3},{5,6},{6,5},{7,8},{8,7},{9,10},{10,9},{11,... | collective-permute-start | bytes 3145736 | tf_op jit(solution)/shard_map/ppermute | solution.py:286
  20.3 38.2 %collective-permute-start.2 = (bf16[512,1024]{1,0:T(8,128)(2,1)}, bf16[512,1024]{1,0:T(8,128)(2,1)}, u32[]{:S(2)}, u32[]{:S(2)}) collective-permute-start(bf16[512,1024]{1,0:T(8,128)(2,1)} %refs_0_.3), channel_id=1, source_target_pairs={{0,1},{1,0},{2,3},{3,2},{4,5},{5,4},{6,7},{7,6},{8,9},{9,8},{10,11... | collective-permute-start | bytes 3145736 | tf_op jit(solution)/shard_map/ppermute | solution.py:286
  30.6 53.1 %collective-permute-start.3 = (bf16[512,1024]{1,0:T(8,128)(2,1)}, bf16[512,1024]{1,0:T(8,128)(2,1)}, u32[]{:S(2)}, u32[]{:S(2)}) collective-permute-start(bf16[512,1024]{1,0:T(8,128)(2,1)} %refs_0_.3), channel_id=1, source_target_pairs={{2,1},{1,2},{4,3},{3,4},{6,5},{5,6},{8,7},{7,8},{10,9},{9,10},{12,... | collective-permute-start | bytes 3145736 | tf_op jit(solution)/shard_map/ppermute | solution.py:286
  52.2 37.4 %collective-permute-start.4 = (bf16[512,512]{1,0:T(8,128)(2,1)}, bf16[512,512]{1,0:T(8,128)(2,1)}, u32[]{:S(2)}, u32[]{:S(2)}) collective-permute-start(bf16[512,512]{1,0:T(8,128)(2,1)} %attention.2), channel_id=1, source_target_pairs={{0,31},{1,30},{2,29},{3,28},{4,27},{5,26},{6,25},{7,24},{8,23},{9,... | collective-permute-start | bytes 1572872 | tf_op jit(solution)/shard_map/ppermute | solution.py:286
  69.8 10.8 %copy-start.1 = (s32[32]{0:T(128)S(1)}, s32[32]{0:T(128)}, u32[]{:S(2)}) copy-start(s32[32]{0:T(128)} %constant.29.clone) | copy-start | bytes 388
  69.8 11.4 %copy-start = (s32[32]{0:T(128)S(1)}, s32[32]{0:T(128)}, u32[]{:S(2)}) copy-start(s32[32]{0:T(128)} %constant.28.clone) | copy-start | bytes 388
  80.5 52.2 %collective-permute-start.7 = (bf16[512,512]{1,0:T(8,128)(2,1)}, bf16[512,512]{1,0:T(8,128)(2,1)}, u32[]{:S(2)}, u32[]{:S(2)}) collective-permute-start(bf16[512,512]{1,0:T(8,128)(2,1)} %attention.3), channel_id=1, source_target_pairs={{0,31},{1,30},{2,29},{3,28},{4,27},{5,26},{6,25},{7,24},{8,23},{9,... | collective-permute-start | bytes 1572872 | tf_op jit(solution)/shard_map/ppermute | solution.py:286
  96.0 36.7 %collective-permute-start.6 = (bf16[512,256]{1,0:T(8,128)(2,1)}, bf16[512,256]{1,0:T(8,128)(2,1)}, u32[]{:S(2)}, u32[]{:S(2)}) collective-permute-start(bf16[512,256]{1,0:T(8,128)(2,1)} %attention_mirrored.4.mine_ref), channel_id=1, source_target_pairs={{0,31},{1,30},{2,29},{3,28},{4,27},{5,26},{6,25},{7,24},{8,23},{9,... | collective-permute-start | bytes 786440 | tf_op jit(solution)/shard_map/ppermute | solution.py:286
  107.8 31.4 %collective-permute-start.5 = (bf16[512,256]{1,0:T(8,128)(2,1)}, bf16[512,256]{1,0:T(8,128)(2,1)}, u32[]{:S(2)}, u32[]{:S(2)}) collective-permute-start(bf16[512,256]{1,0:T(8,128)(2,1)} %attention_mirrored.5.mine_ref), channel_id=1, source_target_pairs={{0,31},{1,30},{2,29},{3,28},{4,27},{5,26},{6,25},{7,24},{8,23},{9,... | collective-permute-start | bytes 786440 | tf_op jit(solution)/shard_map/ppermute | solution.py:286
  139.1 16.8 %collective-permute-start.9 = (bf16[512,256]{1,0:T(8,128)(2,1)}, bf16[512,256]{1,0:T(8,128)(2,1)}, u32[]{:S(2)}, u32[]{:S(2)}) collective-permute-start(bf16[512,256]{1,0:T(8,128)(2,1)} %attention_mirrored.6.mine_ref), channel_id=1, source_target_pairs={{0,31},{1,30},{2,29},{3,28},{4,27},{5,26},{6,25},{7,24},{8,23},{9,... | collective-permute-start | bytes 786440 | tf_op jit(solution)/shard_map/ppermute | solution.py:286
  145.6 12.8 %collective-permute-start.8 = (bf16[512,256]{1,0:T(8,128)(2,1)}, bf16[512,256]{1,0:T(8,128)(2,1)}, u32[]{:S(2)}, u32[]{:S(2)}) collective-permute-start(bf16[512,256]{1,0:T(8,128)(2,1)} %attention_mirrored.7.mine_ref), channel_id=1, source_target_pairs={{0,31},{1,30},{2,29},{3,28},{4,27},{5,26},{6,25},{7,24},{8,23},{9,... | collective-permute-start | bytes 786440 | tf_op jit(solution)/shard_map/ppermute | solution.py:286
where the time goes:
time: 161 us
  Pallas kernels  90.3 us (56%)
  starting transfers between devices  36.8 us (23%)
  waiting for transfers between devices  28.1 us (17%)
  other arithmetic  2.56 us (2%)
  local copies, waits for them, and re-layouts  2.51 us (2%)
    pallas_call x6, Pallas kernels, attention(): pl.pallas_call(functools.partial(attention_kernel, min(256, rows), mirror...  47.2 us
    ppermute x10, starting transfers between devices, send(): return lax.ppermute(x, 'seq', pairs)  36.8 us
    pallas_call x4, Pallas kernels, project(): pl.pallas_call(functools.partial(project_kernel, scale, mirrored, with_q,...  33.2 us
    ppermute x10, waiting for transfers between devices, send(): return lax.ppermute(x, 'seq', pairs)  28.1 us
    pallas_call x4, Pallas kernels, finish(): pl.pallas_call(finish_kernel, out_shape=(out, out), grid=(piece // pw,),...  9.94 us
  transfers between devices with their start and end apart: 10, of which 2 were waited for; matrix products, arithmetic and copies ran while one was open for 3% of the time, Pallas kernels for 55%

commit v1 on v0

v1 whole, which is shorter than its diff:
```python
import functools

import jax
import jax.numpy as jnp
from jax import lax
from jax.experimental import pallas as pl
from jax.experimental.pallas import tpu as pltpu
from jax.sharding import PartitionSpec as P

HEADS = 16
WINDOW = 512
LOG2E = 1.4426950408889634
NEG = -1e30
SMALL = pl.CostEstimate(flops=1, bytes_accessed=1, transcendentals=0)
VMEM_LIMIT = 64 * 1024 * 1024 - 256 * 1024
CHUNKS = (2, 2, 2, 2)


def after(x, *others):
    return lax.optimization_barrier((x, *others))[0]


def exchange_matrix(n):
    r = lax.broadcasted_iota(jnp.int32, (n, n), 0)
    c = lax.broadcasted_iota(jnp.int32, (n, n), 1)
    return (r + c == n - 1).astype(jnp.bfloat16)


def rows_reversed(x, out_ref):
    half = x.shape[0] // 2
    ex = exchange_matrix(half)
    out_ref[:half] = jnp.dot(ex, x[half:], preferred_element_type=jnp.float32).astype(out_ref.dtype)
    out_ref[half:] = jnp.dot(ex, x[:half], preferred_element_type=jnp.float32).astype(out_ref.dtype)


def columns_reversed(x, out_ref):
    width = x.shape[1]
    size = min(256, width)
    ex = exchange_matrix(size)
    for n in range(width // size):
        t = jnp.dot(x[:, n * size : (n + 1) * size], ex, preferred_element_type=jnp.float32)
        out_ref[:, width - (n + 1) * size : width - n * size] = t.astype(out_ref.dtype)


def project_kernel(scale, mirrored, with_q, n, *refs):
    x_refs = refs[:n]
    gain_ref, w_ref = refs[n : n + 2]
    refs = refs[n + 2 :]
    if with_q:
        q_ref, kv_ref, hn_ref, turned_ref = refs
    else:
        kv_ref, hn_ref, turned_ref = refs
    j = pl.program_id(0)
    rows = x_refs[0].shape[0]

    @pl.when(j == 0)
    def _():
        for m in range(n):
            xf = x_refs[m][...].astype(jnp.float32)
            meansq = jnp.mean(xf * xf, axis=-1, keepdims=True)
            hn = xf * lax.rsqrt(meansq + 1e-6) * gain_ref[...].astype(jnp.float32)
            hn_ref[m * rows : (m + 1) * rows] = hn.astype(jnp.bfloat16)

    def product(h):
        return jnp.dot(h, w_ref[...], preferred_element_type=jnp.float32)

    first = 1 if with_q else 0
    if with_q:

        @pl.when(j == 0)
        def _():
            if mirrored:
                rows_reversed(hn_ref[:rows], turned_ref)
                q_ref[...] = (product(turned_ref[...]) * scale).astype(jnp.bfloat16)
            else:
                q_ref[...] = (product(hn_ref[:rows]) * scale).astype(jnp.bfloat16)

    @pl.when(j == first)
    def _():
        kv_ref[...] = product(hn_ref[...]).astype(jnp.bfloat16)

    @pl.when(j == first + 1)
    def _():
        v = product(hn_ref[...]).astype(jnp.bfloat16)
        if mirrored:
            columns_reversed(v, kv_ref)
        else:
            kv_ref[...] = v


def project(xs, gain, w, scale, mirrored, with_q, part=0, parts=1):
    rows, width = xs[0].shape
    n = len(xs)
    block = width // parts
    first = 1 if with_q else 0
    kv = jax.ShapeDtypeStruct((n * rows, 2 * block), jnp.bfloat16)
    kv_spec = pl.BlockSpec((n * rows, block), lambda j: (0, jnp.maximum(j - first, 0)))
    q = jax.ShapeDtypeStruct((rows, width), jnp.bfloat16)
    q_spec = pl.BlockSpec((rows, width), lambda j: (0, 0))
    return pl.pallas_call(
        functools.partial(project_kernel, scale, mirrored, with_q, n),
        out_shape=(q, kv) if with_q else kv,
        grid=(2 + first,),
        in_specs=[pl.BlockSpec((rows, width), lambda j: (0, 0))] * n
        + [
            pl.BlockSpec((1, width), lambda j: (0, 0)),
            pl.BlockSpec((width, block), lambda j: (0, parts * (j + 1 - first) + part)),
        ],
        out_specs=(q_spec, kv_spec) if with_q else kv_spec,
        scratch_shapes=[
            pltpu.VMEM((n * rows, width), jnp.bfloat16),
            pltpu.VMEM((rows, width), jnp.bfloat16),
        ],
        compiler_params=pltpu.CompilerParams(vmem_limit_bytes=VMEM_LIMIT),
        cost_estimate=SMALL,
        name="project",
    )(*xs, gain, w)


def attention_kernel(tile, mirrored, flags_ref, q_ref, ko_ref, ks_ref, kr_ref, vo_ref, vs_ref, vr_ref, *refs):
    if mirrored:
        near_ref, out_ref, kbuf, vbuf = refs
    else:
        out_ref, kbuf, vbuf = refs
    rows, width = q_ref.shape
    head = width // 2
    sibling_left = flags_ref[0] > 0
    has_remote = flags_ref[1] > 0
    at_s = pl.multiple_of(jnp.where(sibling_left, 0, 2 * rows), rows)
    at_r = pl.multiple_of(jnp.where(sibling_left, 2 * rows, 0), rows)
    ones = jnp.ones((rows, width), jnp.bfloat16)
    none = jnp.zeros((rows, width), jnp.bfloat16)
    kbuf[rows : 2 * rows] = ko_ref[...]
    vbuf[rows : 2 * rows, :width] = vo_ref[...]
    vbuf[rows : 2 * rows, width:] = ones
    kbuf[pl.ds(at_s, rows)] = ks_ref[...]
    vbuf[pl.ds(at_s, rows), :width] = vs_ref[...]
    vbuf[pl.ds(at_s, rows), width:] = ones
    kbuf[pl.ds(at_r, rows)] = jnp.where(has_remote, kr_ref[...], ko_ref[...])
    vbuf[pl.ds(at_r, rows), :width] = jnp.where(has_remote, vr_ref[...], none)
    vbuf[pl.ds(at_r, rows), width:] = jnp.where(has_remote, ones, none)

    span = tile + 2 * WINDOW
    r = lax.broadcasted_iota(jnp.int32, (tile, tile), 0)
    c = lax.broadcasted_iota(jnp.int32, (tile, tile), 1)
    if mirrored:
        r = tile - 1 - r
    low = c >= r
    high = c <= r
    lane = lax.broadcasted_iota(jnp.int32, (tile, width), 1)
    tiles = rows // tile
    for t in range(tiles):
        here = slice(t * tile, (t + 1) * tile)
        q = q_ref[here, :]
        first = (tiles - 1 - t if mirrored else t) * tile
        keys = kbuf[first : first + span, :]
        values = vbuf[first : first + span, :]
        outs = []
        for h in range(2):
            mine = (lane < head) if h == 0 else (lane >= head)
            qh = jnp.where(mine, q, jnp.zeros_like(q))
            s = lax.dot_general(
                qh, keys, (((1,), (1,)), ((), ())), preferred_element_type=jnp.float32
            )
            s_low = jnp.where(low, s[:, :tile], NEG)
            s_mid = s[:, tile : 2 * WINDOW]
            s_high = jnp.where(high, s[:, 2 * WINDOW :], NEG)
            s = jnp.concatenate([s_low, s_mid, s_high], axis=1)
            top = jnp.max(s, axis=-1, keepdims=True)
            p = jnp.exp2(s - top).astype(jnp.bfloat16)
            o = jnp.dot(p, values, preferred_element_type=jnp.float32)
            outs.append(o[:, :width] / o[:, width:])
        if mirrored:
            outs = outs[::-1]
        a = jnp.where(lane < head, outs[0], outs[1]).astype(jnp.bfloat16)
        if mirrored:
            a = (near_ref[here, :].astype(jnp.float32) + a.astype(jnp.float32)).astype(jnp.bfloat16)
        out_ref[here, :] = a


def attention(q, own, sibling, remote, flags, first, count, base=0, near=None):
    rows, width = q.shape
    pw = 2 * (width // HEADS)
    n = width // pw
    f = first
    mirrored = near is not None

    def key(g):
        return n - 1 - f - g if mirrored else f + g

    def keys(row):
        return pl.BlockSpec((rows, pw), lambda g: (row, key(g)))

    def values(row):
        return pl.BlockSpec((rows, pw), lambda g: (row, n + f + g))

    there = sibling.shape[0] // rows - 1
    held = remote.shape[1] // (2 * pw)
    remote_keys = pl.BlockSpec((rows, pw), lambda g: (0, key(g) - base))
    remote_values = pl.BlockSpec((rows, pw), lambda g: (0, held + f + g - base))
    out_spec = pl.BlockSpec((rows, pw), lambda g: (0, g))
    return pl.pallas_call(
        functools.partial(attention_kernel, min(256, rows), mirrored),
        out_shape=jax.ShapeDtypeStruct((rows, count * pw), jnp.bfloat16),
        grid=(count,),
        in_specs=[pl.BlockSpec(memory_space=pltpu.SMEM)]
        + [keys(0), keys(0), keys(there), remote_keys, values(0), values(there), remote_values]
        + [out_spec] * mirrored,
        out_specs=out_spec,
        scratch_shapes=[
            pltpu.VMEM((rows + 2 * WINDOW, pw), jnp.bfloat16),
            pltpu.VMEM((rows + 2 * WINDOW, 2 * pw), jnp.bfloat16),
        ],
        compiler_params=pltpu.CompilerParams(vmem_limit_bytes=VMEM_LIMIT),
        cost_estimate=pl.CostEstimate(
            flops=16 * count * rows * (256 + 2 * WINDOW) * 2 * pw,
            bytes_accessed=16 * count * rows * pw,
            transcendentals=0,
        ),
        name="attention_mirrored" if mirrored else "attention",
    )(flags, q, own, sibling, remote, own, sibling, remote, *([near] if mirrored else []))


def place_kernel(turned, piece_ref, *refs):
    out_ref = refs[-1]
    if turned:
        t = jnp.dot(piece_ref[...], exchange_matrix(piece_ref.shape[1]), preferred_element_type=jnp.float32)
        rows_reversed(t.astype(jnp.bfloat16), out_ref)
    else:
        out_ref[...] = piece_ref[...]


def place(piece, first, width, held, turned):
    rows, columns = piece.shape
    pw = 2 * (width // HEADS)
    n = width // pw
    f = first
    held = [] if held is None else [held]
    return pl.pallas_call(
        functools.partial(place_kernel, turned),
        out_shape=jax.ShapeDtypeStruct((rows, width), jnp.bfloat16),
        grid=(columns // pw,),
        in_specs=[pl.BlockSpec((rows, pw), lambda g: (0, g))]
        + [pl.BlockSpec(memory_space=pl.ANY)] * len(held),
        out_specs=pl.BlockSpec((rows, pw), lambda g: (0, n - 1 - f - g if turned else f + g)),
        input_output_aliases={1: 0} if held else {},
        compiler_params=pltpu.CompilerParams(vmem_limit_bytes=VMEM_LIMIT),
        cost_estimate=SMALL,
        name="place",
    )(piece, *held)


def per_device(x_fwd, x_rev, gain, w_qkv):
    count = lax.axis_size("seq")
    index = lax.axis_index("seq")
    rows, width = x_fwd.shape
    scale = (width // HEADS) ** (-0.5) * LOG2E
    gain = gain.reshape(1, width)
    sibling = [(i, i ^ 1) for i in range(count)]
    beside = [(i, i - 1 if i % 2 == 0 else i + 1) for i in range(1, count - 1)]
    mirror = [(i, count - 1 - i) for i in range(count)]
    firsts = [sum(CHUNKS[:k]) for k in range(len(CHUNKS))]
    half = HEADS // 4

    def send(x, pairs):
        return lax.ppermute(x, "seq", pairs)

    flags = jnp.stack([index % 2, ((index > 0) & (index < count - 1)).astype(jnp.int32)])

    f_x = send(x_fwd, beside)
    f_y = send(x_fwd, sibling)
    f_q, f_chip = project([x_fwd, f_y], gain, w_qkv, scale, False, True)
    s_q, s_own = project([after(x_rev, f_q)], gain, w_qkv, scale, True, True)
    s_x = send(after(x_rev, s_q), beside)

    s_sib = send(s_own, sibling)
    f_x = after(f_x, s_q)
    a_f, a_moved = [], []
    f_rem = None
    for k in range(len(CHUNKS)):
        if firsts[k] % half == 0:
            f_rem = project([f_x], gain, w_qkv, scale, False, False, firsts[k] // half, 2)
            flags = after(flags, f_rem)
        if k >= 2:
            a_moved[k - 2], flags = lax.optimization_barrier((a_moved[k - 2], flags))
        a = attention(f_q, f_chip, f_chip, f_rem, flags, firsts[k], CHUNKS[k], firsts[k] // half * half)
        flags, f_x = lax.optimization_barrier((flags, f_x, a))[:2]
        a_f.append(a)
        a_moved.append(send(a, mirror))
    s_rem = project([after(s_x, a_f[-1])], gain, w_qkv, scale, True, False)

    mine, moved, fwd, rev = [], [], None, None
    for k in range(len(CHUNKS)):
        if k >= 2:
            moved[k - 2], flags = lax.optimization_barrier((moved[k - 2], flags))
        ahead = min(k + 2, len(CHUNKS) - 1)
        a_moved[ahead], flags = lax.optimization_barrier((a_moved[ahead], flags))
        y = attention(s_q, s_own, s_sib, s_rem, flags, firsts[k], CHUNKS[k], 0, a_moved[k])
        flags = after(flags, y)
        mine.append(y)
        moved.append(send(y, mirror))
    for k in range(len(CHUNKS)):
        rev = place(mine[k], firsts[k], width, rev, True)
    for k in range(len(CHUNKS)):
        fwd = place(after(moved[k], rev), firsts[k], width, fwd, False)
    return fwd, rev


def solution(mesh):
    in_specs = (P(("dp", "seq"), None), P(("dp", "seq"), None), P(), P())
    out_specs = (P(("dp", "seq"), None), P(("dp", "seq"), None))
    return jax.shard_map(
        per_device, mesh=mesh, in_specs=in_specs, out_specs=out_specs, check_vma=False
    )
```

time: 161 us -> 169 us (1.050)
  the two profiles are of different devices: /device:TPU:25 before, /device:TPU:125 now
where the time goes in v1:
time: 169 us
  Pallas kernels  99.4 us (59%)
  starting transfers between devices  36.6 us (22%)
  waiting for transfers between devices  30.2 us (18%)
    pallas_call x8, Pallas kernels, attention(): pl.pallas_call(functools.partial(attention_kernel, min(256, rows), mirror...  51 us
    ppermute x12, starting transfers between devices, send(): return lax.ppermute(x, 'seq', pairs)  36.6 us
    pallas_call x5, Pallas kernels, project(): pl.pallas_call(functools.partial(project_kernel, scale, mirrored, with_q,...  32.5 us
    ppermute x12, waiting for transfers between devices, send(): return lax.ppermute(x, 'seq', pairs)  30.2 us
    pallas_call x8, Pallas kernels, place(): pl.pallas_call(functools.partial(place_kernel, turned), out_shape=jax.Sha...  15.9 us
  transfers between devices with their start and end apart: 12, of which 3 were waited for; matrix products, arithmetic and copies ran while one was open for 1% of the time, Pallas kernels for 57%

profile of v1, /device:TPU:125, one launch (start us, length us, event | category | flops | bytes accessed | tf_op | source)
XLA Modules:
  0.0 168.8 jit_solution(1933163119886344530)
XLA Ops:
  1.4 5.3 %collective-permute-start = (bf16[512,1024]{1,0:T(8,128)(2,1)}, bf16[512,1024]{1,0:T(8,128)(2,1)}, u32[]{:S(2)}, u32[]{:S(2)}) collective-permute-start(bf16[512,1024]{1,0:T(8,128)(2,1)} %refs_0_.1), channel_id=1, source_target_pairs={{1,2},{2,1},{3,4},{4,3},{5,6},{6,5},{7,8},{8,7},{9,10},{10,9},{11,... | collective-permute-start | bytes 3145736 | tf_op jit(solution)/shard_map/ppermute | solution.py:266
  8.0 10.4 %project.5 = (bf16[512,1024]{1,0:T(8,128)(2,1)}, bf16[1024,2048]{1,0:T(8,128)(2,1)}) custom-call(bf16[512,1024]{1,0:T(8,128)(2,1)} %refs_0_.1, bf16[512,1024]{1,0:T(8,128)(2,1)} %collective-permute-done.1.refs_1_, bf16[1,1024]{1,0:T(2,128)(2,1)} %reshape.7.refs_2_.refs_1_, bf16[1024,3072]{1,0:T(8,128)(2,1)} %refs_2_.7), custom_call_target="tpu_custom_call" | custom-call | flops 1 | bytes 1 | tf_op jit(solution)/shard_map/project/pallas_call | solution.py:100
  18.4 8.2 %project.6 = (bf16[512,1024]{1,0:T(8,128)(2,1)}, bf16[512,2048]{1,0:T(8,128)(2,1)}) custom-call(bf16[512,1024]{1,0:T(8,128)(2,1)} %refs_0_.2, bf16[1,1024]{1,0:T(2,128)(2,1)} %reshape.7.refs_2_.refs_1_, bf16[1024,3072]{1,0:T(8,128)(2,1)} %refs_2_.7), custom_call_target="tpu_custom_call" | custom-call | flops 1 | bytes 1 | tf_op jit(solution)/shard_map/project/pallas_call | solution.py:100
  27.2 4.0 %project.7.kr_ref.vr_ref = bf16[512,1024]{1,0:T(8,128)(2,1)} custom-call(bf16[512,1024]{1,0:T(8,128)(2,1)} %collective-permute-done.refs_0_, bf16[1,1024]{1,0:T(2,128)(2,1)} %reshape.7.refs_2_.refs_1_, bf16[1024,3072]{1,0:T(8,128)(2,1)} %refs_2_.7), custom_call_target="tpu_custom_call" | custom-call | flops 1 | bytes 1 | tf_op jit(solution)/shard_map/project/pallas_call | solution.py:100
  31.2 6.3 %attention.4 = bf16[512,256]{1,0:T(8,128)(2,1)} custom-call(s32[2]{0:T(128)} %pad_add_fusion.flags_ref, bf16[512,1024]{1,0:T(8,128)(2,1)} %get-tuple-element.41.q_ref, bf16[1024,2048]{1,0:T(8,128)(2,1)} %get-tuple-element.46.ko_ref.ks_ref.vo_ref.vs_ref, bf16[1024,2048]{1,0:T(8,128)(2,1)} %get-tuple-element.46.ko_ref.ks_ref.vo_ref.vs_ref, ...), custom_call_target="tpu_custom_call" | custom-call | flops 5368709120 | bytes 2097152 | tf_op jit(solution)/shard_map/attention/pallas_call | solution.py:202
  37.5 2.4 %collective-permute-start.3 = (bf16[512,256]{1,0:T(8,128)(2,1)}, bf16[512,256]{1,0:T(8,128)(2,1)}, u32[]{:S(2)}, u32[]{:S(2)}) collective-permute-start(bf16[512,256]{1,0:T(8,128)(2,1)} %attention.4), channel_id=1, source_target_pairs={{0,31},{1,30},{2,29},{3,28},{4,27},{5,26},{6,25},{7,24},{8,23},{9,... | collective-permute-start | bytes 786440 | tf_op jit(solution)/shard_map/ppermute | solution.py:266
  39.9 4.9 %collective-permute-start.7 = (bf16[512,1024]{1,0:T(8,128)(2,1)}, bf16[512,1024]{1,0:T(8,128)(2,1)}, u32[]{:S(2)}, u32[]{:S(2)}) collective-permute-start(bf16[512,1024]{1,0:T(8,128)(2,1)} %refs_0_.2), channel_id=1, source_target_pairs={{1,2},{2,1},{3,4},{4,3},{5,6},{6,5},{7,8},{8,7},{9,10},{10,9},{11,... | collective-permute-start | bytes 3145736 | tf_op jit(solution)/shard_map/ppermute | solution.py:266
  44.8 6.3 %attention.5 = bf16[512,256]{1,0:T(8,128)(2,1)} custom-call(s32[2]{0:T(128)} %pad_add_fusion.flags_ref, bf16[512,1024]{1,0:T(8,128)(2,1)} %get-tuple-element.41.q_ref, bf16[1024,2048]{1,0:T(8,128)(2,1)} %get-tuple-element.46.ko_ref.ks_ref.vo_ref.vs_ref, bf16[1024,2048]{1,0:T(8,128)(2,1)} %get-tuple-element.46.ko_ref.ks_ref.vo_ref.vs_ref, ...), custom_call_target="tpu_custom_call" | custom-call | flops 5368709120 | bytes 2097152 | tf_op jit(solution)/shard_map/attention/pallas_call | solution.py:202
  51.1 2.4 %collective-permute-start.2 = (bf16[512,256]{1,0:T(8,128)(2,1)}, bf16[512,256]{1,0:T(8,128)(2,1)}, u32[]{:S(2)}, u32[]{:S(2)}) collective-permute-start(bf16[512,256]{1,0:T(8,128)(2,1)} %attention.5), channel_id=1, source_target_pairs={{0,31},{1,30},{2,29},{3,28},{4,27},{5,26},{6,25},{7,24},{8,23},{9,... | collective-permute-start | bytes 786440 | tf_op jit(solution)/shard_map/ppermute | solution.py:266
  53.5 4.0 %project.8.kr_ref.vr_ref = bf16[512,1024]{1,0:T(8,128)(2,1)} custom-call(bf16[512,1024]{1,0:T(8,128)(2,1)} %collective-permute-done.refs_0_, bf16[1,1024]{1,0:T(2,128)(2,1)} %reshape.7.refs_2_.refs_1_, bf16[1024,3072]{1,0:T(8,128)(2,1)} %refs_2_.7), custom_call_target="tpu_custom_call" | custom-call | flops 1 | bytes 1 | tf_op jit(solution)/shard_map/project/pallas_call | solution.py:100
  57.5 6.3 %attention.6 = bf16[512,256]{1,0:T(8,128)(2,1)} custom-call(s32[2]{0:T(128)} %pad_add_fusion.flags_ref, bf16[512,1024]{1,0:T(8,128)(2,1)} %get-tuple-element.41.q_ref, bf16[1024,2048]{1,0:T(8,128)(2,1)} %get-tuple-element.46.ko_ref.ks_ref.vo_ref.vs_ref, bf16[1024,2048]{1,0:T(8,128)(2,1)} %get-tuple-element.46.ko_ref.ks_ref.vo_ref.vs_ref, ...), custom_call_target="tpu_custom_call" | custom-call | flops 5368709120 | bytes 2097152 | tf_op jit(solution)/shard_map/attention/pallas_call | solution.py:202
  63.9 3.0 %collective-permute-start.5 = (bf16[512,256]{1,0:T(8,128)(2,1)}, bf16[512,256]{1,0:T(8,128)(2,1)}, u32[]{:S(2)}, u32[]{:S(2)}) collective-permute-start(bf16[512,256]{1,0:T(8,128)(2,1)} %attention.6), channel_id=1, source_target_pairs={{0,31},{1,30},{2,29},{3,28},{4,27},{5,26},{6,25},{7,24},{8,23},{9,... | collective-permute-start | bytes 786440 | tf_op jit(solution)/shard_map/ppermute | solution.py:266
  66.8 22.2 %collective-permute-done.2.refs_0_ = bf16[512,256]{1,0:T(8,128)(2,1)} collective-permute-done((bf16[512,256]{1,0:T(8,128)(2,1)}, bf16[512,256]{1,0:T(8,128)(2,1)}, u32[]{:S(2)}, u32[]{:S(2)}) %collective-permute-start.2) | collective-permute-done | bytes 262176 | tf_op jit(solution)/shard_map/ppermute | solution.py:266
  89.0 6.4 %attention.7 = bf16[512,256]{1,0:T(8,128)(2,1)} custom-call(s32[2]{0:T(128)} %pad_add_fusion.flags_ref, bf16[512,1024]{1,0:T(8,128)(2,1)} %get-tuple-element.41.q_ref, bf16[1024,2048]{1,0:T(8,128)(2,1)} %get-tuple-element.46.ko_ref.ks_ref.vo_ref.vs_ref, bf16[1024,2048]{1,0:T(8,128)(2,1)} %get-tuple-element.46.ko_ref.ks_ref.vo_ref.vs_ref, ...), custom_call_target="tpu_custom_call" | custom-call | flops 5368709120 | bytes 2097152 | tf_op jit(solution)/shard_map/attention/pallas_call | solution.py:202
  95.3 6.2 %collective-permute-start.4 = (bf16[512,256]{1,0:T(8,128)(2,1)}, bf16[512,256]{1,0:T(8,128)(2,1)}, u32[]{:S(2)}, u32[]{:S(2)}) collective-permute-start(bf16[512,256]{1,0:T(8,128)(2,1)} %attention.7), channel_id=1, source_target_pairs={{0,31},{1,30},{2,29},{3,28},{4,27},{5,26},{6,25},{7,24},{8,23},{9,... | collective-permute-start | bytes 786440 | tf_op jit(solution)/shard_map/ppermute | solution.py:266
  101.6 5.9 %project.9.kr_ref.vr_ref = bf16[512,2048]{1,0:T(8,128)(2,1)} custom-call(bf16[512,1024]{1,0:T(8,128)(2,1)} %collective-permute-done.7.refs_0_, bf16[1,1024]{1,0:T(2,128)(2,1)} %reshape.7.refs_2_.refs_1_, bf16[1024,3072]{1,0:T(8,128)(2,1)} %refs_2_.7), custom_call_target="tpu_custom_call" | custom-call | flops 1 | bytes 1 | tf_op jit(solution)/shard_map/project/pallas_call | solution.py:100
  107.5 6.4 %attention_mirrored.4.piece_ref = bf16[512,256]{1,0:T(8,128)(2,1)} custom-call(s32[2]{0:T(128)} %pad_add_fusion.flags_ref, bf16[512,1024]{1,0:T(8,128)(2,1)} %get-tuple-element.43.q_ref, bf16[512,2048]{1,0:T(8,128)(2,1)} %get-tuple-element.57.ko_ref.vo_ref, bf16[512,2048]{1,0:T(8,128)(2,1)} %collective-permute-done.6.ks_ref.vs_ref, ...), custom_call_target="tpu_custom_call" | custom-call | flops 5368709120 | bytes 2097152 | tf_op jit(solution)/shard_map/attention_mirrored/pallas_call | solution.py:202
  113.9 6.4 %attention_mirrored.5.piece_ref = bf16[512,256]{1,0:T(8,128)(2,1)} custom-call(s32[2]{0:T(128)} %pad_add_fusion.flags_ref, bf16[512,1024]{1,0:T(8,128)(2,1)} %get-tuple-element.43.q_ref, bf16[512,2048]{1,0:T(8,128)(2,1)} %get-tuple-element.57.ko_ref.vo_ref, bf16[512,2048]{1,0:T(8,128)(2,1)} %collective-permute-done.6.ks_ref.vs_ref, ...), custom_call_target="tpu_custom_call" | custom-call | flops 5368709120 | bytes 2097152 | tf_op jit(solution)/shard_map/attention_mirrored/pallas_call | solution.py:202
  120.4 5.3 %collective-permute-start.9 = (bf16[512,256]{1,0:T(8,128)(2,1)}, bf16[512,256]{1,0:T(8,128)(2,1)}, u32[]{:S(2)}, u32[]{:S(2)}) collective-permute-start(bf16[512,256]{1,0:T(8,128)(2,1)} %attention_mirrored.5.piece_ref), channel_id=1, source_target_pairs={{0,31},{1,30},{2,29},{3,28},{4,27},{5,26},{6,25},{7,24},{8,23},{9,... | collective-permute-start | bytes 786440 | tf_op jit(solution)/shard_map/ppermute | solution.py:266
  125.7 4.5 %collective-permute-done.8.piece_ref = bf16[512,256]{1,0:T(8,128)(2,1)} collective-permute-done((bf16[512,256]{1,0:T(8,128)(2,1)}, bf16[512,256]{1,0:T(8,128)(2,1)}, u32[]{:S(2)}, u32[]{:S(2)}) %collective-permute-start.8) | collective-permute-done | bytes 262176 | tf_op jit(solution)/shard_map/ppermute | solution.py:266
  130.2 6.4 %attention_mirrored.6.piece_ref = bf16[512,256]{1,0:T(8,128)(2,1)} custom-call(s32[2]{0:T(128)} %pad_add_fusion.flags_ref, bf16[512,1024]{1,0:T(8,128)(2,1)} %get-tuple-element.43.q_ref, bf16[512,2048]{1,0:T(8,128)(2,1)} %get-tuple-element.57.ko_ref.vo_ref, bf16[512,2048]{1,0:T(8,128)(2,1)} %collective-permute-done.6.ks_ref.vs_ref, ...), custom_call_target="tpu_custom_call" | custom-call | flops 5368709120 | bytes 2097152 | tf_op jit(solution)/shard_map/attention_mirrored/pallas_call | solution.py:202
  136.8 3.5 %collective-permute-done.9.piece_ref = bf16[512,256]{1,0:T(8,128)(2,1)} collective-permute-done((bf16[512,256]{1,0:T(8,128)(2,1)}, bf16[512,256]{1,0:T(8,128)(2,1)}, u32[]{:S(2)}, u32[]{:S(2)}) %collective-permute-start.9) | collective-permute-done | bytes 262176 | tf_op jit(solution)/shard_map/ppermute | solution.py:266
  140.4 6.4 %attention_mirrored.7.piece_ref = bf16[512,256]{1,0:T(8,128)(2,1)} custom-call(s32[2]{0:T(128)} %pad_add_fusion.flags_ref, bf16[512,1024]{1,0:T(8,128)(2,1)} %get-tuple-element.43.q_ref, bf16[512,2048]{1,0:T(8,128)(2,1)} %get-tuple-element.57.ko_ref.vo_ref, bf16[512,2048]{1,0:T(8,128)(2,1)} %collective-permute-done.6.ks_ref.vs_ref, ...), custom_call_target="tpu_custom_call" | custom-call | flops 5368709120 | bytes 2097152 | tf_op jit(solution)/shard_map/attention_mirrored/pallas_call | solution.py:202
  146.8 6.1 %collective-permute-start.10 = (bf16[512,256]{1,0:T(8,128)(2,1)}, bf16[512,256]{1,0:T(8,128)(2,1)}, u32[]{:S(2)}, u32[]{:S(2)}) collective-permute-start(bf16[512,256]{1,0:T(8,128)(2,1)} %attention_mirrored.7.piece_ref), channel_id=1, source_target_pairs={{0,31},{1,30},{2,29},{3,28},{4,27},{5,26},{6,25},{7,24},{8,23},{9,... | collective-permute-start | bytes 786440 | tf_op jit(solution)/shard_map/ppermute | solution.py:266
  (23 shorter events, 18.8 us)
Async XLA Ops:
  0.6 7.4 %collective-permute-start.1 = (bf16[512,1024]{1,0:T(8,128)(2,1)}, bf16[512,1024]{1,0:T(8,128)(2,1)}, u32[]{:S(2)}, u32[]{:S(2)}) collective-permute-start(bf16[512,1024]{1,0:T(8,128)(2,1)} %refs_0_.1), channel_id=1, source_target_pairs={{0,1},{1,0},{2,3},{3,2},{4,5},{5,4},{6,7},{7,6},{8,9},{9,8},{10,11... | collective-permute-start | bytes 3145736 | tf_op jit(solution)/shard_map/ppermute | solution.py:266
  1.4 25.8 %collective-permute-start = (bf16[512,1024]{1,0:T(8,128)(2,1)}, bf16[512,1024]{1,0:T(8,128)(2,1)}, u32[]{:S(2)}, u32[]{:S(2)}) collective-permute-start(bf16[512,1024]{1,0:T(8,128)(2,1)} %refs_0_.1), channel_id=1, source_target_pairs={{1,2},{2,1},{3,4},{4,3},{5,6},{6,5},{7,8},{8,7},{9,10},{10,9},{11,... | collective-permute-start | bytes 3145736 | tf_op jit(solution)/shard_map/ppermute | solution.py:266
  26.6 80.9 %collective-permute-start.6 = (bf16[512,2048]{1,0:T(8,128)(2,1)}, bf16[512,2048]{1,0:T(8,128)(2,1)}, u32[]{:S(2)}, u32[]{:S(2)}) collective-permute-start(bf16[512,2048]{1,0:T(8,128)(2,1)} %get-tuple-element.57.ko_ref.vo_ref), channel_id=1, source_target_pairs={{0,1},{1,0},{2,3},{3,2},{4,5},{5,4},{6,7},{7,6},{8,9},{9,8},{10,11... | collective-permute-start | bytes 6291464 | tf_op jit(solution)/shard_map/ppermute | solution.py:266
  37.5 20.0 %collective-permute-start.3 = (bf16[512,256]{1,0:T(8,128)(2,1)}, bf16[512,256]{1,0:T(8,128)(2,1)}, u32[]{:S(2)}, u32[]{:S(2)}) collective-permute-start(bf16[512,256]{1,0:T(8,128)(2,1)} %attention.4), channel_id=1, source_target_pairs={{0,31},{1,30},{2,29},{3,28},{4,27},{5,26},{6,25},{7,24},{8,23},{9,... | collective-permute-start | bytes 786440 | tf_op jit(solution)/shard_map/ppermute | solution.py:266
  39.9 61.7 %collective-permute-start.7 = (bf16[512,1024]{1,0:T(8,128)(2,1)}, bf16[512,1024]{1,0:T(8,128)(2,1)}, u32[]{:S(2)}, u32[]{:S(2)}) collective-permute-start(bf16[512,1024]{1,0:T(8,128)(2,1)} %refs_0_.2), channel_id=1, source_target_pairs={{1,2},{2,1},{3,4},{4,3},{5,6},{6,5},{7,8},{8,7},{9,10},{10,9},{11,... | collective-permute-start | bytes 3145736 | tf_op jit(solution)/shard_map/ppermute | solution.py:266
  51.1 37.9 %collective-permute-start.2 = (bf16[512,256]{1,0:T(8,128)(2,1)}, bf16[512,256]{1,0:T(8,128)(2,1)}, u32[]{:S(2)}, u32[]{:S(2)}) collective-permute-start(bf16[512,256]{1,0:T(8,128)(2,1)} %attention.5), channel_id=1, source_target_pairs={{0,31},{1,30},{2,29},{3,28},{4,27},{5,26},{6,25},{7,24},{8,23},{9,... | collective-permute-start | bytes 786440 | tf_op jit(solution)/shard_map/ppermute | solution.py:266
  63.9 37.7 %collective-permute-start.5 = (bf16[512,256]{1,0:T(8,128)(2,1)}, bf16[512,256]{1,0:T(8,128)(2,1)}, u32[]{:S(2)}, u32[]{:S(2)}) collective-permute-start(bf16[512,256]{1,0:T(8,128)(2,1)} %attention.6), channel_id=1, source_target_pairs={{0,31},{1,30},{2,29},{3,28},{4,27},{5,26},{6,25},{7,24},{8,23},{9,... | collective-permute-start | bytes 786440 | tf_op jit(solution)/shard_map/ppermute | solution.py:266
  95.3 18.6 %collective-permute-start.4 = (bf16[512,256]{1,0:T(8,128)(2,1)}, bf16[512,256]{1,0:T(8,128)(2,1)}, u32[]{:S(2)}, u32[]{:S(2)}) collective-permute-start(bf16[512,256]{1,0:T(8,128)(2,1)} %attention.7), channel_id=1, source_target_pairs={{0,31},{1,30},{2,29},{3,28},{4,27},{5,26},{6,25},{7,24},{8,23},{9,... | collective-permute-start | bytes 786440 | tf_op jit(solution)/shard_map/ppermute | solution.py:266
  113.9 16.3 %collective-permute-start.8 = (bf16[512,256]{1,0:T(8,128)(2,1)}, bf16[512,256]{1,0:T(8,128)(2,1)}, u32[]{:S(2)}, u32[]{:S(2)}) collective-permute-start(bf16[512,256]{1,0:T(8,128)(2,1)} %attention_mirrored.4.piece_ref), channel_id=1, source_target_pairs={{0,31},{1,30},{2,29},{3,28},{4,27},{5,26},{6,25},{7,24},{8,23},{9,... | collective-permute-start | bytes 786440 | tf_op jit(solution)/shard_map/ppermute | solution.py:266
  120.4 20.0 %collective-permute-start.9 = (bf16[512,256]{1,0:T(8,128)(2,1)}, bf16[512,256]{1,0:T(8,128)(2,1)}, u32[]{:S(2)}, u32[]{:S(2)}) collective-permute-start(bf16[512,256]{1,0:T(8,128)(2,1)} %attention_mirrored.5.piece_ref), channel_id=1, source_target_pairs={{0,31},{1,30},{2,29},{3,28},{4,27},{5,26},{6,25},{7,24},{8,23},{9,... | collective-permute-start | bytes 786440 | tf_op jit(solution)/shard_map/ppermute | solution.py:266
  136.6 28.9 %collective-permute-start.11 = (bf16[512,256]{1,0:T(8,128)(2,1)}, bf16[512,256]{1,0:T(8,128)(2,1)}, u32[]{:S(2)}, u32[]{:S(2)}) collective-permute-start(bf16[512,256]{1,0:T(8,128)(2,1)} %attention_mirrored.6.piece_ref), channel_id=1, source_target_pairs={{0,31},{1,30},{2,29},{3,28},{4,27},{5,26},{6,25},{7,24},{8,23},{9,... | collective-permute-start | bytes 786440 | tf_op jit(solution)/shard_map/ppermute | solution.py:266
  146.8 18.7 %collective-permute-start.10 = (bf16[512,256]{1,0:T(8,128)(2,1)}, bf16[512,256]{1,0:T(8,128)(2,1)}, u32[]{:S(2)}, u32[]{:S(2)}) collective-permute-start(bf16[512,256]{1,0:T(8,128)(2,1)} %attention_mirrored.7.piece_ref), channel_id=1, source_target_pairs={{0,31},{1,30},{2,29},{3,28},{4,27},{5,26},{6,25},{7,24},{8,23},{9,... | collective-permute-start | bytes 786440 | tf_op jit(solution)/shard_map/ppermute | solution.py:266

commit v2 on v1

--- a/solution.py
+++ b/solution.py
@@ -13,7 +13,7 @@
 NEG = -1e30
 SMALL = pl.CostEstimate(flops=1, bytes_accessed=1, transcendentals=0)
 VMEM_LIMIT = 64 * 1024 * 1024 - 256 * 1024
-CHUNKS = (2, 2, 2, 2)
+CHUNKS = (2, 3, 3)
 
 
 def after(x, *others):
@@ -178,7 +178,7 @@
         out_ref[here, :] = a
 
 
-def attention(q, own, sibling, remote, flags, first, count, base=0, near=None):
+def attention(q, own, sibling, remote, flags, first, count, near=None):
     rows, width = q.shape
     pw = 2 * (width // HEADS)
     n = width // pw
@@ -196,8 +196,8 @@
 
     there = sibling.shape[0] // rows - 1
     held = remote.shape[1] // (2 * pw)
-    remote_keys = pl.BlockSpec((rows, pw), lambda g: (0, key(g) - base))
-    remote_values = pl.BlockSpec((rows, pw), lambda g: (0, held + f + g - base))
+    remote_keys = pl.BlockSpec((rows, pw), lambda g: (0, key(g)))
+    remote_values = pl.BlockSpec((rows, pw), lambda g: (0, held + f + g))
     out_spec = pl.BlockSpec((rows, pw), lambda g: (0, g))
     return pl.pallas_call(
         functools.partial(attention_kernel, min(256, rows), mirrored),
@@ -213,8 +213,8 @@
         ],
         compiler_params=pltpu.CompilerParams(vmem_limit_bytes=VMEM_LIMIT),
         cost_estimate=pl.CostEstimate(
-            flops=16 * count * rows * (256 + 2 * WINDOW) * 2 * pw,
-            bytes_accessed=16 * count * rows * pw,
+            flops=4 * count * rows * (256 + 2 * WINDOW) * 2 * pw,
+            bytes_accessed=4 * count * rows * pw,
             transcendentals=0,
         ),
         name="attention_mirrored" if mirrored else "attention",
@@ -260,7 +260,7 @@
     beside = [(i, i - 1 if i % 2 == 0 else i + 1) for i in range(1, count - 1)]
     mirror = [(i, count - 1 - i) for i in range(count)]
     firsts = [sum(CHUNKS[:k]) for k in range(len(CHUNKS))]
-    half = HEADS // 4
+    parts = HEADS // 2 // CHUNKS[0]
 
     def send(x, pairs):
         return lax.ppermute(x, "seq", pairs)
@@ -269,39 +269,41 @@
 
     f_x = send(x_fwd, beside)
     f_y = send(x_fwd, sibling)
+    s_y = send(x_rev, sibling)
     f_q, f_chip = project([x_fwd, f_y], gain, w_qkv, scale, False, True)
-    s_q, s_own = project([after(x_rev, f_q)], gain, w_qkv, scale, True, True)
+    s_q, s_chip = project([after(x_rev, f_q), s_y], gain, w_qkv, scale, True, True)
     s_x = send(after(x_rev, s_q), beside)
 
-    s_sib = send(s_own, sibling)
+    a_moved = []
     f_x = after(f_x, s_q)
-    a_f, a_moved = [], []
-    f_rem = None
+    f_rem = project([f_x], gain, w_qkv, scale, False, False, 0, parts)
+    flags = after(flags, f_rem)
     for k in range(len(CHUNKS)):
-        if firsts[k] % half == 0:
-            f_rem = project([f_x], gain, w_qkv, scale, False, False, firsts[k] // half, 2)
-            flags = after(flags, f_rem)
+        if k == 2:
+            a_moved[0], s_x, flags = lax.optimization_barrier((a_moved[0], s_x, flags))
+        a = attention(f_q, f_chip, f_chip, f_rem, flags, firsts[k], CHUNKS[k])
+        flags = after(flags, a)
+        if k == 0:
+            f_rem = project([after(f_x, a)], gain, w_qkv, scale, False, False)
+        a_moved.append(send(a, mirror))
+    s_rem = project([after(s_x, a)], gain, w_qkv, scale, True, False)
+
+    mine, moved, fwd, rev = [], [], None, None
+    last = len(CHUNKS) - 1
+    for k in range(last + 1):
+        ahead = min(k + 1, last)
+        a_moved[ahead], flags = lax.optimization_barrier((a_moved[ahead], flags))
         if k >= 2:
-            a_moved[k - 2], flags = lax.optimization_barrier((a_moved[k - 2], flags))
-        a = attention(f_q, f_chip, f_chip, f_rem, flags, firsts[k], CHUNKS[k], firsts[k] // half * half)
-        flags, f_x = lax.optimization_barrier((flags, f_x, a))[:2]
-        a_f.append(a)
-        a_moved.append(send(a, mirror))
-    s_rem = project([after(s_x, a_f[-1])], gain, w_qkv, scale, True, False)
-
-    mine, moved, fwd, rev = [], [], None, None
-    for k in range(len(CHUNKS)):
-        if k >= 2:
-            moved[k - 2], flags = lax.optimization_barrier((moved[k - 2], flags))
-        ahead = min(k + 2, len(CHUNKS) - 1)
-        a_moved[ahead], flags = lax.optimization_barrier((a_moved[ahead], flags))
-        y = attention(s_q, s_own, s_sib, s_rem, flags, firsts[k], CHUNKS[k], 0, a_moved[k])
+            rev = place(after(mine[k - 2], mine[k - 1]), firsts[k - 2], width, rev, True)
+            fwd = place(after(moved[k - 2], rev), firsts[k - 2], width, fwd, False)
+            flags = after(flags, fwd)
+        y = attention(s_q, s_chip, s_chip, s_rem, flags, firsts[k], CHUNKS[k], a_moved[k])
         flags = after(flags, y)
         mine.append(y)
         moved.append(send(y, mirror))
-    for k in range(len(CHUNKS)):
-        rev = place(mine[k], firsts[k], width, rev, True)
-    for k in range(len(CHUNKS)):
+    for k in (last - 1, last):
+        rev = place(after(mine[k], mine[-1]), firsts[k], width, rev, True)
+    for k in (last - 1, last):
         fwd = place(after(moved[k], rev), firsts[k], width, fwd, False)
     return fwd, rev
 

time: 169 us -> 157 us (0.929)
  the two profiles are of different devices: /device:TPU:125 before, /device:TPU:25 now
where the time goes in v2:
time: 157 us
  Pallas kernels  99.3 us (63%)
  waiting for transfers between devices  28.8 us (18%)
  starting transfers between devices  26.2 us (17%)
    pallas_call x6, Pallas kernels, attention(): pl.pallas_call(functools.partial(attention_kernel, min(256, rows), mirror...  47.2 us
    pallas_call x5, Pallas kernels, project(): pl.pallas_call(functools.partial(project_kernel, scale, mirrored, with_q,...  36.4 us
    ppermute x10, waiting for transfers between devices, send(): return lax.ppermute(x, 'seq', pairs)  28.8 us
    ppermute x10, starting transfers between devices, send(): return lax.ppermute(x, 'seq', pairs)  26.2 us
    pallas_call x6, Pallas kernels, place(): pl.pallas_call(functools.partial(place_kernel, turned), out_shape=jax.Sha...  15.7 us
  transfers between devices with their start and end apart: 10, of which 2 were waited for; matrix products, arithmetic and copies ran while one was open for 1% of the time, Pallas kernels for 62%

profile of v2, /device:TPU:25, one launch (start us, length us, event | category | flops | bytes accessed | tf_op | source)
XLA Modules:
  0.0 156.9 jit_solution(15350067389061116967)
XLA Ops:
  1.5 4.5 %collective-permute-start = (bf16[512,1024]{1,0:T(8,128)(2,1)}, bf16[512,1024]{1,0:T(8,128)(2,1)}, u32[]{:S(2)}, u32[]{:S(2)}) collective-permute-start(bf16[512,1024]{1,0:T(8,128)(2,1)} %refs_0_.1), channel_id=1, source_target_pairs={{1,2},{2,1},{3,4},{4,3},{5,6},{6,5},{7,8},{8,7},{9,10},{10,9},{11,... | collective-permute-start | bytes 3145736 | tf_op jit(solution)/shard_map/ppermute | solution.py:266
  7.3 10.4 %project.5 = (bf16[512,1024]{1,0:T(8,128)(2,1)}, bf16[1024,2048]{1,0:T(8,128)(2,1)}) custom-call(bf16[512,1024]{1,0:T(8,128)(2,1)} %refs_0_.1, bf16[512,1024]{1,0:T(8,128)(2,1)} %collective-permute-done.1.refs_1_, bf16[1,1024]{1,0:T(2,128)(2,1)} %reshape.7.refs_2_.refs_1_, bf16[1024,3072]{1,0:T(8,128)(2,1)} %refs_2_.5), custom_call_target="tpu_custom_call" | custom-call | flops 1 | bytes 1 | tf_op jit(solution)/shard_map/project/pallas_call | solution.py:100
  17.7 11.2 %project.6 = (bf16[512,1024]{1,0:T(8,128)(2,1)}, bf16[1024,2048]{1,0:T(8,128)(2,1)}) custom-call(bf16[512,1024]{1,0:T(8,128)(2,1)} %refs_0_.2, bf16[512,1024]{1,0:T(8,128)(2,1)} %collective-permute-done.2.refs_1_, bf16[1,1024]{1,0:T(2,128)(2,1)} %reshape.7.refs_2_.refs_1_, bf16[1024,3072]{1,0:T(8,128)(2,1)} %refs_2_.5), custom_call_target="tpu_custom_call" | custom-call | flops 1 | bytes 1 | tf_op jit(solution)/shard_map/project/pallas_call | solution.py:100
  28.9 3.6 %collective-permute-start.4 = (bf16[512,1024]{1,0:T(8,128)(2,1)}, bf16[512,1024]{1,0:T(8,128)(2,1)}, u32[]{:S(2)}, u32[]{:S(2)}) collective-permute-start(bf16[512,1024]{1,0:T(8,128)(2,1)} %refs_0_.2), channel_id=1, source_target_pairs={{1,2},{2,1},{3,4},{4,3},{5,6},{6,5},{7,8},{8,7},{9,10},{10,9},{11,... | collective-permute-start | bytes 3145736 | tf_op jit(solution)/shard_map/ppermute | solution.py:266
  33.2 3.2 %project.7.kr_ref.vr_ref = bf16[512,512]{1,0:T(8,128)(2,1)} custom-call(bf16[512,1024]{1,0:T(8,128)(2,1)} %collective-permute-done.refs_0_, bf16[1,1024]{1,0:T(2,128)(2,1)} %reshape.7.refs_2_.refs_1_, bf16[1024,3072]{1,0:T(8,128)(2,1)} %refs_2_.5), custom_call_target="tpu_custom_call" | custom-call | flops 1 | bytes 1 | tf_op jit(solution)/shard_map/project/pallas_call | solution.py:100
  36.4 6.3 %attention.3 = bf16[512,256]{1,0:T(8,128)(2,1)} custom-call(s32[2]{0:T(128)} %pad_add_fusion.flags_ref, bf16[512,1024]{1,0:T(8,128)(2,1)} %get-tuple-element.33.q_ref, bf16[1024,2048]{1,0:T(8,128)(2,1)} %get-tuple-element.38.ko_ref.ks_ref.vo_ref.vs_ref, bf16[1024,2048]{1,0:T(8,128)(2,1)} %get-tuple-element.38.ko_ref.ks_ref.vo_ref.vs_ref, ...), custom_call_target="tpu_custom_call" | custom-call | flops 1342177280 | bytes 524288 | tf_op jit(solution)/shard_map/attention/pallas_call | solution.py:202
  42.7 6.5 %collective-permute-start.3 = (bf16[512,256]{1,0:T(8,128)(2,1)}, bf16[512,256]{1,0:T(8,128)(2,1)}, u32[]{:S(2)}, u32[]{:S(2)}) collective-permute-start(bf16[512,256]{1,0:T(8,128)(2,1)} %attention.3), channel_id=1, source_target_pairs={{0,31},{1,30},{2,29},{3,28},{4,27},{5,26},{6,25},{7,24},{8,23},{9,... | collective-permute-start | bytes 786440 | tf_op jit(solution)/shard_map/ppermute | solution.py:266
  49.2 5.7 %project.8.kr_ref.vr_ref = bf16[512,2048]{1,0:T(8,128)(2,1)} custom-call(bf16[512,1024]{1,0:T(8,128)(2,1)} %collective-permute-done.refs_0_, bf16[1,1024]{1,0:T(2,128)(2,1)} %reshape.7.refs_2_.refs_1_, bf16[1024,3072]{1,0:T(8,128)(2,1)} %refs_2_.5), custom_call_target="tpu_custom_call" | custom-call | flops 1 | bytes 1 | tf_op jit(solution)/shard_map/project/pallas_call | solution.py:100
  54.9 8.5 %attention.4 = bf16[512,384]{1,0:T(8,128)(2,1)} custom-call(s32[2]{0:T(128)} %pad_add_fusion.flags_ref, bf16[512,1024]{1,0:T(8,128)(2,1)} %get-tuple-element.33.q_ref, bf16[1024,2048]{1,0:T(8,128)(2,1)} %get-tuple-element.38.ko_ref.ks_ref.vo_ref.vs_ref, bf16[1024,2048]{1,0:T(8,128)(2,1)} %get-tuple-element.38.ko_ref.ks_ref.vo_ref.vs_ref, ...), custom_call_target="tpu_custom_call" | custom-call | flops 2013265920 | bytes 786432 | tf_op jit(solution)/shard_map/attention/pallas_call | solution.py:202
  63.5 8.5 %attention.5 = bf16[512,384]{1,0:T(8,128)(2,1)} custom-call(s32[2]{0:T(128)} %pad_add_fusion.flags_ref, bf16[512,1024]{1,0:T(8,128)(2,1)} %get-tuple-element.33.q_ref, bf16[1024,2048]{1,0:T(8,128)(2,1)} %get-tuple-element.38.ko_ref.ks_ref.vo_ref.vs_ref, bf16[1024,2048]{1,0:T(8,128)(2,1)} %get-tuple-element.38.ko_ref.ks_ref.vo_ref.vs_ref, ...), custom_call_target="tpu_custom_call" | custom-call | flops 2013265920 | bytes 786432 | tf_op jit(solution)/shard_map/attention/pallas_call | solution.py:202
  72.0 5.3 %collective-permute-start.5 = (bf16[512,384]{1,0:T(8,128)(2,1)}, bf16[512,384]{1,0:T(8,128)(2,1)}, u32[]{:S(2)}, u32[]{:S(2)}) collective-permute-start(bf16[512,384]{1,0:T(8,128)(2,1)} %attention.5), channel_id=1, source_target_pairs={{0,31},{1,30},{2,29},{3,28},{4,27},{5,26},{6,25},{7,24},{8,23},{9,... | collective-permute-start | bytes 1179656 | tf_op jit(solution)/shard_map/ppermute | solution.py:266
  77.3 5.9 %project.9.kr_ref.vr_ref = bf16[512,2048]{1,0:T(8,128)(2,1)} custom-call(bf16[512,1024]{1,0:T(8,128)(2,1)} %collective-permute-done.4.refs_0_, bf16[1,1024]{1,0:T(2,128)(2,1)} %reshape.7.refs_2_.refs_1_, bf16[1024,3072]{1,0:T(8,128)(2,1)} %refs_2_.5), custom_call_target="tpu_custom_call" | custom-call | flops 1 | bytes 1 | tf_op jit(solution)/shard_map/project/pallas_call | solution.py:100
  83.2 12.8 %collective-permute-done.6.refs_0_ = bf16[512,384]{1,0:T(8,128)(2,1)} collective-permute-done((bf16[512,384]{1,0:T(8,128)(2,1)}, bf16[512,384]{1,0:T(8,128)(2,1)}, u32[]{:S(2)}, u32[]{:S(2)}) %collective-permute-start.6) | collective-permute-done | bytes 393248 | tf_op jit(solution)/shard_map/ppermute | solution.py:266
  96.0 6.4 %attention_mirrored.3.piece_ref = bf16[512,256]{1,0:T(8,128)(2,1)} custom-call(s32[2]{0:T(128)} %pad_add_fusion.flags_ref, bf16[512,1024]{1,0:T(8,128)(2,1)} %get-tuple-element.35.q_ref, bf16[1024,2048]{1,0:T(8,128)(2,1)} %get-tuple-element.46.ko_ref.ks_ref.vo_ref.vs_ref, bf16[1024,2048]{1,0:T(8,128)(2,1)} %get-tuple-element.46.ko_ref.ks_ref.vo_ref.vs_ref, ...), custom_call_target="tpu_custom_call" | custom-call | flops 1342177280 | bytes 524288 | tf_op jit(solution)/shard_map/attention_mirrored/pallas_call | solution.py:202
  102.4 16.0 %collective-permute-done.5.refs_0_ = bf16[512,384]{1,0:T(8,128)(2,1)} collective-permute-done((bf16[512,384]{1,0:T(8,128)(2,1)}, bf16[512,384]{1,0:T(8,128)(2,1)}, u32[]{:S(2)}, u32[]{:S(2)}) %collective-permute-start.5) | collective-permute-done | bytes 393248 | tf_op jit(solution)/shard_map/ppermute | solution.py:266
  118.5 8.7 %attention_mirrored.4.piece_ref = bf16[512,384]{1,0:T(8,128)(2,1)} custom-call(s32[2]{0:T(128)} %pad_add_fusion.flags_ref, bf16[512,1024]{1,0:T(8,128)(2,1)} %get-tuple-element.35.q_ref, bf16[1024,2048]{1,0:T(8,128)(2,1)} %get-tuple-element.46.ko_ref.ks_ref.vo_ref.vs_ref, bf16[1024,2048]{1,0:T(8,128)(2,1)} %get-tuple-element.46.ko_ref.ks_ref.vo_ref.vs_ref, ...), custom_call_target="tpu_custom_call" | custom-call | flops 2013265920 | bytes 786432 | tf_op jit(solution)/shard_map/attention_mirrored/pallas_call | solution.py:202
  127.2 2.3 %place.6.refs_0_ = bf16[512,1024]{1,0:T(8,128)(2,1)} custom-call(bf16[512,256]{1,0:T(8,128)(2,1)} %attention_mirrored.3.piece_ref), custom_call_target="tpu_custom_call" | custom-call | flops 1 | bytes 1 | tf_op jit(solution)/shard_map/place/pallas_call | solution.py:239
  129.5 1.6 %place.7.refs_0_ = bf16[512,1024]{1,0:T(8,128)(2,1)} custom-call(bf16[512,256]{1,0:T(8,128)(2,1)} %collective-permute-done.7.piece_ref), custom_call_target="tpu_custom_call" | custom-call | flops 1 | bytes 1 | tf_op jit(solution)/shard_map/place/pallas_call | solution.py:239
  131.1 8.7 %attention_mirrored.5.piece_ref = bf16[512,384]{1,0:T(8,128)(2,1)} custom-call(s32[2]{0:T(128)} %pad_add_fusion.flags_ref, bf16[512,1024]{1,0:T(8,128)(2,1)} %get-tuple-element.35.q_ref, bf16[1024,2048]{1,0:T(8,128)(2,1)} %get-tuple-element.46.ko_ref.ks_ref.vo_ref.vs_ref, bf16[1024,2048]{1,0:T(8,128)(2,1)} %get-tuple-element.46.ko_ref.ks_ref.vo_ref.vs_ref, ...), custom_call_target="tpu_custom_call" | custom-call | flops 2013265920 | bytes 786432 | tf_op jit(solution)/shard_map/attention_mirrored/pallas_call | solution.py:202
  139.8 5.3 %collective-permute-start.8 = (bf16[512,384]{1,0:T(8,128)(2,1)}, bf16[512,384]{1,0:T(8,128)(2,1)}, u32[]{:S(2)}, u32[]{:S(2)}) collective-permute-start(bf16[512,384]{1,0:T(8,128)(2,1)} %attention_mirrored.5.piece_ref), channel_id=1, source_target_pairs={{0,31},{1,30},{2,29},{3,28},{4,27},{5,26},{6,25},{7,24},{8,23},{9,... | collective-permute-start | bytes 1179656 | tf_op jit(solution)/shard_map/ppermute | solution.py:266
  145.2 3.3 %place.8.refs_0_ = bf16[512,1024]{1,0:T(8,128)(2,1)} custom-call(bf16[512,384]{1,0:T(8,128)(2,1)} %attention_mirrored.4.piece_ref, bf16[512,1024]{1,0:T(8,128)(2,1)} %place.6.refs_0_), custom_call_target="tpu_custom_call", output_to_operand_aliasing={{}: (1, {})} | custom-call | flops 1 | bytes 1 | tf_op jit(solution)/shard_map/place/pallas_call | solution.py:239
  148.5 3.3 %place.9 = bf16[512,1024]{1,0:T(8,128)(2,1)} custom-call(bf16[512,384]{1,0:T(8,128)(2,1)} %attention_mirrored.5.piece_ref, bf16[512,1024]{1,0:T(8,128)(2,1)} %place.8.refs_0_), custom_call_target="tpu_custom_call", output_to_operand_aliasing={{}: (1, {})} | custom-call | flops 1 | bytes 1 | tf_op jit(solution)/shard_map/place/pallas_call | solution.py:239
  151.7 2.6 %place.10.refs_0_ = bf16[512,1024]{1,0:T(8,128)(2,1)} custom-call(bf16[512,384]{1,0:T(8,128)(2,1)} %collective-permute-done.9.piece_ref, bf16[512,1024]{1,0:T(8,128)(2,1)} %place.7.refs_0_), custom_call_target="tpu_custom_call", output_to_operand_aliasing={{}: (1, {})} | custom-call | flops 1 | bytes 1 | tf_op jit(solution)/shard_map/place/pallas_call | solution.py:239
  154.3 2.6 %place.11 = bf16[512,1024]{1,0:T(8,128)(2,1)} custom-call(bf16[512,384]{1,0:T(8,128)(2,1)} %collective-permute-done.8.piece_ref, bf16[512,1024]{1,0:T(8,128)(2,1)} %place.10.refs_0_), custom_call_target="tpu_custom_call", output_to_operand_aliasing={{}: (1, {})} | custom-call | flops 1 | bytes 1 | tf_op jit(solution)/shard_map/place/pallas_call | solution.py:239
  (15 shorter events, 2.8 us)
Async XLA Ops:
  0.6 6.7 %collective-permute-start.1 = (bf16[512,1024]{1,0:T(8,128)(2,1)}, bf16[512,1024]{1,0:T(8,128)(2,1)}, u32[]{:S(2)}, u32[]{:S(2)}) collective-permute-start(bf16[512,1024]{1,0:T(8,128)(2,1)} %refs_0_.1), channel_id=1, source_target_pairs={{0,1},{1,0},{2,3},{3,2},{4,5},{5,4},{6,7},{7,6},{8,9},{9,8},{10,11... | collective-permute-start | bytes 3145736 | tf_op jit(solution)/shard_map/ppermute | solution.py:266
  1.4 16.3 %collective-permute-start.2 = (bf16[512,1024]{1,0:T(8,128)(2,1)}, bf16[512,1024]{1,0:T(8,128)(2,1)}, u32[]{:S(2)}, u32[]{:S(2)}) collective-permute-start(bf16[512,1024]{1,0:T(8,128)(2,1)} %refs_0_.2), channel_id=1, source_target_pairs={{0,1},{1,0},{2,3},{3,2},{4,5},{5,4},{6,7},{7,6},{8,9},{9,8},{10,11... | collective-permute-start | bytes 3145736 | tf_op jit(solution)/shard_map/ppermute | solution.py:266
  1.5 31.7 %collective-permute-start = (bf16[512,1024]{1,0:T(8,128)(2,1)}, bf16[512,1024]{1,0:T(8,128)(2,1)}, u32[]{:S(2)}, u32[]{:S(2)}) collective-permute-start(bf16[512,1024]{1,0:T(8,128)(2,1)} %refs_0_.1), channel_id=1, source_target_pairs={{1,2},{2,1},{3,4},{4,3},{5,6},{6,5},{7,8},{8,7},{9,10},{10,9},{11,... | collective-permute-start | bytes 3145736 | tf_op jit(solution)/shard_map/ppermute | solution.py:266
  28.9 34.6 %collective-permute-start.4 = (bf16[512,1024]{1,0:T(8,128)(2,1)}, bf16[512,1024]{1,0:T(8,128)(2,1)}, u32[]{:S(2)}, u32[]{:S(2)}) collective-permute-start(bf16[512,1024]{1,0:T(8,128)(2,1)} %refs_0_.2), channel_id=1, source_target_pairs={{1,2},{2,1},{3,4},{4,3},{5,6},{6,5},{7,8},{8,7},{9,10},{10,9},{11,... | collective-permute-start | bytes 3145736 | tf_op jit(solution)/shard_map/ppermute | solution.py:266
  42.7 20.8 %collective-permute-start.3 = (bf16[512,256]{1,0:T(8,128)(2,1)}, bf16[512,256]{1,0:T(8,128)(2,1)}, u32[]{:S(2)}, u32[]{:S(2)}) collective-permute-start(bf16[512,256]{1,0:T(8,128)(2,1)} %attention.3), channel_id=1, source_target_pairs={{0,31},{1,30},{2,29},{3,28},{4,27},{5,26},{6,25},{7,24},{8,23},{9,... | collective-permute-start | bytes 786440 | tf_op jit(solution)/shard_map/ppermute | solution.py:266
  63.4 32.6 %collective-permute-start.6 = (bf16[512,384]{1,0:T(8,128)(2,1)}, bf16[512,384]{1,0:T(8,128)(2,1)}, u32[]{:S(2)}, u32[]{:S(2)}) collective-permute-start(bf16[512,384]{1,0:T(8,128)(2,1)} %attention.4), channel_id=1, source_target_pairs={{0,31},{1,30},{2,29},{3,28},{4,27},{5,26},{6,25},{7,24},{8,23},{9,... | collective-permute-start | bytes 1179656 | tf_op jit(solution)/shard_map/ppermute | solution.py:266
  72.0 46.5 %collective-permute-start.5 = (bf16[512,384]{1,0:T(8,128)(2,1)}, bf16[512,384]{1,0:T(8,128)(2,1)}, u32[]{:S(2)}, u32[]{:S(2)}) collective-permute-start(bf16[512,384]{1,0:T(8,128)(2,1)} %attention.5), channel_id=1, source_target_pairs={{0,31},{1,30},{2,29},{3,28},{4,27},{5,26},{6,25},{7,24},{8,23},{9,... | collective-permute-start | bytes 1179656 | tf_op jit(solution)/shard_map/ppermute | solution.py:266
  102.4 27.1 %collective-permute-start.7 = (bf16[512,256]{1,0:T(8,128)(2,1)}, bf16[512,256]{1,0:T(8,128)(2,1)}, u32[]{:S(2)}, u32[]{:S(2)}) collective-permute-start(bf16[512,256]{1,0:T(8,128)(2,1)} %attention_mirrored.3.piece_ref), channel_id=1, source_target_pairs={{0,31},{1,30},{2,29},{3,28},{4,27},{5,26},{6,25},{7,24},{8,23},{9,... | collective-permute-start | bytes 786440 | tf_op jit(solution)/shard_map/ppermute | solution.py:266
  127.2 24.6 %collective-permute-start.9 = (bf16[512,384]{1,0:T(8,128)(2,1)}, bf16[512,384]{1,0:T(8,128)(2,1)}, u32[]{:S(2)}, u32[]{:S(2)}) collective-permute-start(bf16[512,384]{1,0:T(8,128)(2,1)} %attention_mirrored.4.piece_ref), channel_id=1, source_target_pairs={{0,31},{1,30},{2,29},{3,28},{4,27},{5,26},{6,25},{7,24},{8,23},{9,... | collective-permute-start | bytes 1179656 | tf_op jit(solution)/shard_map/ppermute | solution.py:266
  139.8 14.5 %collective-permute-start.8 = (bf16[512,384]{1,0:T(8,128)(2,1)}, bf16[512,384]{1,0:T(8,128)(2,1)}, u32[]{:S(2)}, u32[]{:S(2)}) collective-permute-start(bf16[512,384]{1,0:T(8,128)(2,1)} %attention_mirrored.5.piece_ref), channel_id=1, source_target_pairs={{0,31},{1,30},{2,29},{3,28},{4,27},{5,26},{6,25},{7,24},{8,23},{9,... | collective-permute-start | bytes 1179656 | tf_op jit(solution)/shard_map/ppermute | solution.py:266

commit v3 on v2

--- a/solution.py
+++ b/solution.py
@@ -58,7 +58,7 @@
         for m in range(n):
             xf = x_refs[m][...].astype(jnp.float32)
             meansq = jnp.mean(xf * xf, axis=-1, keepdims=True)
-            hn = xf * lax.rsqrt(meansq + 1e-6) * gain_ref[...].astype(jnp.float32)
+            hn = xf * lax.rsqrt(meansq + 1e-6) * gain_ref[...].astype(jnp.float32)[None, :]
             hn_ref[m * rows : (m + 1) * rows] = hn.astype(jnp.bfloat16)
 
     def product(h):
@@ -88,13 +88,12 @@
             kv_ref[...] = v
 
 
-def project(xs, gain, w, scale, mirrored, with_q, part=0, parts=1):
+def project(xs, gain, w, scale, mirrored, with_q):
     rows, width = xs[0].shape
     n = len(xs)
-    block = width // parts
     first = 1 if with_q else 0
-    kv = jax.ShapeDtypeStruct((n * rows, 2 * block), jnp.bfloat16)
-    kv_spec = pl.BlockSpec((n * rows, block), lambda j: (0, jnp.maximum(j - first, 0)))
+    kv = jax.ShapeDtypeStruct((n * rows, 2 * width), jnp.bfloat16)
+    kv_spec = pl.BlockSpec((n * rows, width), lambda j: (0, jnp.maximum(j - first, 0)))
     q = jax.ShapeDtypeStruct((rows, width), jnp.bfloat16)
     q_spec = pl.BlockSpec((rows, width), lambda j: (0, 0))
     return pl.pallas_call(
@@ -103,8 +102,8 @@
         grid=(2 + first,),
         in_specs=[pl.BlockSpec((rows, width), lambda j: (0, 0))] * n
         + [
-            pl.BlockSpec((1, width), lambda j: (0, 0)),
-            pl.BlockSpec((width, block), lambda j: (0, parts * (j + 1 - first) + part)),
+            pl.BlockSpec((width,), lambda j: (0,)),
+            pl.BlockSpec((width, width), lambda j: (0, j + 1 - first)),
         ],
         out_specs=(q_spec, kv_spec) if with_q else kv_spec,
         scratch_shapes=[
@@ -195,16 +194,13 @@
         return pl.BlockSpec((rows, pw), lambda g: (row, n + f + g))
 
     there = sibling.shape[0] // rows - 1
-    held = remote.shape[1] // (2 * pw)
-    remote_keys = pl.BlockSpec((rows, pw), lambda g: (0, key(g)))
-    remote_values = pl.BlockSpec((rows, pw), lambda g: (0, held + f + g))
     out_spec = pl.BlockSpec((rows, pw), lambda g: (0, g))
     return pl.pallas_call(
         functools.partial(attention_kernel, min(256, rows), mirrored),
         out_shape=jax.ShapeDtypeStruct((rows, count * pw), jnp.bfloat16),
         grid=(count,),
         in_specs=[pl.BlockSpec(memory_space=pltpu.SMEM)]
-        + [keys(0), keys(0), keys(there), remote_keys, values(0), values(there), remote_values]
+        + [keys(0), keys(0), keys(there), keys(0), values(0), values(there), values(0)]
         + [out_spec] * mirrored,
         out_specs=out_spec,
         scratch_shapes=[
@@ -221,28 +217,48 @@
     )(flags, q, own, sibling, remote, own, sibling, remote, *([near] if mirrored else []))
 
 
-def place_kernel(turned, piece_ref, *refs):
-    out_ref = refs[-1]
-    if turned:
-        t = jnp.dot(piece_ref[...], exchange_matrix(piece_ref.shape[1]), preferred_element_type=jnp.float32)
-        rows_reversed(t.astype(jnp.bfloat16), out_ref)
-    else:
-        out_ref[...] = piece_ref[...]
-
-
-def place(piece, first, width, held, turned):
+def turn_kernel(piece_ref, *refs):
+    t = jnp.dot(piece_ref[...], exchange_matrix(piece_ref.shape[1]), preferred_element_type=jnp.float32)
+    rows_reversed(t.astype(jnp.bfloat16), refs[-1])
+
+
+def turn(piece, first, width, held):
     rows, columns = piece.shape
     pw = 2 * (width // HEADS)
     n = width // pw
     f = first
     held = [] if held is None else [held]
     return pl.pallas_call(
-        functools.partial(place_kernel, turned),
+        turn_kernel,
         out_shape=jax.ShapeDtypeStruct((rows, width), jnp.bfloat16),
         grid=(columns // pw,),
         in_specs=[pl.BlockSpec((rows, pw), lambda g: (0, g))]
         + [pl.BlockSpec(memory_space=pl.ANY)] * len(held),
-        out_specs=pl.BlockSpec((rows, pw), lambda g: (0, n - 1 - f - g if turned else f + g)),
+        out_specs=pl.BlockSpec((rows, pw), lambda g: (0, n - 1 - f - g)),
+        input_output_aliases={1: 0} if held else {},
+        compiler_params=pltpu.CompilerParams(vmem_limit_bytes=VMEM_LIMIT),
+        cost_estimate=SMALL,
+        name="turn",
+    )(piece, *held)
+
+
+def place_kernel(first, piece_ref, *refs):
+    out_ref, sem = refs[-2:]
+    copy = pltpu.make_async_copy(piece_ref, out_ref.at[:, pl.ds(first, piece_ref.shape[1])], sem)
+    copy.start()
+    copy.wait()
+
+
+def place(piece, first, width, held):
+    rows = piece.shape[0]
+    held = [] if held is None else [held]
+    anywhere = pl.BlockSpec(memory_space=pl.ANY)
+    return pl.pallas_call(
+        functools.partial(place_kernel, first * 2 * (width // HEADS)),
+        out_shape=jax.ShapeDtypeStruct((rows, width), jnp.bfloat16),
+        in_specs=[anywhere] * (1 + len(held)),
+        out_specs=anywhere,
+        scratch_shapes=[pltpu.SemaphoreType.DMA(())],
         input_output_aliases={1: 0} if held else {},
         compiler_params=pltpu.CompilerParams(vmem_limit_bytes=VMEM_LIMIT),
         cost_estimate=SMALL,
@@ -255,12 +271,10 @@
     index = lax.axis_index("seq")
     rows, width = x_fwd.shape
     scale = (width // HEADS) ** (-0.5) * LOG2E
-    gain = gain.reshape(1, width)
     sibling = [(i, i ^ 1) for i in range(count)]
     beside = [(i, i - 1 if i % 2 == 0 else i + 1) for i in range(1, count - 1)]
     mirror = [(i, count - 1 - i) for i in range(count)]
     firsts = [sum(CHUNKS[:k]) for k in range(len(CHUNKS))]
-    parts = HEADS // 2 // CHUNKS[0]
 
     def send(x, pairs):
         return lax.ppermute(x, "seq", pairs)
@@ -270,21 +284,19 @@
     f_x = send(x_fwd, beside)
     f_y = send(x_fwd, sibling)
     s_y = send(x_rev, sibling)
-    f_q, f_chip = project([x_fwd, f_y], gain, w_qkv, scale, False, True)
+    f_q, f_chip = project([after(x_fwd, flags), f_y], gain, w_qkv, scale, False, True)
     s_q, s_chip = project([after(x_rev, f_q), s_y], gain, w_qkv, scale, True, True)
     s_x = send(after(x_rev, s_q), beside)
 
     a_moved = []
     f_x = after(f_x, s_q)
-    f_rem = project([f_x], gain, w_qkv, scale, False, False, 0, parts)
+    f_rem = project([f_x], gain, w_qkv, scale, False, False)
     flags = after(flags, f_rem)
     for k in range(len(CHUNKS)):
         if k == 2:
             a_moved[0], s_x, flags = lax.optimization_barrier((a_moved[0], s_x, flags))
         a = attention(f_q, f_chip, f_chip, f_rem, flags, firsts[k], CHUNKS[k])
         flags = after(flags, a)
-        if k == 0:
-            f_rem = project([after(f_x, a)], gain, w_qkv, scale, False, False)
         a_moved.append(send(a, mirror))
     s_rem = project([after(s_x, a)], gain, w_qkv, scale, True, False)
 
@@ -294,17 +306,17 @@
         ahead = min(k + 1, last)
         a_moved[ahead], flags = lax.optimization_barrier((a_moved[ahead], flags))
         if k >= 2:
-            rev = place(after(mine[k - 2], mine[k - 1]), firsts[k - 2], width, rev, True)
-            fwd = place(after(moved[k - 2], rev), firsts[k - 2], width, fwd, False)
+            rev = turn(after(mine[k - 2], mine[k - 1]), firsts[k - 2], width, rev)
+            fwd = place(after(moved[k - 2], rev), firsts[k - 2], width, fwd)
             flags = after(flags, fwd)
         y = attention(s_q, s_chip, s_chip, s_rem, flags, firsts[k], CHUNKS[k], a_moved[k])
         flags = after(flags, y)
         mine.append(y)
         moved.append(send(y, mirror))
     for k in (last - 1, last):
-        rev = place(after(mine[k], mine[-1]), firsts[k], width, rev, True)
+        rev = turn(after(mine[k], mine[-1]), firsts[k], width, rev)
     for k in (last - 1, last):
-        fwd = place(after(moved[k], rev), firsts[k], width, fwd, False)
+        fwd = place(after(moved[k], rev), firsts[k], width, fwd)
     return fwd, rev
 
 

time: 157 us -> 172 us (1.096); the launches traced: 157 us -> 170 us
  Pallas kernels: 99.3 us -> 124 us
  waiting for transfers between devices: 28.8 us -> 16.8 us
    pallas_call x6, Pallas kernels: 15.7 us -> 44 us  [the longest x3 35.1 us: place(): pl.pallas_call(functools.partial(place_kernel, first * 2 * (width // HEAD...]
    ppermute x10, waiting for transfers between devices: 28.8 us -> 16.8 us  [send(): return lax.ppermute(x, 'seq', pairs)]
    pallas_call x5 -> x4, Pallas kernels: 36.4 us -> 33.2 us  [project(): pl.pallas_call(functools.partial(project_kernel, scale, mirrored, with_q,...]
  transfers between devices with their start and end apart: 10 -> 10, of which waited for: 2 -> 2; matrix products, arithmetic and copies ran while one was open for 1% -> 0% of each run, Pallas kernels for 62% -> 66%
where the time goes in v3:
time: 172 us; the launch traced here: 170 us
  Pallas kernels  124 us (72%)
  starting transfers between devices  27.2 us (16%)
  waiting for transfers between devices  16.8 us (10%)
    pallas_call x6, Pallas kernels, attention(): pl.pallas_call(functools.partial(attention_kernel, min(256, rows), mirror...  47.2 us
    pallas_call x3, Pallas kernels, place(): pl.pallas_call(functools.partial(place_kernel, first * 2 * (width // HEAD...  35.1 us
    pallas_call x4, Pallas kernels, project(): pl.pallas_call(functools.partial(project_kernel, scale, mirrored, with_q,...  33.2 us
    ppermute x10, starting transfers between devices, send(): return lax.ppermute(x, 'seq', pairs)  27.2 us
    ppermute x10, waiting for transfers between devices, send(): return lax.ppermute(x, 'seq', pairs)  16.8 us
    pallas_call x3, Pallas kernels, turn(): pl.pallas_call(turn_kernel, out_shape=jax.ShapeDtypeStruct((rows, width),...  8.88 us
  transfers between devices with their start and end apart: 10, of which 2 were waited for; matrix products, arithmetic and copies ran while one was open for 0% of the time, Pallas kernels for 66%

profile of v3, /device:TPU:25, one launch (start us, length us, event | category | flops | bytes accessed | tf_op | source)
XLA Modules:
  0.0 169.9 jit_solution(13183836936215014535)
XLA Ops:
  1.5 4.5 %collective-permute-start = (bf16[512,1024]{1,0:T(8,128)(2,1)}, bf16[512,1024]{1,0:T(8,128)(2,1)}, u32[]{:S(2)}, u32[]{:S(2)}) collective-permute-start(bf16[512,1024]{1,0:T(8,128)(2,1)} %refs_0_), channel_id=1, source_target_pairs={{1,2},{2,1},{3,4},{4,3},{5,6},{6,5},{7,8},{8,7},{9,10},{10,9},{11,... | collective-permute-start | bytes 3145736 | tf_op jit(solution)/shard_map/ppermute | solution.py:280
  6.6 10.4 %project.4 = (bf16[512,1024]{1,0:T(8,128)(2,1)}, bf16[1024,2048]{1,0:T(8,128)(2,1)}) custom-call(bf16[512,1024]{1,0:T(8,128)(2,1)} %refs_0_, bf16[512,1024]{1,0:T(8,128)(2,1)} %collective-permute-done.1.refs_1_, bf16[1024]{0:T(1024)(128)(2,1)} %refs_1_.3, bf16[1024,3072]{1,0:T(8,128)(2,1)} %refs_2_.7), custom_call_target="tpu_custom_call" | custom-call | flops 1 | bytes 1 | tf_op jit(solution)/shard_map/project/pallas_call | solution.py:99
  17.0 11.2 %project.5 = (bf16[512,1024]{1,0:T(8,128)(2,1)}, bf16[1024,2048]{1,0:T(8,128)(2,1)}) custom-call(bf16[512,1024]{1,0:T(8,128)(2,1)} %refs_0_.1, bf16[512,1024]{1,0:T(8,128)(2,1)} %collective-permute-done.2.refs_1_, bf16[1024]{0:T(1024)(128)(2,1)} %refs_1_.3, bf16[1024,3072]{1,0:T(8,128)(2,1)} %refs_2_.7), custom_call_target="tpu_custom_call" | custom-call | flops 1 | bytes 1 | tf_op jit(solution)/shard_map/project/pallas_call | solution.py:99
  28.2 3.6 %collective-permute-start.4 = (bf16[512,1024]{1,0:T(8,128)(2,1)}, bf16[512,1024]{1,0:T(8,128)(2,1)}, u32[]{:S(2)}, u32[]{:S(2)}) collective-permute-start(bf16[512,1024]{1,0:T(8,128)(2,1)} %refs_0_.1), channel_id=1, source_target_pairs={{1,2},{2,1},{3,4},{4,3},{5,6},{6,5},{7,8},{8,7},{9,10},{10,9},{11,... | collective-permute-start | bytes 3145736 | tf_op jit(solution)/shard_map/ppermute | solution.py:280
  31.9 5.7 %project.6.kr_ref.vr_ref = bf16[512,2048]{1,0:T(8,128)(2,1)} custom-call(bf16[512,1024]{1,0:T(8,128)(2,1)} %collective-permute-done.refs_0_, bf16[1024]{0:T(1024)(128)(2,1)} %refs_1_.3, bf16[1024,3072]{1,0:T(8,128)(2,1)} %refs_2_.7), custom_call_target="tpu_custom_call" | custom-call | flops 1 | bytes 1 | tf_op jit(solution)/shard_map/project/pallas_call | solution.py:99
  37.6 6.3 %attention.3 = bf16[512,256]{1,0:T(8,128)(2,1)} custom-call(s32[2]{0:T(128)} %pad_add_fusion.flags_ref, bf16[512,1024]{1,0:T(8,128)(2,1)} %get-tuple-element.34.q_ref, bf16[1024,2048]{1,0:T(8,128)(2,1)} %get-tuple-element.39.ko_ref.ks_ref.vo_ref.vs_ref, bf16[1024,2048]{1,0:T(8,128)(2,1)} %get-tuple-element.39.ko_ref.ks_ref.vo_ref.vs_ref, ...), custom_call_target="tpu_custom_call" | custom-call | flops 1342177280 | bytes 524288 | tf_op jit(solution)/shard_map/attention/pallas_call | solution.py:198
  43.9 6.5 %collective-permute-start.3 = (bf16[512,256]{1,0:T(8,128)(2,1)}, bf16[512,256]{1,0:T(8,128)(2,1)}, u32[]{:S(2)}, u32[]{:S(2)}) collective-permute-start(bf16[512,256]{1,0:T(8,128)(2,1)} %attention.3), channel_id=1, source_target_pairs={{0,31},{1,30},{2,29},{3,28},{4,27},{5,26},{6,25},{7,24},{8,23},{9,... | collective-permute-start | bytes 786440 | tf_op jit(solution)/shard_map/ppermute | solution.py:280
  50.4 8.5 %attention.4 = bf16[512,384]{1,0:T(8,128)(2,1)} custom-call(s32[2]{0:T(128)} %pad_add_fusion.flags_ref, bf16[512,1024]{1,0:T(8,128)(2,1)} %get-tuple-element.34.q_ref, bf16[1024,2048]{1,0:T(8,128)(2,1)} %get-tuple-element.39.ko_ref.ks_ref.vo_ref.vs_ref, bf16[1024,2048]{1,0:T(8,128)(2,1)} %get-tuple-element.39.ko_ref.ks_ref.vo_ref.vs_ref, ...), custom_call_target="tpu_custom_call" | custom-call | flops 2013265920 | bytes 786432 | tf_op jit(solution)/shard_map/attention/pallas_call | solution.py:198
  59.0 11.8 %collective-permute-done.3.refs_0_ = bf16[512,256]{1,0:T(8,128)(2,1)} collective-permute-done((bf16[512,256]{1,0:T(8,128)(2,1)}, bf16[512,256]{1,0:T(8,128)(2,1)}, u32[]{:S(2)}, u32[]{:S(2)}) %collective-permute-start.3) | collective-permute-done | bytes 262176 | tf_op jit(solution)/shard_map/ppermute | solution.py:280
  70.7 8.5 %attention.5 = bf16[512,384]{1,0:T(8,128)(2,1)} custom-call(s32[2]{0:T(128)} %pad_add_fusion.flags_ref, bf16[512,1024]{1,0:T(8,128)(2,1)} %get-tuple-element.34.q_ref, bf16[1024,2048]{1,0:T(8,128)(2,1)} %get-tuple-element.39.ko_ref.ks_ref.vo_ref.vs_ref, bf16[1024,2048]{1,0:T(8,128)(2,1)} %get-tuple-element.39.ko_ref.ks_ref.vo_ref.vs_ref, ...), custom_call_target="tpu_custom_call" | custom-call | flops 2013265920 | bytes 786432 | tf_op jit(solution)/shard_map/attention/pallas_call | solution.py:198
  79.3 6.2 %collective-permute-start.5 = (bf16[512,384]{1,0:T(8,128)(2,1)}, bf16[512,384]{1,0:T(8,128)(2,1)}, u32[]{:S(2)}, u32[]{:S(2)}) collective-permute-start(bf16[512,384]{1,0:T(8,128)(2,1)} %attention.5), channel_id=1, source_target_pairs={{0,31},{1,30},{2,29},{3,28},{4,27},{5,26},{6,25},{7,24},{8,23},{9,... | collective-permute-start | bytes 1179656 | tf_op jit(solution)/shard_map/ppermute | solution.py:280
  85.5 5.9 %project.7.kr_ref.vr_ref = bf16[512,2048]{1,0:T(8,128)(2,1)} custom-call(bf16[512,1024]{1,0:T(8,128)(2,1)} %collective-permute-done.4.refs_0_, bf16[1024]{0:T(1024)(128)(2,1)} %refs_1_.3, bf16[1024,3072]{1,0:T(8,128)(2,1)} %refs_2_.7), custom_call_target="tpu_custom_call" | custom-call | flops 1 | bytes 1 | tf_op jit(solution)/shard_map/project/pallas_call | solution.py:99
  91.4 6.4 %attention_mirrored.3.piece_ref = bf16[512,256]{1,0:T(8,128)(2,1)} custom-call(s32[2]{0:T(128)} %pad_add_fusion.flags_ref, bf16[512,1024]{1,0:T(8,128)(2,1)} %get-tuple-element.36.q_ref, bf16[1024,2048]{1,0:T(8,128)(2,1)} %get-tuple-element.46.ko_ref.ks_ref.vo_ref.vs_ref, bf16[1024,2048]{1,0:T(8,128)(2,1)} %get-tuple-element.46.ko_ref.ks_ref.vo_ref.vs_ref, ...), custom_call_target="tpu_custom_call" | custom-call | flops 1342177280 | bytes 524288 | tf_op jit(solution)/shard_map/attention_mirrored/pallas_call | solution.py:198
  97.8 5.0 %collective-permute-done.5.refs_0_ = bf16[512,384]{1,0:T(8,128)(2,1)} collective-permute-done((bf16[512,384]{1,0:T(8,128)(2,1)}, bf16[512,384]{1,0:T(8,128)(2,1)}, u32[]{:S(2)}, u32[]{:S(2)}) %collective-permute-start.5) | collective-permute-done | bytes 393248 | tf_op jit(solution)/shard_map/ppermute | solution.py:280
  102.9 8.7 %attention_mirrored.4.piece_ref = bf16[512,384]{1,0:T(8,128)(2,1)} custom-call(s32[2]{0:T(128)} %pad_add_fusion.flags_ref, bf16[512,1024]{1,0:T(8,128)(2,1)} %get-tuple-element.36.q_ref, bf16[1024,2048]{1,0:T(8,128)(2,1)} %get-tuple-element.46.ko_ref.ks_ref.vo_ref.vs_ref, bf16[1024,2048]{1,0:T(8,128)(2,1)} %get-tuple-element.46.ko_ref.ks_ref.vo_ref.vs_ref, ...), custom_call_target="tpu_custom_call" | custom-call | flops 2013265920 | bytes 786432 | tf_op jit(solution)/shard_map/attention_mirrored/pallas_call | solution.py:198
  111.5 4.0 %collective-permute-start.9 = (bf16[512,384]{1,0:T(8,128)(2,1)}, bf16[512,384]{1,0:T(8,128)(2,1)}, u32[]{:S(2)}, u32[]{:S(2)}) collective-permute-start(bf16[512,384]{1,0:T(8,128)(2,1)} %attention_mirrored.4.piece_ref), channel_id=1, source_target_pairs={{0,31},{1,30},{2,29},{3,28},{4,27},{5,26},{6,25},{7,24},{8,23},{9,... | collective-permute-start | bytes 1179656 | tf_op jit(solution)/shard_map/ppermute | solution.py:280
  115.5 2.3 %turn.3.refs_0_ = bf16[512,1024]{1,0:T(8,128)(2,1)} custom-call(bf16[512,256]{1,0:T(8,128)(2,1)} %attention_mirrored.3.piece_ref), custom_call_target="tpu_custom_call" | custom-call | flops 1 | bytes 1 | tf_op jit(solution)/shard_map/turn/pallas_call | solution.py:231
  117.8 9.0 %place.3.refs_0_ = bf16[512,1024]{1,0:T(8,128)(2,1)} custom-call(bf16[512,256]{1,0:T(8,128)(2,1)} %collective-permute-done.7.piece_ref), custom_call_target="tpu_custom_call" | custom-call | flops 1 | bytes 1 | tf_op jit(solution)/shard_map/place/pallas_call | solution.py:256
  126.9 8.8 %attention_mirrored.5.piece_ref = bf16[512,384]{1,0:T(8,128)(2,1)} custom-call(s32[2]{0:T(128)} %pad_add_fusion.flags_ref, bf16[512,1024]{1,0:T(8,128)(2,1)} %get-tuple-element.36.q_ref, bf16[1024,2048]{1,0:T(8,128)(2,1)} %get-tuple-element.46.ko_ref.ks_ref.vo_ref.vs_ref, bf16[1024,2048]{1,0:T(8,128)(2,1)} %get-tuple-element.46.ko_ref.ks_ref.vo_ref.vs_ref, ...), custom_call_target="tpu_custom_call" | custom-call | flops 2013265920 | bytes 786432 | tf_op jit(solution)/shard_map/attention_mirrored/pallas_call | solution.py:198
  135.6 1.4 collective-permute-start.8
  137.1 3.3 %turn.4.refs_0_ = bf16[512,1024]{1,0:T(8,128)(2,1)} custom-call(bf16[512,384]{1,0:T(8,128)(2,1)} %attention_mirrored.4.piece_ref, bf16[512,1024]{1,0:T(8,128)(2,1)} %turn.3.refs_0_), custom_call_target="tpu_custom_call", output_to_operand_aliasing={{}: (1, {})} | custom-call | flops 1 | bytes 1 | tf_op jit(solution)/shard_map/turn/pallas_call | solution.py:231
  140.3 3.3 %turn.5 = bf16[512,1024]{1,0:T(8,128)(2,1)} custom-call(bf16[512,384]{1,0:T(8,128)(2,1)} %attention_mirrored.5.piece_ref, bf16[512,1024]{1,0:T(8,128)(2,1)} %turn.4.refs_0_), custom_call_target="tpu_custom_call", output_to_operand_aliasing={{}: (1, {})} | custom-call | flops 1 | bytes 1 | tf_op jit(solution)/shard_map/turn/pallas_call | solution.py:231
  143.6 13.0 %place.4.refs_0_ = bf16[512,1024]{1,0:T(8,128)(2,1)} custom-call(bf16[512,384]{1,0:T(8,128)(2,1)} %collective-permute-done.9.piece_ref, bf16[512,1024]{1,0:T(8,128)(2,1)} %place.3.refs_0_), custom_call_target="tpu_custom_call", output_to_operand_aliasing={{}: (1, {})} | custom-call | flops 1 | bytes 1 | tf_op jit(solution)/shard_map/place/pallas_call | solution.py:256
  156.6 13.0 %place.5 = bf16[512,1024]{1,0:T(8,128)(2,1)} custom-call(bf16[512,384]{1,0:T(8,128)(2,1)} %collective-permute-done.8.piece_ref, bf16[512,1024]{1,0:T(8,128)(2,1)} %place.4.refs_0_), custom_call_target="tpu_custom_call", output_to_operand_aliasing={{}: (1, {})} | custom-call | flops 1 | bytes 1 | tf_op jit(solution)/shard_map/place/pallas_call | solution.py:256
  (13 shorter events, 1.5 us)
Async XLA Ops:
  0.6 6.0 %collective-permute-start.1 = (bf16[512,1024]{1,0:T(8,128)(2,1)}, bf16[512,1024]{1,0:T(8,128)(2,1)}, u32[]{:S(2)}, u32[]{:S(2)}) collective-permute-start(bf16[512,1024]{1,0:T(8,128)(2,1)} %refs_0_), channel_id=1, source_target_pairs={{0,1},{1,0},{2,3},{3,2},{4,5},{5,4},{6,7},{7,6},{8,9},{9,8},{10,11... | collective-permute-start | bytes 3145736 | tf_op jit(solution)/shard_map/ppermute | solution.py:280
  1.4 15.6 %collective-permute-start.2 = (bf16[512,1024]{1,0:T(8,128)(2,1)}, bf16[512,1024]{1,0:T(8,128)(2,1)}, u32[]{:S(2)}, u32[]{:S(2)}) collective-permute-start(bf16[512,1024]{1,0:T(8,128)(2,1)} %refs_0_.1), channel_id=1, source_target_pairs={{0,1},{1,0},{2,3},{3,2},{4,5},{5,4},{6,7},{7,6},{8,9},{9,8},{10,11... | collective-permute-start | bytes 3145736 | tf_op jit(solution)/shard_map/ppermute | solution.py:280
  1.5 30.4 %collective-permute-start = (bf16[512,1024]{1,0:T(8,128)(2,1)}, bf16[512,1024]{1,0:T(8,128)(2,1)}, u32[]{:S(2)}, u32[]{:S(2)}) collective-permute-start(bf16[512,1024]{1,0:T(8,128)(2,1)} %refs_0_), channel_id=1, source_target_pairs={{1,2},{2,1},{3,4},{4,3},{5,6},{6,5},{7,8},{8,7},{9,10},{10,9},{11,... | collective-permute-start | bytes 3145736 | tf_op jit(solution)/shard_map/ppermute | solution.py:280
  28.2 42.5 %collective-permute-start.4 = (bf16[512,1024]{1,0:T(8,128)(2,1)}, bf16[512,1024]{1,0:T(8,128)(2,1)}, u32[]{:S(2)}, u32[]{:S(2)}) collective-permute-start(bf16[512,1024]{1,0:T(8,128)(2,1)} %refs_0_.1), channel_id=1, source_target_pairs={{1,2},{2,1},{3,4},{4,3},{5,6},{6,5},{7,8},{8,7},{9,10},{10,9},{11,... | collective-permute-start | bytes 3145736 | tf_op jit(solution)/shard_map/ppermute | solution.py:280
  43.9 26.9 %collective-permute-start.3 = (bf16[512,256]{1,0:T(8,128)(2,1)}, bf16[512,256]{1,0:T(8,128)(2,1)}, u32[]{:S(2)}, u32[]{:S(2)}) collective-permute-start(bf16[512,256]{1,0:T(8,128)(2,1)} %attention.3), channel_id=1, source_target_pairs={{0,31},{1,30},{2,29},{3,28},{4,27},{5,26},{6,25},{7,24},{8,23},{9,... | collective-permute-start | bytes 786440 | tf_op jit(solution)/shard_map/ppermute | solution.py:280
  58.9 32.4 %collective-permute-start.6 = (bf16[512,384]{1,0:T(8,128)(2,1)}, bf16[512,384]{1,0:T(8,128)(2,1)}, u32[]{:S(2)}, u32[]{:S(2)}) collective-permute-start(bf16[512,384]{1,0:T(8,128)(2,1)} %attention.4), channel_id=1, source_target_pairs={{0,31},{1,30},{2,29},{3,28},{4,27},{5,26},{6,25},{7,24},{8,23},{9,... | collective-permute-start | bytes 1179656 | tf_op jit(solution)/shard_map/ppermute | solution.py:280
  79.3 23.6 %collective-permute-start.5 = (bf16[512,384]{1,0:T(8,128)(2,1)}, bf16[512,384]{1,0:T(8,128)(2,1)}, u32[]{:S(2)}, u32[]{:S(2)}) collective-permute-start(bf16[512,384]{1,0:T(8,128)(2,1)} %attention.5), channel_id=1, source_target_pairs={{0,31},{1,30},{2,29},{3,28},{4,27},{5,26},{6,25},{7,24},{8,23},{9,... | collective-permute-start | bytes 1179656 | tf_op jit(solution)/shard_map/ppermute | solution.py:280
  97.8 20.0 %collective-permute-start.7 = (bf16[512,256]{1,0:T(8,128)(2,1)}, bf16[512,256]{1,0:T(8,128)(2,1)}, u32[]{:S(2)}, u32[]{:S(2)}) collective-permute-start(bf16[512,256]{1,0:T(8,128)(2,1)} %attention_mirrored.3.piece_ref), channel_id=1, source_target_pairs={{0,31},{1,30},{2,29},{3,28},{4,27},{5,26},{6,25},{7,24},{8,23},{9,... | collective-permute-start | bytes 786440 | tf_op jit(solution)/shard_map/ppermute | solution.py:280
  111.5 32.1 %collective-permute-start.9 = (bf16[512,384]{1,0:T(8,128)(2,1)}, bf16[512,384]{1,0:T(8,128)(2,1)}, u32[]{:S(2)}, u32[]{:S(2)}) collective-permute-start(bf16[512,384]{1,0:T(8,128)(2,1)} %attention_mirrored.4.piece_ref), channel_id=1, source_target_pairs={{0,31},{1,30},{2,29},{3,28},{4,27},{5,26},{6,25},{7,24},{8,23},{9,... | collective-permute-start | bytes 1179656 | tf_op jit(solution)/shard_map/ppermute | solution.py:280
  135.6 21.0 %collective-permute-start.8 = (bf16[512,384]{1,0:T(8,128)(2,1)}, bf16[512,384]{1,0:T(8,128)(2,1)}, u32[]{:S(2)}, u32[]{:S(2)}) collective-permute-start(bf16[512,384]{1,0:T(8,128)(2,1)} %attention_mirrored.5.piece_ref), channel_id=1, source_target_pairs={{0,31},{1,30},{2,29},{3,28},{4,27},{5,26},{6,25},{7,24},{8,23},{9,... | collective-permute-start | bytes 1179656 | tf_op jit(solution)/shard_map/ppermute | solution.py:280

commit v4 on v3

--- a/solution.py
+++ b/solution.py
@@ -117,10 +117,7 @@
 
 
 def attention_kernel(tile, mirrored, flags_ref, q_ref, ko_ref, ks_ref, kr_ref, vo_ref, vs_ref, vr_ref, *refs):
-    if mirrored:
-        near_ref, out_ref, kbuf, vbuf = refs
-    else:
-        out_ref, kbuf, vbuf = refs
+    out_ref, kbuf, vbuf = refs
     rows, width = q_ref.shape
     head = width // 2
     sibling_left = flags_ref[0] > 0
@@ -172,17 +169,14 @@
         if mirrored:
             outs = outs[::-1]
         a = jnp.where(lane < head, outs[0], outs[1]).astype(jnp.bfloat16)
-        if mirrored:
-            a = (near_ref[here, :].astype(jnp.float32) + a.astype(jnp.float32)).astype(jnp.bfloat16)
         out_ref[here, :] = a
 
 
-def attention(q, own, sibling, remote, flags, first, count, near=None):
+def attention(q, own, sibling, remote, flags, first, count, mirrored):
     rows, width = q.shape
     pw = 2 * (width // HEADS)
     n = width // pw
     f = first
-    mirrored = near is not None
 
     def key(g):
         return n - 1 - f - g if mirrored else f + g
@@ -200,8 +194,7 @@
         out_shape=jax.ShapeDtypeStruct((rows, count * pw), jnp.bfloat16),
         grid=(count,),
         in_specs=[pl.BlockSpec(memory_space=pltpu.SMEM)]
-        + [keys(0), keys(0), keys(there), keys(0), values(0), values(there), values(0)]
-        + [out_spec] * mirrored,
+        + [keys(0), keys(0), keys(there), keys(0), values(0), values(there), values(0)],
         out_specs=out_spec,
         scratch_shapes=[
             pltpu.VMEM((rows + 2 * WINDOW, pw), jnp.bfloat16),
@@ -209,61 +202,66 @@
         ],
         compiler_params=pltpu.CompilerParams(vmem_limit_bytes=VMEM_LIMIT),
         cost_estimate=pl.CostEstimate(
-            flops=4 * count * rows * (256 + 2 * WINDOW) * 2 * pw,
-            bytes_accessed=4 * count * rows * pw,
+            flops=4 * count * rows * (256 + 2 * WINDOW) * 2 * pw // 1,
+            bytes_accessed=count * rows * pw // 1,
             transcendentals=0,
         ),
         name="attention_mirrored" if mirrored else "attention",
-    )(flags, q, own, sibling, remote, own, sibling, remote, *([near] if mirrored else []))
-
-
-def turn_kernel(piece_ref, *refs):
-    t = jnp.dot(piece_ref[...], exchange_matrix(piece_ref.shape[1]), preferred_element_type=jnp.float32)
+    )(flags, q, own, sibling, remote, own, sibling, remote)
+
+
+def added(a_ref, b_ref):
+    return (a_ref[...].astype(jnp.float32) + b_ref[...].astype(jnp.float32)).astype(jnp.bfloat16)
+
+
+def turn_kernel(a_ref, b_ref, *refs):
+    t = jnp.dot(added(a_ref, b_ref), exchange_matrix(a_ref.shape[1]), preferred_element_type=jnp.float32)
     rows_reversed(t.astype(jnp.bfloat16), refs[-1])
 
 
-def turn(piece, first, width, held):
-    rows, columns = piece.shape
+def turn(a, b, first, width, held):
+    rows, columns = a.shape
     pw = 2 * (width // HEADS)
     n = width // pw
     f = first
     held = [] if held is None else [held]
+    block = pl.BlockSpec((rows, pw), lambda g: (0, g))
     return pl.pallas_call(
         turn_kernel,
         out_shape=jax.ShapeDtypeStruct((rows, width), jnp.bfloat16),
         grid=(columns // pw,),
-        in_specs=[pl.BlockSpec((rows, pw), lambda g: (0, g))]
-        + [pl.BlockSpec(memory_space=pl.ANY)] * len(held),
+        in_specs=[block, block] + [pl.BlockSpec(memory_space=pl.ANY)] * len(held),
         out_specs=pl.BlockSpec((rows, pw), lambda g: (0, n - 1 - f - g)),
-        input_output_aliases={1: 0} if held else {},
+        input_output_aliases={2: 0} if held else {},
         compiler_params=pltpu.CompilerParams(vmem_limit_bytes=VMEM_LIMIT),
         cost_estimate=SMALL,
         name="turn",
-    )(piece, *held)
-
-
-def place_kernel(first, piece_ref, *refs):
-    out_ref, sem = refs[-2:]
-    copy = pltpu.make_async_copy(piece_ref, out_ref.at[:, pl.ds(first, piece_ref.shape[1])], sem)
+    )(a, b, *held)
+
+
+def place_kernel(first, a_ref, b_ref, *refs):
+    out_ref, sum_ref, sem = refs[-3:]
+    sum_ref[...] = added(a_ref, b_ref)
+    copy = pltpu.make_async_copy(sum_ref, out_ref.at[:, pl.ds(first, sum_ref.shape[1])], sem)
     copy.start()
     copy.wait()
 
 
-def place(piece, first, width, held):
-    rows = piece.shape[0]
+def place(a, b, first, width, held):
+    rows = a.shape[0]
     held = [] if held is None else [held]
     anywhere = pl.BlockSpec(memory_space=pl.ANY)
     return pl.pallas_call(
         functools.partial(place_kernel, first * 2 * (width // HEADS)),
         out_shape=jax.ShapeDtypeStruct((rows, width), jnp.bfloat16),
-        in_specs=[anywhere] * (1 + len(held)),
+        in_specs=[pl.BlockSpec(memory_space=pltpu.VMEM)] * 2 + [anywhere] * len(held),
         out_specs=anywhere,
-        scratch_shapes=[pltpu.SemaphoreType.DMA(())],
-        input_output_aliases={1: 0} if held else {},
+        scratch_shapes=[pltpu.VMEM(a.shape, jnp.bfloat16), pltpu.SemaphoreType.DMA(())],
+        input_output_aliases={2: 0} if held else {},
         compiler_params=pltpu.CompilerParams(vmem_limit_bytes=VMEM_LIMIT),
         cost_estimate=SMALL,
         name="place",
-    )(piece, *held)
+    )(a, b, *held)
 
 
 def per_device(x_fwd, x_rev, gain, w_qkv):
@@ -288,35 +286,33 @@
     s_q, s_chip = project([after(x_rev, f_q), s_y], gain, w_qkv, scale, True, True)
     s_x = send(after(x_rev, s_q), beside)
 
-    a_moved = []
+    last = len(CHUNKS) - 1
     f_x = after(f_x, s_q)
     f_rem = project([f_x], gain, w_qkv, scale, False, False)
     flags = after(flags, f_rem)
-    for k in range(len(CHUNKS)):
-        if k == 2:
-            a_moved[0], s_x, flags = lax.optimization_barrier((a_moved[0], s_x, flags))
-        a = attention(f_q, f_chip, f_chip, f_rem, flags, firsts[k], CHUNKS[k])
-        flags = after(flags, a)
-        a_moved.append(send(a, mirror))
-    s_rem = project([after(s_x, a)], gain, w_qkv, scale, True, False)
-
-    mine, moved, fwd, rev = [], [], None, None
-    last = len(CHUNKS) - 1
+    a_f, f_moved = [], []
     for k in range(last + 1):
-        ahead = min(k + 1, last)
-        a_moved[ahead], flags = lax.optimization_barrier((a_moved[ahead], flags))
-        if k >= 2:
-            rev = turn(after(mine[k - 2], mine[k - 1]), firsts[k - 2], width, rev)
-            fwd = place(after(moved[k - 2], rev), firsts[k - 2], width, fwd)
-            flags = after(flags, fwd)
-        y = attention(s_q, s_chip, s_chip, s_rem, flags, firsts[k], CHUNKS[k], a_moved[k])
-        flags = after(flags, y)
-        mine.append(y)
-        moved.append(send(y, mirror))
-    for k in (last - 1, last):
-        rev = turn(after(mine[k], mine[-1]), firsts[k], width, rev)
-    for k in (last - 1, last):
-        fwd = place(after(moved[k], rev), firsts[k], width, fwd)
+        if k == last:
+            f_moved[0], s_x, flags = lax.optimization_barrier((f_moved[0], s_x, flags))
+        a_f.append(attention(f_q, f_chip, f_chip, f_rem, flags, firsts[k], CHUNKS[k], False))
+        flags = after(flags, a_f[k])
+        f_moved.append(send(a_f[k], mirror))
+    s_rem = project([after(s_x, a_f[last])], gain, w_qkv, scale, True, False)
+    flags = after(flags, s_rem)
+    a_s, s_moved = [], []
+    for k in range(last + 1):
+        if 1 <= k <= last:
+            f_moved[k], flags = lax.optimization_barrier((f_moved[k], flags))
+        if 0 <= k - 2:
+            s_moved[k - 2], flags = lax.optimization_barrier((s_moved[k - 2], flags))
+        a_s.append(attention(s_q, s_chip, s_chip, s_rem, flags, firsts[k], CHUNKS[k], True))
+        flags = after(flags, a_s[k])
+        s_moved.append(send(a_s[k], mirror))
+    fwd, rev = None, None
+    for k in range(last + 1):
+        rev = turn(after(a_s[k], a_s[last]), f_moved[k], firsts[k], width, rev)
+    for k in range(last + 1):
+        fwd = place(after(a_f[k], rev), s_moved[k], firsts[k], width, fwd)
     return fwd, rev
 
 

time: 172 us -> 152 us (0.88)
  Pallas kernels: 124 us -> 95.1 us
  waiting for transfers between devices: 16.8 us -> 25.8 us
    pallas_call x3, Pallas kernels: 35.1 us -> 5.73 us  [place(): pl.pallas_call(functools.partial(place_kernel, first * 2 * (width // HEAD...]
    ppermute x10, waiting for transfers between devices: 16.8 us -> 25.8 us  [send(): return lax.ppermute(x, 'seq', pairs)]
  transfers between devices with their start and end apart: 10 -> 10, of which waited for: 2 -> 2; matrix products, arithmetic and copies ran while one was open for 0% -> 0% of each run, Pallas kernels for 66% -> 62%
where the time goes in v4:
time: 152 us; the launch traced here: 150 us
  Pallas kernels  95.1 us (63%)
  starting transfers between devices  27.2 us (18%)
  waiting for transfers between devices  25.8 us (17%)
    pallas_call x6, Pallas kernels, attention(): pl.pallas_call(functools.partial(attention_kernel, min(256, rows), mirror...  47 us
    pallas_call x4, Pallas kernels, project(): pl.pallas_call(functools.partial(project_kernel, scale, mirrored, with_q,...  33.2 us
    ppermute x10, starting transfers between devices, send(): return lax.ppermute(x, 'seq', pairs)  27.2 us
    ppermute x10, waiting for transfers between devices, send(): return lax.ppermute(x, 'seq', pairs)  25.8 us
    pallas_call x3, Pallas kernels, turn(): pl.pallas_call(turn_kernel, out_shape=jax.ShapeDtypeStruct((rows, width),...  9.22 us
    pallas_call x3, Pallas kernels, place(): pl.pallas_call(functools.partial(place_kernel, first * 2 * (width // HEAD...  5.73 us
  transfers between devices with their start and end apart: 10, of which 2 were waited for; matrix products, arithmetic and copies ran while one was open for 0% of the time, Pallas kernels for 62%

profile of v4, /device:TPU:25, one launch (start us, length us, event | category | flops | bytes accessed | tf_op | source)
XLA Modules:
  0.0 149.7 jit_solution(4210118265096379618)
XLA Ops:
  0.6 0.8 collective-permute-start.1
  1.5 4.5 %collective-permute-start = (bf16[512,1024]{1,0:T(8,128)(2,1)}, bf16[512,1024]{1,0:T(8,128)(2,1)}, u32[]{:S(2)}, u32[]{:S(2)}) collective-permute-start(bf16[512,1024]{1,0:T(8,128)(2,1)} %refs_0_), channel_id=1, source_target_pairs={{1,2},{2,1},{3,4},{4,3},{5,6},{6,5},{7,8},{8,7},{9,10},{10,9},{11,... | collective-permute-start | bytes 3145736 | tf_op jit(solution)/shard_map/ppermute | solution.py:278
  6.6 10.4 %project.4 = (bf16[512,1024]{1,0:T(8,128)(2,1)}, bf16[1024,2048]{1,0:T(8,128)(2,1)}) custom-call(bf16[512,1024]{1,0:T(8,128)(2,1)} %refs_0_, bf16[512,1024]{1,0:T(8,128)(2,1)} %collective-permute-done.1.refs_1_, bf16[1024]{0:T(1024)(128)(2,1)} %refs_1_.3, bf16[1024,3072]{1,0:T(8,128)(2,1)} %refs_2_.7), custom_call_target="tpu_custom_call" | custom-call | flops 1 | bytes 1 | tf_op jit(solution)/shard_map/project/pallas_call | solution.py:99
  17.0 11.3 %project.5 = (bf16[512,1024]{1,0:T(8,128)(2,1)}, bf16[1024,2048]{1,0:T(8,128)(2,1)}) custom-call(bf16[512,1024]{1,0:T(8,128)(2,1)} %refs_0_.1, bf16[512,1024]{1,0:T(8,128)(2,1)} %collective-permute-done.2.refs_1_, bf16[1024]{0:T(1024)(128)(2,1)} %refs_1_.3, bf16[1024,3072]{1,0:T(8,128)(2,1)} %refs_2_.7), custom_call_target="tpu_custom_call" | custom-call | flops 1 | bytes 1 | tf_op jit(solution)/shard_map/project/pallas_call | solution.py:99
  28.3 3.6 %collective-permute-start.4 = (bf16[512,1024]{1,0:T(8,128)(2,1)}, bf16[512,1024]{1,0:T(8,128)(2,1)}, u32[]{:S(2)}, u32[]{:S(2)}) collective-permute-start(bf16[512,1024]{1,0:T(8,128)(2,1)} %refs_0_.1), channel_id=1, source_target_pairs={{1,2},{2,1},{3,4},{4,3},{5,6},{6,5},{7,8},{8,7},{9,10},{10,9},{11,... | collective-permute-start | bytes 3145736 | tf_op jit(solution)/shard_map/ppermute | solution.py:278
  31.9 5.7 %project.6.kr_ref.vr_ref = bf16[512,2048]{1,0:T(8,128)(2,1)} custom-call(bf16[512,1024]{1,0:T(8,128)(2,1)} %collective-permute-done.refs_0_, bf16[1024]{0:T(1024)(128)(2,1)} %refs_1_.3, bf16[1024,3072]{1,0:T(8,128)(2,1)} %refs_2_.7), custom_call_target="tpu_custom_call" | custom-call | flops 1 | bytes 1 | tf_op jit(solution)/shard_map/project/pallas_call | solution.py:99
  37.6 6.3 %attention.3.a_ref = bf16[512,256]{1,0:T(8,128)(2,1)} custom-call(s32[2]{0:T(128)} %pad_add_fusion.flags_ref, bf16[512,1024]{1,0:T(8,128)(2,1)} %get-tuple-element.34.q_ref, bf16[1024,2048]{1,0:T(8,128)(2,1)} %get-tuple-element.39.ko_ref.ks_ref.vo_ref.vs_ref, bf16[1024,2048]{1,0:T(8,128)(2,1)} %get-tuple-element.39.ko_ref.ks_ref.vo_ref.vs_ref, ...), custom_call_target="tpu_custom_call" | custom-call | flops 1342177280 | bytes 131072 | tf_op jit(solution)/shard_map/attention/pallas_call | solution.py:192
  44.0 6.5 %collective-permute-start.3 = (bf16[512,256]{1,0:T(8,128)(2,1)}, bf16[512,256]{1,0:T(8,128)(2,1)}, u32[]{:S(2)}, u32[]{:S(2)}) collective-permute-start(bf16[512,256]{1,0:T(8,128)(2,1)} %attention.3.a_ref), channel_id=1, source_target_pairs={{0,31},{1,30},{2,29},{3,28},{4,27},{5,26},{6,25},{7,24},{8,23},{9,... | collective-permute-start | bytes 786440 | tf_op jit(solution)/shard_map/ppermute | solution.py:278
  50.5 8.5 %attention.4.a_ref = bf16[512,384]{1,0:T(8,128)(2,1)} custom-call(s32[2]{0:T(128)} %pad_add_fusion.flags_ref, bf16[512,1024]{1,0:T(8,128)(2,1)} %get-tuple-element.34.q_ref, bf16[1024,2048]{1,0:T(8,128)(2,1)} %get-tuple-element.39.ko_ref.ks_ref.vo_ref.vs_ref, bf16[1024,2048]{1,0:T(8,128)(2,1)} %get-tuple-element.39.ko_ref.ks_ref.vo_ref.vs_ref, ...), custom_call_target="tpu_custom_call" | custom-call | flops 2013265920 | bytes 196608 | tf_op jit(solution)/shard_map/attention/pallas_call | solution.py:192
  59.0 11.8 %collective-permute-done.3.b_ref = bf16[512,256]{1,0:T(8,128)(2,1)} collective-permute-done((bf16[512,256]{1,0:T(8,128)(2,1)}, bf16[512,256]{1,0:T(8,128)(2,1)}, u32[]{:S(2)}, u32[]{:S(2)}) %collective-permute-start.3) | collective-permute-done | bytes 262176 | tf_op jit(solution)/shard_map/ppermute | solution.py:278
  70.8 8.5 %attention.5.a_ref = bf16[512,384]{1,0:T(8,128)(2,1)} custom-call(s32[2]{0:T(128)} %pad_add_fusion.flags_ref, bf16[512,1024]{1,0:T(8,128)(2,1)} %get-tuple-element.34.q_ref, bf16[1024,2048]{1,0:T(8,128)(2,1)} %get-tuple-element.39.ko_ref.ks_ref.vo_ref.vs_ref, bf16[1024,2048]{1,0:T(8,128)(2,1)} %get-tuple-element.39.ko_ref.ks_ref.vo_ref.vs_ref, ...), custom_call_target="tpu_custom_call" | custom-call | flops 2013265920 | bytes 196608 | tf_op jit(solution)/shard_map/attention/pallas_call | solution.py:192
  79.3 6.2 %collective-permute-start.6 = (bf16[512,384]{1,0:T(8,128)(2,1)}, bf16[512,384]{1,0:T(8,128)(2,1)}, u32[]{:S(2)}, u32[]{:S(2)}) collective-permute-start(bf16[512,384]{1,0:T(8,128)(2,1)} %attention.5.a_ref), channel_id=1, source_target_pairs={{0,31},{1,30},{2,29},{3,28},{4,27},{5,26},{6,25},{7,24},{8,23},{9,... | collective-permute-start | bytes 1179656 | tf_op jit(solution)/shard_map/ppermute | solution.py:278
  85.6 5.9 %project.7.kr_ref.vr_ref = bf16[512,2048]{1,0:T(8,128)(2,1)} custom-call(bf16[512,1024]{1,0:T(8,128)(2,1)} %collective-permute-done.4.refs_0_, bf16[1024]{0:T(1024)(128)(2,1)} %refs_1_.3, bf16[1024,3072]{1,0:T(8,128)(2,1)} %refs_2_.7), custom_call_target="tpu_custom_call" | custom-call | flops 1 | bytes 1 | tf_op jit(solution)/shard_map/project/pallas_call | solution.py:99
  91.5 6.4 %attention_mirrored.3.a_ref = bf16[512,256]{1,0:T(8,128)(2,1)} custom-call(s32[2]{0:T(128)} %pad_add_fusion.flags_ref, bf16[512,1024]{1,0:T(8,128)(2,1)} %get-tuple-element.36.q_ref, bf16[1024,2048]{1,0:T(8,128)(2,1)} %get-tuple-element.48.ko_ref.ks_ref.vo_ref.vs_ref, bf16[1024,2048]{1,0:T(8,128)(2,1)} %get-tuple-element.48.ko_ref.ks_ref.vo_ref.vs_ref, ...), custom_call_target="tpu_custom_call" | custom-call | flops 1342177280 | bytes 131072 | tf_op jit(solution)/shard_map/attention_mirrored/pallas_call | solution.py:192
  97.9 8.7 %attention_mirrored.4.a_ref = bf16[512,384]{1,0:T(8,128)(2,1)} custom-call(s32[2]{0:T(128)} %pad_add_fusion.flags_ref, bf16[512,1024]{1,0:T(8,128)(2,1)} %get-tuple-element.36.q_ref, bf16[1024,2048]{1,0:T(8,128)(2,1)} %get-tuple-element.48.ko_ref.ks_ref.vo_ref.vs_ref, bf16[1024,2048]{1,0:T(8,128)(2,1)} %get-tuple-element.48.ko_ref.ks_ref.vo_ref.vs_ref, ...), custom_call_target="tpu_custom_call" | custom-call | flops 2013265920 | bytes 196608 | tf_op jit(solution)/shard_map/attention_mirrored/pallas_call | solution.py:192
  106.5 5.3 %collective-permute-start.9 = (bf16[512,384]{1,0:T(8,128)(2,1)}, bf16[512,384]{1,0:T(8,128)(2,1)}, u32[]{:S(2)}, u32[]{:S(2)}) collective-permute-start(bf16[512,384]{1,0:T(8,128)(2,1)} %attention_mirrored.4.a_ref), channel_id=1, source_target_pairs={{0,31},{1,30},{2,29},{3,28},{4,27},{5,26},{6,25},{7,24},{8,23},{9,... | collective-permute-start | bytes 1179656 | tf_op jit(solution)/shard_map/ppermute | solution.py:278
  111.9 14.0 %collective-permute-done.5.b_ref = bf16[512,256]{1,0:T(8,128)(2,1)} collective-permute-done((bf16[512,256]{1,0:T(8,128)(2,1)}, bf16[512,256]{1,0:T(8,128)(2,1)}, u32[]{:S(2)}, u32[]{:S(2)}) %collective-permute-start.5) | collective-permute-done | bytes 262176 | tf_op jit(solution)/shard_map/ppermute | solution.py:278
  125.9 8.6 %attention_mirrored.5.a_ref = bf16[512,384]{1,0:T(8,128)(2,1)} custom-call(s32[2]{0:T(128)} %pad_add_fusion.flags_ref, bf16[512,1024]{1,0:T(8,128)(2,1)} %get-tuple-element.36.q_ref, bf16[1024,2048]{1,0:T(8,128)(2,1)} %get-tuple-element.48.ko_ref.ks_ref.vo_ref.vs_ref, bf16[1024,2048]{1,0:T(8,128)(2,1)} %get-tuple-element.48.ko_ref.ks_ref.vo_ref.vs_ref, ...), custom_call_target="tpu_custom_call" | custom-call | flops 2013265920 | bytes 196608 | tf_op jit(solution)/shard_map/attention_mirrored/pallas_call | solution.py:192
  134.5 2.4 %turn.3.refs_0_ = bf16[512,1024]{1,0:T(8,128)(2,1)} custom-call(bf16[512,256]{1,0:T(8,128)(2,1)} %attention_mirrored.3.a_ref, bf16[512,256]{1,0:T(8,128)(2,1)} %collective-permute-done.3.b_ref), custom_call_target="tpu_custom_call" | custom-call | flops 1 | bytes 1 | tf_op jit(solution)/shard_map/turn/pallas_call | solution.py:229
  136.9 3.4 %turn.4.refs_0_ = bf16[512,1024]{1,0:T(8,128)(2,1)} custom-call(bf16[512,384]{1,0:T(8,128)(2,1)} %attention_mirrored.4.a_ref, bf16[512,384]{1,0:T(8,128)(2,1)} %collective-permute-done.7.b_ref, bf16[512,1024]{1,0:T(8,128)(2,1)} %turn.3.refs_0_), custom_call_target="tpu_custom_call", output_to_operand_aliasing={{}: (2, {})} | custom-call | flops 1 | bytes 1 | tf_op jit(solution)/shard_map/turn/pallas_call | solution.py:229
  140.3 3.4 %turn.5 = bf16[512,1024]{1,0:T(8,128)(2,1)} custom-call(bf16[512,384]{1,0:T(8,128)(2,1)} %attention_mirrored.5.a_ref, bf16[512,384]{1,0:T(8,128)(2,1)} %collective-permute-done.6.b_ref, bf16[512,1024]{1,0:T(8,128)(2,1)} %turn.4.refs_0_), custom_call_target="tpu_custom_call", output_to_operand_aliasing={{}: (2, {})} | custom-call | flops 1 | bytes 1 | tf_op jit(solution)/shard_map/turn/pallas_call | solution.py:229
  143.7 1.8 %place.3.refs_0_ = bf16[512,1024]{1,0:T(8,128)(2,1)} custom-call(bf16[512,256]{1,0:T(8,128)(2,1)} %attention.3.a_ref, bf16[512,256]{1,0:T(8,128)(2,1)} %collective-permute-done.5.b_ref), custom_call_target="tpu_custom_call" | custom-call | flops 1 | bytes 1 | tf_op jit(solution)/shard_map/place/pallas_call | solution.py:254
  145.5 2.0 %place.4.refs_0_ = bf16[512,1024]{1,0:T(8,128)(2,1)} custom-call(bf16[512,384]{1,0:T(8,128)(2,1)} %attention.4.a_ref, bf16[512,384]{1,0:T(8,128)(2,1)} %collective-permute-done.9.b_ref, bf16[512,1024]{1,0:T(8,128)(2,1)} %place.3.refs_0_), custom_call_target="tpu_custom_call", output_to_operand_aliasing={{}: (2, {})} | custom-call | flops 1 | bytes 1 | tf_op jit(solution)/shard_map/place/pallas_call | solution.py:254
  147.5 2.0 %place.5 = bf16[512,1024]{1,0:T(8,128)(2,1)} custom-call(bf16[512,384]{1,0:T(8,128)(2,1)} %attention.5.a_ref, bf16[512,384]{1,0:T(8,128)(2,1)} %collective-permute-done.8.b_ref, bf16[512,1024]{1,0:T(8,128)(2,1)} %place.4.refs_0_), custom_call_target="tpu_custom_call", output_to_operand_aliasing={{}: (2, {})} | custom-call | flops 1 | bytes 1 | tf_op jit(solution)/shard_map/place/pallas_call | solution.py:254
  (13 shorter events, 0.8 us)
Async XLA Ops:
  0.6 6.0 %collective-permute-start.1 = (bf16[512,1024]{1,0:T(8,128)(2,1)}, bf16[512,1024]{1,0:T(8,128)(2,1)}, u32[]{:S(2)}, u32[]{:S(2)}) collective-permute-start(bf16[512,1024]{1,0:T(8,128)(2,1)} %refs_0_), channel_id=1, source_target_pairs={{0,1},{1,0},{2,3},{3,2},{4,5},{5,4},{6,7},{7,6},{8,9},{9,8},{10,11... | collective-permute-start | bytes 3145736 | tf_op jit(solution)/shard_map/ppermute | solution.py:278
  1.4 15.6 %collective-permute-start.2 = (bf16[512,1024]{1,0:T(8,128)(2,1)}, bf16[512,1024]{1,0:T(8,128)(2,1)}, u32[]{:S(2)}, u32[]{:S(2)}) collective-permute-start(bf16[512,1024]{1,0:T(8,128)(2,1)} %refs_0_.1), channel_id=1, source_target_pairs={{0,1},{1,0},{2,3},{3,2},{4,5},{5,4},{6,7},{7,6},{8,9},{9,8},{10,11... | collective-permute-start | bytes 3145736 | tf_op jit(solution)/shard_map/ppermute | solution.py:278
  1.5 30.4 %collective-permute-start = (bf16[512,1024]{1,0:T(8,128)(2,1)}, bf16[512,1024]{1,0:T(8,128)(2,1)}, u32[]{:S(2)}, u32[]{:S(2)}) collective-permute-start(bf16[512,1024]{1,0:T(8,128)(2,1)} %refs_0_), channel_id=1, source_target_pairs={{1,2},{2,1},{3,4},{4,3},{5,6},{6,5},{7,8},{8,7},{9,10},{10,9},{11,... | collective-permute-start | bytes 3145736 | tf_op jit(solution)/shard_map/ppermute | solution.py:278
  28.3 42.6 %collective-permute-start.4 = (bf16[512,1024]{1,0:T(8,128)(2,1)}, bf16[512,1024]{1,0:T(8,128)(2,1)}, u32[]{:S(2)}, u32[]{:S(2)}) collective-permute-start(bf16[512,1024]{1,0:T(8,128)(2,1)} %refs_0_.1), channel_id=1, source_target_pairs={{1,2},{2,1},{3,4},{4,3},{5,6},{6,5},{7,8},{8,7},{9,10},{10,9},{11,... | collective-permute-start | bytes 3145736 | tf_op jit(solution)/shard_map/ppermute | solution.py:278
  44.0 26.9 %collective-permute-start.3 = (bf16[512,256]{1,0:T(8,128)(2,1)}, bf16[512,256]{1,0:T(8,128)(2,1)}, u32[]{:S(2)}, u32[]{:S(2)}) collective-permute-start(bf16[512,256]{1,0:T(8,128)(2,1)} %attention.3.a_ref), channel_id=1, source_target_pairs={{0,31},{1,30},{2,29},{3,28},{4,27},{5,26},{6,25},{7,24},{8,23},{9,... | collective-permute-start | bytes 786440 | tf_op jit(solution)/shard_map/ppermute | solution.py:278
  59.0 38.9 %collective-permute-start.7 = (bf16[512,384]{1,0:T(8,128)(2,1)}, bf16[512,384]{1,0:T(8,128)(2,1)}, u32[]{:S(2)}, u32[]{:S(2)}) collective-permute-start(bf16[512,384]{1,0:T(8,128)(2,1)} %attention.4.a_ref), channel_id=1, source_target_pairs={{0,31},{1,30},{2,29},{3,28},{4,27},{5,26},{6,25},{7,24},{8,23},{9,... | collective-permute-start | bytes 1179656 | tf_op jit(solution)/shard_map/ppermute | solution.py:278
  79.3 32.5 %collective-permute-start.6 = (bf16[512,384]{1,0:T(8,128)(2,1)}, bf16[512,384]{1,0:T(8,128)(2,1)}, u32[]{:S(2)}, u32[]{:S(2)}) collective-permute-start(bf16[512,384]{1,0:T(8,128)(2,1)} %attention.5.a_ref), channel_id=1, source_target_pairs={{0,31},{1,30},{2,29},{3,28},{4,27},{5,26},{6,25},{7,24},{8,23},{9,... | collective-permute-start | bytes 1179656 | tf_op jit(solution)/shard_map/ppermute | solution.py:278
  97.8 28.0 %collective-permute-start.5 = (bf16[512,256]{1,0:T(8,128)(2,1)}, bf16[512,256]{1,0:T(8,128)(2,1)}, u32[]{:S(2)}, u32[]{:S(2)}) collective-permute-start(bf16[512,256]{1,0:T(8,128)(2,1)} %attention_mirrored.3.a_ref), channel_id=1, source_target_pairs={{0,31},{1,30},{2,29},{3,28},{4,27},{5,26},{6,25},{7,24},{8,23},{9,... | collective-permute-start | bytes 786440 | tf_op jit(solution)/shard_map/ppermute | solution.py:278
  106.5 39.0 %collective-permute-start.9 = (bf16[512,384]{1,0:T(8,128)(2,1)}, bf16[512,384]{1,0:T(8,128)(2,1)}, u32[]{:S(2)}, u32[]{:S(2)}) collective-permute-start(bf16[512,384]{1,0:T(8,128)(2,1)} %attention_mirrored.4.a_ref), channel_id=1, source_target_pairs={{0,31},{1,30},{2,29},{3,28},{4,27},{5,26},{6,25},{7,24},{8,23},{9,... | collective-permute-start | bytes 1179656 | tf_op jit(solution)/shard_map/ppermute | solution.py:278
  134.5 13.0 %collective-permute-start.8 = (bf16[512,384]{1,0:T(8,128)(2,1)}, bf16[512,384]{1,0:T(8,128)(2,1)}, u32[]{:S(2)}, u32[]{:S(2)}) collective-permute-start(bf16[512,384]{1,0:T(8,128)(2,1)} %attention_mirrored.5.a_ref), channel_id=1, source_target_pairs={{0,31},{1,30},{2,29},{3,28},{4,27},{5,26},{6,25},{7,24},{8,23},{9,... | collective-permute-start | bytes 1179656 | tf_op jit(solution)/shard_map/ppermute | solution.py:278

commit v5 on v4

--- a/solution.py
+++ b/solution.py
@@ -293,24 +293,25 @@
     a_f, f_moved = [], []
     for k in range(last + 1):
         if k == last:
-            f_moved[0], s_x, flags = lax.optimization_barrier((f_moved[0], s_x, flags))
+            s_x, flags = lax.optimization_barrier((s_x, flags))
         a_f.append(attention(f_q, f_chip, f_chip, f_rem, flags, firsts[k], CHUNKS[k], False))
         flags = after(flags, a_f[k])
         f_moved.append(send(a_f[k], mirror))
     s_rem = project([after(s_x, a_f[last])], gain, w_qkv, scale, True, False)
     flags = after(flags, s_rem)
-    a_s, s_moved = [], []
+    f_moved[0], flags = lax.optimization_barrier((f_moved[0], flags))
+    a_s, s_moved, fwd, rev = [], [], None, None
     for k in range(last + 1):
         if 1 <= k <= last:
             f_moved[k], flags = lax.optimization_barrier((f_moved[k], flags))
-        if 0 <= k - 2:
-            s_moved[k - 2], flags = lax.optimization_barrier((s_moved[k - 2], flags))
+        if k == last:
+            for m in range(last):
+                rev = turn(after(a_s[m], a_s[last - 1]), f_moved[m], firsts[m], width, rev)
+            s_moved[0], flags = lax.optimization_barrier((s_moved[0], flags, rev))[:2]
         a_s.append(attention(s_q, s_chip, s_chip, s_rem, flags, firsts[k], CHUNKS[k], True))
         flags = after(flags, a_s[k])
         s_moved.append(send(a_s[k], mirror))
-    fwd, rev = None, None
-    for k in range(last + 1):
-        rev = turn(after(a_s[k], a_s[last]), f_moved[k], firsts[k], width, rev)
+    rev = turn(a_s[last], f_moved[last], firsts[last], width, rev)
     for k in range(last + 1):
         fwd = place(after(a_f[k], rev), s_moved[k], firsts[k], width, fwd)
     return fwd, rev

time: 152 us -> 146 us (0.961); the launches traced: 150 us -> 145 us
  waiting for transfers between devices: 25.8 us -> 22.2 us
    ppermute x10, waiting for transfers between devices: 25.8 us -> 22.2 us  [send(): return lax.ppermute(x, 'seq', pairs)]
  transfers between devices with their start and end apart: 10 -> 10, of which waited for: 2 -> 3; matrix products, arithmetic and copies ran while one was open for 0% -> 0% of each run, Pallas kernels for 62% -> 64%
where the time goes in v5:
time: 146 us; the launch traced here: 145 us
  Pallas kernels  95.1 us (65%)
  starting transfers between devices  26.5 us (18%)
  waiting for transfers between devices  22.2 us (15%)
    pallas_call x6, Pallas kernels, attention(): pl.pallas_call(functools.partial(attention_kernel, min(256, rows), mirror...  47 us
    pallas_call x4, Pallas kernels, project(): pl.pallas_call(functools.partial(project_kernel, scale, mirrored, with_q,...  33.2 us
    ppermute x10, starting transfers between devices, send(): return lax.ppermute(x, 'seq', pairs)  26.5 us
    ppermute x10, waiting for transfers between devices, send(): return lax.ppermute(x, 'seq', pairs)  22.2 us
    pallas_call x3, Pallas kernels, turn(): pl.pallas_call(turn_kernel, out_shape=jax.ShapeDtypeStruct((rows, width),...  9.2 us
    pallas_call x3, Pallas kernels, place(): pl.pallas_call(functools.partial(place_kernel, first * 2 * (width // HEAD...  5.73 us
  transfers between devices with their start and end apart: 10, of which 3 were waited for; matrix products, arithmetic and copies ran while one was open for 0% of the time, Pallas kernels for 64%

profile of v5, /device:TPU:25, one launch (start us, length us, event | category | flops | bytes accessed | tf_op | source)
XLA Modules:
  0.0 145.3 jit_solution(10417098555263097512)
XLA Ops:
  1.5 4.5 %collective-permute-start.3 = (bf16[512,1024]{1,0:T(8,128)(2,1)}, bf16[512,1024]{1,0:T(8,128)(2,1)}, u32[]{:S(2)}, u32[]{:S(2)}) collective-permute-start(bf16[512,1024]{1,0:T(8,128)(2,1)} %refs_0_), channel_id=1, source_target_pairs={{1,2},{2,1},{3,4},{4,3},{5,6},{6,5},{7,8},{8,7},{9,10},{10,9},{11,... | collective-permute-start | bytes 3145736 | tf_op jit(solution)/shard_map/ppermute | solution.py:278
  6.6 10.4 %project.4 = (bf16[512,1024]{1,0:T(8,128)(2,1)}, bf16[1024,2048]{1,0:T(8,128)(2,1)}) custom-call(bf16[512,1024]{1,0:T(8,128)(2,1)} %refs_0_, bf16[512,1024]{1,0:T(8,128)(2,1)} %collective-permute-done.refs_1_, bf16[1024]{0:T(1024)(128)(2,1)} %refs_1_.3, bf16[1024,3072]{1,0:T(8,128)(2,1)} %refs_2_.7), custom_call_target="tpu_custom_call" | custom-call | flops 1 | bytes 1 | tf_op jit(solution)/shard_map/project/pallas_call | solution.py:99
  17.0 11.3 %project.5 = (bf16[512,1024]{1,0:T(8,128)(2,1)}, bf16[1024,2048]{1,0:T(8,128)(2,1)}) custom-call(bf16[512,1024]{1,0:T(8,128)(2,1)} %refs_0_.1, bf16[512,1024]{1,0:T(8,128)(2,1)} %collective-permute-done.1.refs_1_, bf16[1024]{0:T(1024)(128)(2,1)} %refs_1_.3, bf16[1024,3072]{1,0:T(8,128)(2,1)} %refs_2_.7), custom_call_target="tpu_custom_call" | custom-call | flops 1 | bytes 1 | tf_op jit(solution)/shard_map/project/pallas_call | solution.py:99
  28.3 3.6 %collective-permute-start.2 = (bf16[512,1024]{1,0:T(8,128)(2,1)}, bf16[512,1024]{1,0:T(8,128)(2,1)}, u32[]{:S(2)}, u32[]{:S(2)}) collective-permute-start(bf16[512,1024]{1,0:T(8,128)(2,1)} %refs_0_.1), channel_id=1, source_target_pairs={{1,2},{2,1},{3,4},{4,3},{5,6},{6,5},{7,8},{8,7},{9,10},{10,9},{11,... | collective-permute-start | bytes 3145736 | tf_op jit(solution)/shard_map/ppermute | solution.py:278
  31.9 5.7 %project.6.kr_ref.vr_ref = bf16[512,2048]{1,0:T(8,128)(2,1)} custom-call(bf16[512,1024]{1,0:T(8,128)(2,1)} %collective-permute-done.3.refs_0_, bf16[1024]{0:T(1024)(128)(2,1)} %refs_1_.3, bf16[1024,3072]{1,0:T(8,128)(2,1)} %refs_2_.7), custom_call_target="tpu_custom_call" | custom-call | flops 1 | bytes 1 | tf_op jit(solution)/shard_map/project/pallas_call | solution.py:99
  37.6 6.3 %attention.3.a_ref = bf16[512,256]{1,0:T(8,128)(2,1)} custom-call(s32[2]{0:T(128)} %pad_add_fusion.flags_ref, bf16[512,1024]{1,0:T(8,128)(2,1)} %get-tuple-element.34.q_ref, bf16[1024,2048]{1,0:T(8,128)(2,1)} %get-tuple-element.40.ko_ref.ks_ref.vo_ref.vs_ref, bf16[1024,2048]{1,0:T(8,128)(2,1)} %get-tuple-element.40.ko_ref.ks_ref.vo_ref.vs_ref, ...), custom_call_target="tpu_custom_call" | custom-call | flops 1342177280 | bytes 131072 | tf_op jit(solution)/shard_map/attention/pallas_call | solution.py:192
  44.0 6.5 %collective-permute-start.4 = (bf16[512,256]{1,0:T(8,128)(2,1)}, bf16[512,256]{1,0:T(8,128)(2,1)}, u32[]{:S(2)}, u32[]{:S(2)}) collective-permute-start(bf16[512,256]{1,0:T(8,128)(2,1)} %attention.3.a_ref), channel_id=1, source_target_pairs={{0,31},{1,30},{2,29},{3,28},{4,27},{5,26},{6,25},{7,24},{8,23},{9,... | collective-permute-start | bytes 786440 | tf_op jit(solution)/shard_map/ppermute | solution.py:278
  50.5 8.5 %attention.4.a_ref = bf16[512,384]{1,0:T(8,128)(2,1)} custom-call(s32[2]{0:T(128)} %pad_add_fusion.flags_ref, bf16[512,1024]{1,0:T(8,128)(2,1)} %get-tuple-element.34.q_ref, bf16[1024,2048]{1,0:T(8,128)(2,1)} %get-tuple-element.40.ko_ref.ks_ref.vo_ref.vs_ref, bf16[1024,2048]{1,0:T(8,128)(2,1)} %get-tuple-element.40.ko_ref.ks_ref.vo_ref.vs_ref, ...), custom_call_target="tpu_custom_call" | custom-call | flops 2013265920 | bytes 196608 | tf_op jit(solution)/shard_map/attention/pallas_call | solution.py:192
  59.0 8.5 %attention.5.a_ref = bf16[512,384]{1,0:T(8,128)(2,1)} custom-call(s32[2]{0:T(128)} %pad_add_fusion.flags_ref, bf16[512,1024]{1,0:T(8,128)(2,1)} %get-tuple-element.34.q_ref, bf16[1024,2048]{1,0:T(8,128)(2,1)} %get-tuple-element.40.ko_ref.ks_ref.vo_ref.vs_ref, bf16[1024,2048]{1,0:T(8,128)(2,1)} %get-tuple-element.40.ko_ref.ks_ref.vo_ref.vs_ref, ...), custom_call_target="tpu_custom_call" | custom-call | flops 2013265920 | bytes 196608 | tf_op jit(solution)/shard_map/attention/pallas_call | solution.py:192
  67.6 5.3 %collective-permute-start.6 = (bf16[512,384]{1,0:T(8,128)(2,1)}, bf16[512,384]{1,0:T(8,128)(2,1)}, u32[]{:S(2)}, u32[]{:S(2)}) collective-permute-start(bf16[512,384]{1,0:T(8,128)(2,1)} %attention.5.a_ref), channel_id=1, source_target_pairs={{0,31},{1,30},{2,29},{3,28},{4,27},{5,26},{6,25},{7,24},{8,23},{9,... | collective-permute-start | bytes 1179656 | tf_op jit(solution)/shard_map/ppermute | solution.py:278
  72.9 5.9 %project.7.kr_ref.vr_ref = bf16[512,2048]{1,0:T(8,128)(2,1)} custom-call(bf16[512,1024]{1,0:T(8,128)(2,1)} %collective-permute-done.2.refs_0_, bf16[1024]{0:T(1024)(128)(2,1)} %refs_1_.3, bf16[1024,3072]{1,0:T(8,128)(2,1)} %refs_2_.7), custom_call_target="tpu_custom_call" | custom-call | flops 1 | bytes 1 | tf_op jit(solution)/shard_map/project/pallas_call | solution.py:99
  78.8 6.4 %attention_mirrored.3.a_ref = bf16[512,256]{1,0:T(8,128)(2,1)} custom-call(s32[2]{0:T(128)} %pad_add_fusion.flags_ref, bf16[512,1024]{1,0:T(8,128)(2,1)} %get-tuple-element.36.q_ref, bf16[1024,2048]{1,0:T(8,128)(2,1)} %get-tuple-element.49.ko_ref.ks_ref.vo_ref.vs_ref, bf16[1024,2048]{1,0:T(8,128)(2,1)} %get-tuple-element.49.ko_ref.ks_ref.vo_ref.vs_ref, ...), custom_call_target="tpu_custom_call" | custom-call | flops 1342177280 | bytes 131072 | tf_op jit(solution)/shard_map/attention_mirrored/pallas_call | solution.py:192
  85.2 2.2 %collective-permute-done.7.b_ref = bf16[512,384]{1,0:T(8,128)(2,1)} collective-permute-done((bf16[512,384]{1,0:T(8,128)(2,1)}, bf16[512,384]{1,0:T(8,128)(2,1)}, u32[]{:S(2)}, u32[]{:S(2)}) %collective-permute-start.7) | collective-permute-done | bytes 393248 | tf_op jit(solution)/shard_map/ppermute | solution.py:278
  87.3 8.6 %attention_mirrored.4.a_ref = bf16[512,384]{1,0:T(8,128)(2,1)} custom-call(s32[2]{0:T(128)} %pad_add_fusion.flags_ref, bf16[512,1024]{1,0:T(8,128)(2,1)} %get-tuple-element.36.q_ref, bf16[1024,2048]{1,0:T(8,128)(2,1)} %get-tuple-element.49.ko_ref.ks_ref.vo_ref.vs_ref, bf16[1024,2048]{1,0:T(8,128)(2,1)} %get-tuple-element.49.ko_ref.ks_ref.vo_ref.vs_ref, ...), custom_call_target="tpu_custom_call" | custom-call | flops 2013265920 | bytes 196608 | tf_op jit(solution)/shard_map/attention_mirrored/pallas_call | solution.py:192
  96.0 3.2 %collective-permute-start.9 = (bf16[512,384]{1,0:T(8,128)(2,1)}, bf16[512,384]{1,0:T(8,128)(2,1)}, u32[]{:S(2)}, u32[]{:S(2)}) collective-permute-start(bf16[512,384]{1,0:T(8,128)(2,1)} %attention_mirrored.4.a_ref), channel_id=1, source_target_pairs={{0,31},{1,30},{2,29},{3,28},{4,27},{5,26},{6,25},{7,24},{8,23},{9,... | collective-permute-start | bytes 1179656 | tf_op jit(solution)/shard_map/ppermute | solution.py:278
  99.1 2.4 %turn.3.refs_0_ = bf16[512,1024]{1,0:T(8,128)(2,1)} custom-call(bf16[512,256]{1,0:T(8,128)(2,1)} %attention_mirrored.3.a_ref, bf16[512,256]{1,0:T(8,128)(2,1)} %collective-permute-done.4.b_ref), custom_call_target="tpu_custom_call" | custom-call | flops 1 | bytes 1 | tf_op jit(solution)/shard_map/turn/pallas_call | solution.py:229
  101.5 3.4 %turn.4.refs_0_ = bf16[512,1024]{1,0:T(8,128)(2,1)} custom-call(bf16[512,384]{1,0:T(8,128)(2,1)} %attention_mirrored.4.a_ref, bf16[512,384]{1,0:T(8,128)(2,1)} %collective-permute-done.7.b_ref, bf16[512,1024]{1,0:T(8,128)(2,1)} %turn.3.refs_0_), custom_call_target="tpu_custom_call", output_to_operand_aliasing={{}: (2, {})} | custom-call | flops 1 | bytes 1 | tf_op jit(solution)/shard_map/turn/pallas_call | solution.py:229
  104.9 10.5 %collective-permute-done.5.b_ref = bf16[512,256]{1,0:T(8,128)(2,1)} collective-permute-done((bf16[512,256]{1,0:T(8,128)(2,1)}, bf16[512,256]{1,0:T(8,128)(2,1)}, u32[]{:S(2)}, u32[]{:S(2)}) %collective-permute-start.5) | collective-permute-done | bytes 262176 | tf_op jit(solution)/shard_map/ppermute | solution.py:278
  115.4 8.6 %attention_mirrored.5.a_ref = bf16[512,384]{1,0:T(8,128)(2,1)} custom-call(s32[2]{0:T(128)} %pad_add_fusion.flags_ref, bf16[512,1024]{1,0:T(8,128)(2,1)} %get-tuple-element.36.q_ref, bf16[1024,2048]{1,0:T(8,128)(2,1)} %get-tuple-element.49.ko_ref.ks_ref.vo_ref.vs_ref, bf16[1024,2048]{1,0:T(8,128)(2,1)} %get-tuple-element.49.ko_ref.ks_ref.vo_ref.vs_ref, ...), custom_call_target="tpu_custom_call" | custom-call | flops 2013265920 | bytes 196608 | tf_op jit(solution)/shard_map/attention_mirrored/pallas_call | solution.py:192
  124.1 2.4 %collective-permute-start.8 = (bf16[512,384]{1,0:T(8,128)(2,1)}, bf16[512,384]{1,0:T(8,128)(2,1)}, u32[]{:S(2)}, u32[]{:S(2)}) collective-permute-start(bf16[512,384]{1,0:T(8,128)(2,1)} %attention_mirrored.5.a_ref), channel_id=1, source_target_pairs={{0,31},{1,30},{2,29},{3,28},{4,27},{5,26},{6,25},{7,24},{8,23},{9,... | collective-permute-start | bytes 1179656 | tf_op jit(solution)/shard_map/ppermute | solution.py:278
  126.4 3.4 %turn.5 = bf16[512,1024]{1,0:T(8,128)(2,1)} custom-call(bf16[512,384]{1,0:T(8,128)(2,1)} %attention_mirrored.5.a_ref, bf16[512,384]{1,0:T(8,128)(2,1)} %collective-permute-done.6.b_ref, bf16[512,1024]{1,0:T(8,128)(2,1)} %turn.4.refs_0_), custom_call_target="tpu_custom_call", output_to_operand_aliasing={{}: (2, {})} | custom-call | flops 1 | bytes 1 | tf_op jit(solution)/shard_map/turn/pallas_call | solution.py:229
  131.7 2.0 %place.4.refs_0_ = bf16[512,1024]{1,0:T(8,128)(2,1)} custom-call(bf16[512,384]{1,0:T(8,128)(2,1)} %attention.4.a_ref, bf16[512,384]{1,0:T(8,128)(2,1)} %collective-permute-done.9.b_ref, bf16[512,1024]{1,0:T(8,128)(2,1)} %place.3.refs_0_), custom_call_target="tpu_custom_call", output_to_operand_aliasing={{}: (2, {})} | custom-call | flops 1 | bytes 1 | tf_op jit(solution)/shard_map/place/pallas_call | solution.py:254
  133.6 9.5 %collective-permute-done.8.b_ref = bf16[512,384]{1,0:T(8,128)(2,1)} collective-permute-done((bf16[512,384]{1,0:T(8,128)(2,1)}, bf16[512,384]{1,0:T(8,128)(2,1)}, u32[]{:S(2)}, u32[]{:S(2)}) %collective-permute-start.8) | collective-permute-done | bytes 393248 | tf_op jit(solution)/shard_map/ppermute | solution.py:278
  143.2 2.0 %place.5 = bf16[512,1024]{1,0:T(8,128)(2,1)} custom-call(bf16[512,384]{1,0:T(8,128)(2,1)} %attention.5.a_ref, bf16[512,384]{1,0:T(8,128)(2,1)} %collective-permute-done.8.b_ref, bf16[512,1024]{1,0:T(8,128)(2,1)} %place.4.refs_0_), custom_call_target="tpu_custom_call", output_to_operand_aliasing={{}: (2, {})} | custom-call | flops 1 | bytes 1 | tf_op jit(solution)/shard_map/place/pallas_call | solution.py:254
  (13 shorter events, 3.4 us)
Async XLA Ops:
  0.6 6.0 %collective-permute-start = (bf16[512,1024]{1,0:T(8,128)(2,1)}, bf16[512,1024]{1,0:T(8,128)(2,1)}, u32[]{:S(2)}, u32[]{:S(2)}) collective-permute-start(bf16[512,1024]{1,0:T(8,128)(2,1)} %refs_0_), channel_id=1, source_target_pairs={{0,1},{1,0},{2,3},{3,2},{4,5},{5,4},{6,7},{7,6},{8,9},{9,8},{10,11... | collective-permute-start | bytes 3145736 | tf_op jit(solution)/shard_map/ppermute | solution.py:278
  1.4 15.6 %collective-permute-start.1 = (bf16[512,1024]{1,0:T(8,128)(2,1)}, bf16[512,1024]{1,0:T(8,128)(2,1)}, u32[]{:S(2)}, u32[]{:S(2)}) collective-permute-start(bf16[512,1024]{1,0:T(8,128)(2,1)} %refs_0_.1), channel_id=1, source_target_pairs={{0,1},{1,0},{2,3},{3,2},{4,5},{5,4},{6,7},{7,6},{8,9},{9,8},{10,11... | collective-permute-start | bytes 3145736 | tf_op jit(solution)/shard_map/ppermute | solution.py:278
  1.5 30.4 %collective-permute-start.3 = (bf16[512,1024]{1,0:T(8,128)(2,1)}, bf16[512,1024]{1,0:T(8,128)(2,1)}, u32[]{:S(2)}, u32[]{:S(2)}) collective-permute-start(bf16[512,1024]{1,0:T(8,128)(2,1)} %refs_0_), channel_id=1, source_target_pairs={{1,2},{2,1},{3,4},{4,3},{5,6},{6,5},{7,8},{8,7},{9,10},{10,9},{11,... | collective-permute-start | bytes 3145736 | tf_op jit(solution)/shard_map/ppermute | solution.py:278
  28.3 30.8 %collective-permute-start.2 = (bf16[512,1024]{1,0:T(8,128)(2,1)}, bf16[512,1024]{1,0:T(8,128)(2,1)}, u32[]{:S(2)}, u32[]{:S(2)}) collective-permute-start(bf16[512,1024]{1,0:T(8,128)(2,1)} %refs_0_.1), channel_id=1, source_target_pairs={{1,2},{2,1},{3,4},{4,3},{5,6},{6,5},{7,8},{8,7},{9,10},{10,9},{11,... | collective-permute-start | bytes 3145736 | tf_op jit(solution)/shard_map/ppermute | solution.py:278
  44.0 34.8 %collective-permute-start.4 = (bf16[512,256]{1,0:T(8,128)(2,1)}, bf16[512,256]{1,0:T(8,128)(2,1)}, u32[]{:S(2)}, u32[]{:S(2)}) collective-permute-start(bf16[512,256]{1,0:T(8,128)(2,1)} %attention.3.a_ref), channel_id=1, source_target_pairs={{0,31},{1,30},{2,29},{3,28},{4,27},{5,26},{6,25},{7,24},{8,23},{9,... | collective-permute-start | bytes 786440 | tf_op jit(solution)/shard_map/ppermute | solution.py:278
  59.0 28.3 %collective-permute-start.7 = (bf16[512,384]{1,0:T(8,128)(2,1)}, bf16[512,384]{1,0:T(8,128)(2,1)}, u32[]{:S(2)}, u32[]{:S(2)}) collective-permute-start(bf16[512,384]{1,0:T(8,128)(2,1)} %attention.4.a_ref), channel_id=1, source_target_pairs={{0,31},{1,30},{2,29},{3,28},{4,27},{5,26},{6,25},{7,24},{8,23},{9,... | collective-permute-start | bytes 1179656 | tf_op jit(solution)/shard_map/ppermute | solution.py:278
  67.6 37.4 %collective-permute-start.6 = (bf16[512,384]{1,0:T(8,128)(2,1)}, bf16[512,384]{1,0:T(8,128)(2,1)}, u32[]{:S(2)}, u32[]{:S(2)}) collective-permute-start(bf16[512,384]{1,0:T(8,128)(2,1)} %attention.5.a_ref), channel_id=1, source_target_pairs={{0,31},{1,30},{2,29},{3,28},{4,27},{5,26},{6,25},{7,24},{8,23},{9,... | collective-permute-start | bytes 1179656 | tf_op jit(solution)/shard_map/ppermute | solution.py:278
  85.1 30.3 %collective-permute-start.5 = (bf16[512,256]{1,0:T(8,128)(2,1)}, bf16[512,256]{1,0:T(8,128)(2,1)}, u32[]{:S(2)}, u32[]{:S(2)}) collective-permute-start(bf16[512,256]{1,0:T(8,128)(2,1)} %attention_mirrored.3.a_ref), channel_id=1, source_target_pairs={{0,31},{1,30},{2,29},{3,28},{4,27},{5,26},{6,25},{7,24},{8,23},{9,... | collective-permute-start | bytes 786440 | tf_op jit(solution)/shard_map/ppermute | solution.py:278
  96.0 35.7 %collective-permute-start.9 = (bf16[512,384]{1,0:T(8,128)(2,1)}, bf16[512,384]{1,0:T(8,128)(2,1)}, u32[]{:S(2)}, u32[]{:S(2)}) collective-permute-start(bf16[512,384]{1,0:T(8,128)(2,1)} %attention_mirrored.4.a_ref), channel_id=1, source_target_pairs={{0,31},{1,30},{2,29},{3,28},{4,27},{5,26},{6,25},{7,24},{8,23},{9,... | collective-permute-start | bytes 1179656 | tf_op jit(solution)/shard_map/ppermute | solution.py:278
  124.1 19.1 %collective-permute-start.8 = (bf16[512,384]{1,0:T(8,128)(2,1)}, bf16[512,384]{1,0:T(8,128)(2,1)}, u32[]{:S(2)}, u32[]{:S(2)}) collective-permute-start(bf16[512,384]{1,0:T(8,128)(2,1)} %attention_mirrored.5.a_ref), channel_id=1, source_target_pairs={{0,31},{1,30},{2,29},{3,28},{4,27},{5,26},{6,25},{7,24},{8,23},{9,... | collective-permute-start | bytes 1179656 | tf_op jit(solution)/shard_map/ppermute | solution.py:278

commit v6 on v5

--- a/solution.py
+++ b/solution.py
@@ -13,7 +13,7 @@
 NEG = -1e30
 SMALL = pl.CostEstimate(flops=1, bytes_accessed=1, transcendentals=0)
 VMEM_LIMIT = 64 * 1024 * 1024 - 256 * 1024
-CHUNKS = (2, 3, 3)
+CHUNKS = (3, 3, 2)
 
 
 def after(x, *others):

time: 146 us -> 158 us (1.082)
  the two profiles are of different devices: /device:TPU:25 before, /device:TPU:1 now
where the time goes in v6:
time: 158 us
  Pallas kernels  95.2 us (60%)
  starting transfers between devices  35.2 us (22%)
  waiting for transfers between devices  25.8 us (16%)
    pallas_call x6, Pallas kernels, attention(): pl.pallas_call(functools.partial(attention_kernel, min(256, rows), mirror...  47 us
    ppermute x10, starting transfers between devices, send(): return lax.ppermute(x, 'seq', pairs)  35.2 us
    pallas_call x4, Pallas kernels, project(): pl.pallas_call(functools.partial(project_kernel, scale, mirrored, with_q,...  33.2 us
    ppermute x10, waiting for transfers between devices, send(): return lax.ppermute(x, 'seq', pairs)  25.8 us
    pallas_call x3, Pallas kernels, turn(): pl.pallas_call(turn_kernel, out_shape=jax.ShapeDtypeStruct((rows, width),...  9.21 us
    pallas_call x3, Pallas kernels, place(): pl.pallas_call(functools.partial(place_kernel, first * 2 * (width // HEAD...  5.73 us
  transfers between devices with their start and end apart: 10, of which 2 were waited for; matrix products, arithmetic and copies ran while one was open for 0% of the time, Pallas kernels for 59%

profile of v6, /device:TPU:1, one launch (start us, length us, event | category | flops | bytes accessed | tf_op | source)
XLA Modules:
  0.0 157.6 jit_solution(7155099019964810489)
XLA Ops:
  0.6 3.3 %collective-permute-start = (bf16[512,1024]{1,0:T(8,128)(2,1)}, bf16[512,1024]{1,0:T(8,128)(2,1)}, u32[]{:S(2)}, u32[]{:S(2)}) collective-permute-start(bf16[512,1024]{1,0:T(8,128)(2,1)} %refs_0_), channel_id=1, source_target_pairs={{0,1},{1,0},{2,3},{3,2},{4,5},{5,4},{6,7},{7,6},{8,9},{9,8},{10,11... | collective-permute-start | bytes 3145736 | tf_op jit(solution)/shard_map/ppermute | solution.py:278
  4.1 3.4 %collective-permute-start.3 = (bf16[512,1024]{1,0:T(8,128)(2,1)}, bf16[512,1024]{1,0:T(8,128)(2,1)}, u32[]{:S(2)}, u32[]{:S(2)}) collective-permute-start(bf16[512,1024]{1,0:T(8,128)(2,1)} %refs_0_), channel_id=1, source_target_pairs={{1,2},{2,1},{3,4},{4,3},{5,6},{6,5},{7,8},{8,7},{9,10},{10,9},{11,... | collective-permute-start | bytes 3145736 | tf_op jit(solution)/shard_map/ppermute | solution.py:278
  8.0 10.4 %project.4 = (bf16[512,1024]{1,0:T(8,128)(2,1)}, bf16[1024,2048]{1,0:T(8,128)(2,1)}) custom-call(bf16[512,1024]{1,0:T(8,128)(2,1)} %refs_0_, bf16[512,1024]{1,0:T(8,128)(2,1)} %collective-permute-done.refs_1_, bf16[1024]{0:T(1024)(128)(2,1)} %refs_1_.3, bf16[1024,3072]{1,0:T(8,128)(2,1)} %refs_2_.7), custom_call_target="tpu_custom_call" | custom-call | flops 1 | bytes 1 | tf_op jit(solution)/shard_map/project/pallas_call | solution.py:99
  18.4 11.3 %project.5 = (bf16[512,1024]{1,0:T(8,128)(2,1)}, bf16[1024,2048]{1,0:T(8,128)(2,1)}) custom-call(bf16[512,1024]{1,0:T(8,128)(2,1)} %refs_0_.1, bf16[512,1024]{1,0:T(8,128)(2,1)} %collective-permute-done.1.refs_1_, bf16[1024]{0:T(1024)(128)(2,1)} %refs_1_.3, bf16[1024,3072]{1,0:T(8,128)(2,1)} %refs_2_.7), custom_call_target="tpu_custom_call" | custom-call | flops 1 | bytes 1 | tf_op jit(solution)/shard_map/project/pallas_call | solution.py:99
  29.7 3.9 %collective-permute-start.2 = (bf16[512,1024]{1,0:T(8,128)(2,1)}, bf16[512,1024]{1,0:T(8,128)(2,1)}, u32[]{:S(2)}, u32[]{:S(2)}) collective-permute-start(bf16[512,1024]{1,0:T(8,128)(2,1)} %refs_0_.1), channel_id=1, source_target_pairs={{1,2},{2,1},{3,4},{4,3},{5,6},{6,5},{7,8},{8,7},{9,10},{10,9},{11,... | collective-permute-start | bytes 3145736 | tf_op jit(solution)/shard_map/ppermute | solution.py:278
  33.5 5.7 %project.6.kr_ref.vr_ref = bf16[512,2048]{1,0:T(8,128)(2,1)} custom-call(bf16[512,1024]{1,0:T(8,128)(2,1)} %collective-permute-done.3.refs_0_, bf16[1024]{0:T(1024)(128)(2,1)} %refs_1_.3, bf16[1024,3072]{1,0:T(8,128)(2,1)} %refs_2_.7), custom_call_target="tpu_custom_call" | custom-call | flops 1 | bytes 1 | tf_op jit(solution)/shard_map/project/pallas_call | solution.py:99
  39.3 8.5 %attention.3.a_ref = bf16[512,384]{1,0:T(8,128)(2,1)} custom-call(s32[2]{0:T(128)} %pad_add_fusion.flags_ref, bf16[512,1024]{1,0:T(8,128)(2,1)} %get-tuple-element.34.q_ref, bf16[1024,2048]{1,0:T(8,128)(2,1)} %get-tuple-element.40.ko_ref.ks_ref.vo_ref.vs_ref, bf16[1024,2048]{1,0:T(8,128)(2,1)} %get-tuple-element.40.ko_ref.ks_ref.vo_ref.vs_ref, ...), custom_call_target="tpu_custom_call" | custom-call | flops 2013265920 | bytes 196608 | tf_op jit(solution)/shard_map/attention/pallas_call | solution.py:192
  47.8 6.8 %collective-permute-start.4 = (bf16[512,384]{1,0:T(8,128)(2,1)}, bf16[512,384]{1,0:T(8,128)(2,1)}, u32[]{:S(2)}, u32[]{:S(2)}) collective-permute-start(bf16[512,384]{1,0:T(8,128)(2,1)} %attention.3.a_ref), channel_id=1, source_target_pairs={{0,31},{1,30},{2,29},{3,28},{4,27},{5,26},{6,25},{7,24},{8,23},{9,... | collective-permute-start | bytes 1179656 | tf_op jit(solution)/shard_map/ppermute | solution.py:278
  54.5 8.5 %attention.4.a_ref = bf16[512,384]{1,0:T(8,128)(2,1)} custom-call(s32[2]{0:T(128)} %pad_add_fusion.flags_ref, bf16[512,1024]{1,0:T(8,128)(2,1)} %get-tuple-element.34.q_ref, bf16[1024,2048]{1,0:T(8,128)(2,1)} %get-tuple-element.40.ko_ref.ks_ref.vo_ref.vs_ref, bf16[1024,2048]{1,0:T(8,128)(2,1)} %get-tuple-element.40.ko_ref.ks_ref.vo_ref.vs_ref, ...), custom_call_target="tpu_custom_call" | custom-call | flops 2013265920 | bytes 196608 | tf_op jit(solution)/shard_map/attention/pallas_call | solution.py:192
  63.1 6.3 %attention.5.a_ref = bf16[512,256]{1,0:T(8,128)(2,1)} custom-call(s32[2]{0:T(128)} %pad_add_fusion.flags_ref, bf16[512,1024]{1,0:T(8,128)(2,1)} %get-tuple-element.34.q_ref, bf16[1024,2048]{1,0:T(8,128)(2,1)} %get-tuple-element.40.ko_ref.ks_ref.vo_ref.vs_ref, bf16[1024,2048]{1,0:T(8,128)(2,1)} %get-tuple-element.40.ko_ref.ks_ref.vo_ref.vs_ref, ...), custom_call_target="tpu_custom_call" | custom-call | flops 1342177280 | bytes 131072 | tf_op jit(solution)/shard_map/attention/pallas_call | solution.py:192
  69.4 5.9 %project.7.kr_ref.vr_ref = bf16[512,2048]{1,0:T(8,128)(2,1)} custom-call(bf16[512,1024]{1,0:T(8,128)(2,1)} %collective-permute-done.2.refs_0_, bf16[1024]{0:T(1024)(128)(2,1)} %refs_1_.3, bf16[1024,3072]{1,0:T(8,128)(2,1)} %refs_2_.7), custom_call_target="tpu_custom_call" | custom-call | flops 1 | bytes 1 | tf_op jit(solution)/shard_map/project/pallas_call | solution.py:99
  75.3 5.4 %collective-permute-done.4.b_ref = bf16[512,384]{1,0:T(8,128)(2,1)} collective-permute-done((bf16[512,384]{1,0:T(8,128)(2,1)}, bf16[512,384]{1,0:T(8,128)(2,1)}, u32[]{:S(2)}, u32[]{:S(2)}) %collective-permute-start.4) | collective-permute-done | bytes 393248 | tf_op jit(solution)/shard_map/ppermute | solution.py:278
  80.7 8.6 %attention_mirrored.3.a_ref = bf16[512,384]{1,0:T(8,128)(2,1)} custom-call(s32[2]{0:T(128)} %pad_add_fusion.flags_ref, bf16[512,1024]{1,0:T(8,128)(2,1)} %get-tuple-element.36.q_ref, bf16[1024,2048]{1,0:T(8,128)(2,1)} %get-tuple-element.49.ko_ref.ks_ref.vo_ref.vs_ref, bf16[1024,2048]{1,0:T(8,128)(2,1)} %get-tuple-element.49.ko_ref.ks_ref.vo_ref.vs_ref, ...), custom_call_target="tpu_custom_call" | custom-call | flops 2013265920 | bytes 196608 | tf_op jit(solution)/shard_map/attention_mirrored/pallas_call | solution.py:192
  89.4 6.1 %collective-permute-start.5 = (bf16[512,384]{1,0:T(8,128)(2,1)}, bf16[512,384]{1,0:T(8,128)(2,1)}, u32[]{:S(2)}, u32[]{:S(2)}) collective-permute-start(bf16[512,384]{1,0:T(8,128)(2,1)} %attention_mirrored.3.a_ref), channel_id=1, source_target_pairs={{0,31},{1,30},{2,29},{3,28},{4,27},{5,26},{6,25},{7,24},{8,23},{9,... | collective-permute-start | bytes 1179656 | tf_op jit(solution)/shard_map/ppermute | solution.py:278
  95.5 8.6 %attention_mirrored.4.a_ref = bf16[512,384]{1,0:T(8,128)(2,1)} custom-call(s32[2]{0:T(128)} %pad_add_fusion.flags_ref, bf16[512,1024]{1,0:T(8,128)(2,1)} %get-tuple-element.36.q_ref, bf16[1024,2048]{1,0:T(8,128)(2,1)} %get-tuple-element.49.ko_ref.ks_ref.vo_ref.vs_ref, bf16[1024,2048]{1,0:T(8,128)(2,1)} %get-tuple-element.49.ko_ref.ks_ref.vo_ref.vs_ref, ...), custom_call_target="tpu_custom_call" | custom-call | flops 2013265920 | bytes 196608 | tf_op jit(solution)/shard_map/attention_mirrored/pallas_call | solution.py:192
  104.2 5.3 %collective-permute-start.9 = (bf16[512,384]{1,0:T(8,128)(2,1)}, bf16[512,384]{1,0:T(8,128)(2,1)}, u32[]{:S(2)}, u32[]{:S(2)}) collective-permute-start(bf16[512,384]{1,0:T(8,128)(2,1)} %attention_mirrored.4.a_ref), channel_id=1, source_target_pairs={{0,31},{1,30},{2,29},{3,28},{4,27},{5,26},{6,25},{7,24},{8,23},{9,... | collective-permute-start | bytes 1179656 | tf_op jit(solution)/shard_map/ppermute | solution.py:278
  109.4 3.4 %turn.3.refs_0_ = bf16[512,1024]{1,0:T(8,128)(2,1)} custom-call(bf16[512,384]{1,0:T(8,128)(2,1)} %attention_mirrored.3.a_ref, bf16[512,384]{1,0:T(8,128)(2,1)} %collective-permute-done.4.b_ref), custom_call_target="tpu_custom_call" | custom-call | flops 1 | bytes 1 | tf_op jit(solution)/shard_map/turn/pallas_call | solution.py:229
  112.9 3.4 %turn.4.refs_0_ = bf16[512,1024]{1,0:T(8,128)(2,1)} custom-call(bf16[512,384]{1,0:T(8,128)(2,1)} %attention_mirrored.4.a_ref, bf16[512,384]{1,0:T(8,128)(2,1)} %collective-permute-done.7.b_ref, bf16[512,1024]{1,0:T(8,128)(2,1)} %turn.3.refs_0_), custom_call_target="tpu_custom_call", output_to_operand_aliasing={{}: (2, {})} | custom-call | flops 1 | bytes 1 | tf_op jit(solution)/shard_map/turn/pallas_call | solution.py:229
  116.3 20.3 %collective-permute-done.6.b_ref = bf16[512,256]{1,0:T(8,128)(2,1)} collective-permute-done((bf16[512,256]{1,0:T(8,128)(2,1)}, bf16[512,256]{1,0:T(8,128)(2,1)}, u32[]{:S(2)}, u32[]{:S(2)}) %collective-permute-start.6) | collective-permute-done | bytes 262176 | tf_op jit(solution)/shard_map/ppermute | solution.py:278
  136.6 6.4 %attention_mirrored.5.a_ref = bf16[512,256]{1,0:T(8,128)(2,1)} custom-call(s32[2]{0:T(128)} %pad_add_fusion.flags_ref, bf16[512,1024]{1,0:T(8,128)(2,1)} %get-tuple-element.36.q_ref, bf16[1024,2048]{1,0:T(8,128)(2,1)} %get-tuple-element.49.ko_ref.ks_ref.vo_ref.vs_ref, bf16[1024,2048]{1,0:T(8,128)(2,1)} %get-tuple-element.49.ko_ref.ks_ref.vo_ref.vs_ref, ...), custom_call_target="tpu_custom_call" | custom-call | flops 1342177280 | bytes 131072 | tf_op jit(solution)/shard_map/attention_mirrored/pallas_call | solution.py:192
  143.0 6.2 %collective-permute-start.8 = (bf16[512,256]{1,0:T(8,128)(2,1)}, bf16[512,256]{1,0:T(8,128)(2,1)}, u32[]{:S(2)}, u32[]{:S(2)}) collective-permute-start(bf16[512,256]{1,0:T(8,128)(2,1)} %attention_mirrored.5.a_ref), channel_id=1, source_target_pairs={{0,31},{1,30},{2,29},{3,28},{4,27},{5,26},{6,25},{7,24},{8,23},{9,... | collective-permute-start | bytes 786440 | tf_op jit(solution)/shard_map/ppermute | solution.py:278
  149.2 2.4 %turn.5 = bf16[512,1024]{1,0:T(8,128)(2,1)} custom-call(bf16[512,256]{1,0:T(8,128)(2,1)} %attention_mirrored.5.a_ref, bf16[512,256]{1,0:T(8,128)(2,1)} %collective-permute-done.6.b_ref, bf16[512,1024]{1,0:T(8,128)(2,1)} %turn.4.refs_0_), custom_call_target="tpu_custom_call", output_to_operand_aliasing={{}: (2, {})} | custom-call | flops 1 | bytes 1 | tf_op jit(solution)/shard_map/turn/pallas_call | solution.py:229
  151.6 2.0 %place.3.refs_0_ = bf16[512,1024]{1,0:T(8,128)(2,1)} custom-call(bf16[512,384]{1,0:T(8,128)(2,1)} %attention.3.a_ref, bf16[512,384]{1,0:T(8,128)(2,1)} %collective-permute-done.5.b_ref), custom_call_target="tpu_custom_call" | custom-call | flops 1 | bytes 1 | tf_op jit(solution)/shard_map/place/pallas_call | solution.py:254
  153.6 2.0 %place.4.refs_0_ = bf16[512,1024]{1,0:T(8,128)(2,1)} custom-call(bf16[512,384]{1,0:T(8,128)(2,1)} %attention.4.a_ref, bf16[512,384]{1,0:T(8,128)(2,1)} %collective-permute-done.9.b_ref, bf16[512,1024]{1,0:T(8,128)(2,1)} %place.3.refs_0_), custom_call_target="tpu_custom_call", output_to_operand_aliasing={{}: (2, {})} | custom-call | flops 1 | bytes 1 | tf_op jit(solution)/shard_map/place/pallas_call | solution.py:254
  (13 shorter events, 2.6 us)
Async XLA Ops:
  0.6 7.4 %collective-permute-start = (bf16[512,1024]{1,0:T(8,128)(2,1)}, bf16[512,1024]{1,0:T(8,128)(2,1)}, u32[]{:S(2)}, u32[]{:S(2)}) collective-permute-start(bf16[512,1024]{1,0:T(8,128)(2,1)} %refs_0_), channel_id=1, source_target_pairs={{0,1},{1,0},{2,3},{3,2},{4,5},{5,4},{6,7},{7,6},{8,9},{9,8},{10,11... | collective-permute-start | bytes 3145736 | tf_op jit(solution)/shard_map/ppermute | solution.py:278
  4.0 14.4 %collective-permute-start.1 = (bf16[512,1024]{1,0:T(8,128)(2,1)}, bf16[512,1024]{1,0:T(8,128)(2,1)}, u32[]{:S(2)}, u32[]{:S(2)}) collective-permute-start(bf16[512,1024]{1,0:T(8,128)(2,1)} %refs_0_.1), channel_id=1, source_target_pairs={{0,1},{1,0},{2,3},{3,2},{4,5},{5,4},{6,7},{7,6},{8,9},{9,8},{10,11... | collective-permute-start | bytes 3145736 | tf_op jit(solution)/shard_map/ppermute | solution.py:278
  4.1 29.5 %collective-permute-start.3 = (bf16[512,1024]{1,0:T(8,128)(2,1)}, bf16[512,1024]{1,0:T(8,128)(2,1)}, u32[]{:S(2)}, u32[]{:S(2)}) collective-permute-start(bf16[512,1024]{1,0:T(8,128)(2,1)} %refs_0_), channel_id=1, source_target_pairs={{1,2},{2,1},{3,4},{4,3},{5,6},{6,5},{7,8},{8,7},{9,10},{10,9},{11,... | collective-permute-start | bytes 3145736 | tf_op jit(solution)/shard_map/ppermute | solution.py:278
  29.7 33.4 %collective-permute-start.2 = (bf16[512,1024]{1,0:T(8,128)(2,1)}, bf16[512,1024]{1,0:T(8,128)(2,1)}, u32[]{:S(2)}, u32[]{:S(2)}) collective-permute-start(bf16[512,1024]{1,0:T(8,128)(2,1)} %refs_0_.1), channel_id=1, source_target_pairs={{1,2},{2,1},{3,4},{4,3},{5,6},{6,5},{7,8},{8,7},{9,10},{10,9},{11,... | collective-permute-start | bytes 3145736 | tf_op jit(solution)/shard_map/ppermute | solution.py:278
  47.8 32.9 %collective-permute-start.4 = (bf16[512,384]{1,0:T(8,128)(2,1)}, bf16[512,384]{1,0:T(8,128)(2,1)}, u32[]{:S(2)}, u32[]{:S(2)}) collective-permute-start(bf16[512,384]{1,0:T(8,128)(2,1)} %attention.3.a_ref), channel_id=1, source_target_pairs={{0,31},{1,30},{2,29},{3,28},{4,27},{5,26},{6,25},{7,24},{8,23},{9,... | collective-permute-start | bytes 1179656 | tf_op jit(solution)/shard_map/ppermute | solution.py:278
  63.1 32.5 %collective-permute-start.7 = (bf16[512,384]{1,0:T(8,128)(2,1)}, bf16[512,384]{1,0:T(8,128)(2,1)}, u32[]{:S(2)}, u32[]{:S(2)}) collective-permute-start(bf16[512,384]{1,0:T(8,128)(2,1)} %attention.4.a_ref), channel_id=1, source_target_pairs={{0,31},{1,30},{2,29},{3,28},{4,27},{5,26},{6,25},{7,24},{8,23},{9,... | collective-permute-start | bytes 1179656 | tf_op jit(solution)/shard_map/ppermute | solution.py:278
  89.4 47.2 %collective-permute-start.5 = (bf16[512,384]{1,0:T(8,128)(2,1)}, bf16[512,384]{1,0:T(8,128)(2,1)}, u32[]{:S(2)}, u32[]{:S(2)}) collective-permute-start(bf16[512,384]{1,0:T(8,128)(2,1)} %attention_mirrored.3.a_ref), channel_id=1, source_target_pairs={{0,31},{1,30},{2,29},{3,28},{4,27},{5,26},{6,25},{7,24},{8,23},{9,... | collective-permute-start | bytes 1179656 | tf_op jit(solution)/shard_map/ppermute | solution.py:278
  95.5 41.1 %collective-permute-start.6 = (bf16[512,256]{1,0:T(8,128)(2,1)}, bf16[512,256]{1,0:T(8,128)(2,1)}, u32[]{:S(2)}, u32[]{:S(2)}) collective-permute-start(bf16[512,256]{1,0:T(8,128)(2,1)} %attention.5.a_ref), channel_id=1, source_target_pairs={{0,31},{1,30},{2,29},{3,28},{4,27},{5,26},{6,25},{7,24},{8,23},{9,... | collective-permute-start | bytes 786440 | tf_op jit(solution)/shard_map/ppermute | solution.py:278
  104.2 49.4 %collective-permute-start.9 = (bf16[512,384]{1,0:T(8,128)(2,1)}, bf16[512,384]{1,0:T(8,128)(2,1)}, u32[]{:S(2)}, u32[]{:S(2)}) collective-permute-start(bf16[512,384]{1,0:T(8,128)(2,1)} %attention_mirrored.4.a_ref), channel_id=1, source_target_pairs={{0,31},{1,30},{2,29},{3,28},{4,27},{5,26},{6,25},{7,24},{8,23},{9,... | collective-permute-start | bytes 1179656 | tf_op jit(solution)/shard_map/ppermute | solution.py:278
  143.0 12.6 %collective-permute-start.8 = (bf16[512,256]{1,0:T(8,128)(2,1)}, bf16[512,256]{1,0:T(8,128)(2,1)}, u32[]{:S(2)}, u32[]{:S(2)}) collective-permute-start(bf16[512,256]{1,0:T(8,128)(2,1)} %attention_mirrored.5.a_ref), channel_id=1, source_target_pairs={{0,31},{1,30},{2,29},{3,28},{4,27},{5,26},{6,25},{7,24},{8,23},{9,... | collective-permute-start | bytes 786440 | tf_op jit(solution)/shard_map/ppermute | solution.py:278
